TPU v7x, 32 devices: a whole 2x2x4 slice. The times are simulated.
32 devices in a mesh: dp: 8 (over z, x), tensor: 4 (over y, core).
Axes of the slice: x: 2, y: 2, z: 4, core: 2. Of those that a mesh axis runs over, the one named last changes fastest.
Arguments:
- tokens: bfloat16 [8192, 2048], P('dp'), may hold values from -6 to 6
- w_query: bfloat16 [2048, 2048], P('dp', 'tensor'), may hold values from -0.125 to 0.125
- w_key: bfloat16 [2048, 2048], P('dp', 'tensor'), may hold values from -0.125 to 0.125
- w_value: bfloat16 [2048, 4096], P('dp', 'tensor'), may hold values from -0.125 to 0.125
- w_gate: bfloat16 [2048, 4096], P('dp', 'tensor'), may hold values from -0.125 to 0.125
- w_out: bfloat16 [4096, 2048], P('tensor', 'dp'), may hold values from -0.125 to 0.125
- w_ffgate: bfloat16 [2048, 4096], P('dp', 'tensor'), may hold values from -0.125 to 0.125
- w_ffup: bfloat16 [2048, 4096], P('dp', 'tensor'), may hold values from -0.125 to 0.125
- w_down: bfloat16 [4096, 2048], P('tensor', 'dp'), may hold values from -0.125 to 0.125
- norm1_gain: bfloat16 [2048], P('dp'), may hold values from 0.5 to 1.5
- norm1_shift: bfloat16 [2048], P('dp'), may hold values from -1 to 1
- norm2_gain: bfloat16 [2048], P('dp'), may hold values from 0.5 to 1.5
- norm2_shift: bfloat16 [2048], P('dp'), may hold values from -1 to 1
- segment_ids: int32 [8192], P('dp'), may hold values from 0 to 63, never falling along the last dimension, each value on 1 to 512 neighbouring positions
- decay_index: int32 [8], P('tensor'), may hold values from 0 to 4
- cotangent: bfloat16 [8192, 2048], P('dp'), may hold values from -6 to 6
Outputs:
- block_out: bfloat16 [8192, 2048], P('dp')
- grad_tokens: float32 [8192, 2048], P('dp')
- grad_query: float32 [2048, 2048], P('dp', 'tensor')
- grad_key: float32 [2048, 2048], P('dp', 'tensor')
- grad_value: float32 [2048, 4096], P('dp', 'tensor')
- grad_gate: float32 [2048, 4096], P('dp', 'tensor')
- grad_out: float32 [4096, 2048], P('tensor', 'dp')
- grad_ffgate: float32 [2048, 4096], P('dp', 'tensor')
- grad_ffup: float32 [2048, 4096], P('dp', 'tensor')
- grad_down: float32 [4096, 2048], P('tensor', 'dp')
- grad_gain_one: float32 [2048], P('dp')
- grad_shift_one: float32 [2048], P('dp')
- grad_gain_two: float32 [2048], P('dp')
- grad_shift_two: float32 [2048], P('dp')
Inputs may be any that keep to these rules, and one draw needn't show every extreme that they name: `segment_ids`: segment numbers never fall along the tokens; a sequence boundary resets retention even where the number continues.
All inputs are finite; a program needn't handle non-finite values.
Results may differ from a plain program's by a relative error of at most 0.018.
Values may be sent and summed in bfloat16 or wider, within the bound.
No kernel may reach another device: no remote copies, remote signals or barrier semaphores. Data moves between devices by JAX's collectives and lax.ppermute only.
A program may use at most 256 MiB of HBM per device.

v0:
```python
import math

import jax
import jax.numpy as jnp
from jax import lax
from jax.sharding import PartitionSpec as P

HEAD_KEY = 256
HEAD_VALUE = 512
LENGTH = 1024


EPSILON = 1e-05
GROUP_EPSILON = 1.0
XPOS_SPAN = 512.0
INV_ROOT2 = 1.0 / math.sqrt(2.0)
INV_ROOT_TWO_PI = 1.0 / math.sqrt(2.0 * math.pi)


def xpos_tables(length, width):
    half = width // 2
    index = jnp.arange(half, dtype=jnp.float32)
    theta = jnp.exp(index * (-math.log(10000.0) / half))
    zeta = (2.0 * index + 0.4 * width) / (1.4 * width)
    position = jnp.arange(length, dtype=jnp.float32) - float(length // 2)
    angle = position[:, None] * theta[None, :]
    growth = jnp.exp(position[:, None] * (1.0 / XPOS_SPAN) * jnp.log(zeta)[None, :])
    return (jnp.cos(angle), jnp.sin(angle), growth)


def rotate(values, cosine, sine, factor):
    half = values.shape[-1] // 2
    first = values[..., :half]
    second = values[..., half:]
    cos_b = cosine[:, None, :]
    sin_b = sine[:, None, :]
    scale = factor[:, None, :]
    return jnp.concatenate(
        [(first * cos_b - second * sin_b) * scale, (second * cos_b + first * sin_b) * scale],
        axis=-1,
    )


def unrotate(grads, cosine, sine, factor):
    half = grads.shape[-1] // 2
    scale = factor[:, None, :]
    first = grads[..., :half] * scale
    second = grads[..., half:] * scale
    cos_b = cosine[:, None, :]
    sin_b = sine[:, None, :]
    return jnp.concatenate(
        [first * cos_b + second * sin_b, second * cos_b - first * sin_b], axis=-1
    )


def decay_mask(row_start, row_segment, col_segment, log_gamma):
    row_pos = row_start + jnp.arange(row_segment.shape[0], dtype=jnp.int32)
    col_pos = jnp.arange(col_segment.shape[0], dtype=jnp.int32)
    gap = row_pos[:, None] - col_pos[None, :]
    keep = (gap >= 0) & (row_segment[:, None] == col_segment[None, :])
    distance = jnp.maximum(gap, 0).astype(jnp.float32)
    return jnp.where(keep[None], jnp.exp(distance[None] * log_gamma[:, None, None]), 0.0)


def norm_parts(values, offset):
    centred = values - jnp.mean(values, axis=-1, keepdims=True)
    inv_scale = lax.rsqrt(jnp.mean(centred * centred, axis=-1, keepdims=True) + offset)
    return (centred * inv_scale, inv_scale)


def norm_back(grad_out, normed, inv_scale, gain):
    grad_norm = grad_out * gain
    return inv_scale * (
        grad_norm
        - jnp.mean(grad_norm, axis=-1, keepdims=True)
        - normed * jnp.mean(grad_norm * normed, axis=-1, keepdims=True)
    )


def retention_forward(query_rot, key_rot, values, segment, log_gamma):
    length = query_rot.shape[0]
    rows = min(512, length)
    outputs = []
    for block_start in range(0, length, rows):
        raw = jnp.einsum(
            "nhk,mhk->hnm",
            query_rot[block_start : block_start + rows],
            key_rot,
            preferred_element_type=jnp.float32,
        )
        mask = decay_mask(
            block_start, segment[block_start : block_start + rows], segment, log_gamma
        )
        weighted = (raw * mask).astype(jnp.bfloat16)
        outputs.append(
            jnp.einsum("hnm,mhv->nhv", weighted, values, preferred_element_type=jnp.float32)
        )
    return jnp.concatenate(outputs, axis=0)


def retention_backward(query_rot, key_rot, values, segment, log_gamma, grad_mixed):
    length = query_rot.shape[0]
    rows = min(512, length)
    grad_query = []
    grad_key = jnp.zeros(key_rot.shape, jnp.float32)
    grad_value = jnp.zeros(values.shape, jnp.float32)
    for block_start in range(0, length, rows):
        query_block = query_rot[block_start : block_start + rows]
        grad_block = grad_mixed[block_start : block_start + rows]
        raw = jnp.einsum("nhk,mhk->hnm", query_block, key_rot, preferred_element_type=jnp.float32)
        mask = decay_mask(
            block_start, segment[block_start : block_start + rows], segment, log_gamma
        )
        weighted = (raw * mask).astype(jnp.bfloat16)
        grad_value = grad_value + jnp.einsum(
            "hnm,nhv->mhv", weighted, grad_block, preferred_element_type=jnp.float32
        )
        grad_weighted = jnp.einsum(
            "nhv,mhv->hnm", grad_block, values, preferred_element_type=jnp.float32
        )
        grad_raw = (grad_weighted * mask).astype(jnp.bfloat16)
        grad_query.append(
            jnp.einsum("hnm,mhk->nhk", grad_raw, key_rot, preferred_element_type=jnp.float32)
        )
        grad_key = grad_key + jnp.einsum(
            "hnm,nhk->mhk", grad_raw, query_block, preferred_element_type=jnp.float32
        )
    return (jnp.concatenate(grad_query, axis=0), grad_key, grad_value)


def dense(left, right):
    return jnp.dot(left, right, preferred_element_type=jnp.float32)


def local(
    tokens,
    w_query,
    w_key,
    w_value,
    w_gate,
    w_out,
    w_ffgate,
    w_ffup,
    w_down,
    norm1_gain,
    norm1_shift,
    norm2_gain,
    norm2_shift,
    segment_ids,
    decay_index,
    cotangent,
):
    gathered = (
        lax.all_gather(w_query, "dp", axis=0, tiled=True),
        lax.all_gather(w_key, "dp", axis=0, tiled=True),
        lax.all_gather(w_value, "dp", axis=0, tiled=True),
        lax.all_gather(w_gate, "dp", axis=0, tiled=True),
        lax.all_gather(w_out, "dp", axis=1, tiled=True),
        lax.all_gather(w_ffgate, "dp", axis=0, tiled=True),
        lax.all_gather(w_ffup, "dp", axis=0, tiled=True),
        lax.all_gather(w_down, "dp", axis=1, tiled=True),
        lax.all_gather(norm1_gain, "dp", axis=0, tiled=True),
        lax.all_gather(norm1_shift, "dp", axis=0, tiled=True),
        lax.all_gather(norm2_gain, "dp", axis=0, tiled=True),
        lax.all_gather(norm2_shift, "dp", axis=0, tiled=True),
    )
    (
        full_query,
        full_key,
        full_value,
        full_gate,
        full_out,
        full_ffgate,
        full_ffup,
        full_down,
        gain_one,
        shift_one,
        gain_two,
        shift_two,
    ) = gathered
    count = tokens.shape[0]
    seqs = count // LENGTH
    heads = full_query.shape[1] // HEAD_KEY
    inputs = tokens.astype(jnp.float32)
    log_gamma = jnp.log1p(-jnp.exp2(-5.0 - decay_index.astype(jnp.float32)))
    normed_one, scale_one = norm_parts(inputs, EPSILON)
    first_in = (normed_one * gain_one.astype(jnp.float32) + shift_one.astype(jnp.float32)).astype(
        jnp.bfloat16
    )
    query = dense(first_in, full_query).reshape(seqs, LENGTH, heads, HEAD_KEY)
    keys = dense(first_in, full_key).reshape(seqs, LENGTH, heads, HEAD_KEY)
    values_seq = (
        dense(first_in, full_value).astype(jnp.bfloat16).reshape(seqs, LENGTH, heads, HEAD_VALUE)
    )
    gate = dense(first_in, full_gate)
    cosine, sine, growth = xpos_tables(LENGTH, HEAD_KEY)
    query_rot = rotate(query, cosine, sine, growth).astype(jnp.bfloat16)
    key_rot = (rotate(keys, cosine, sine, 1.0 / growth) * HEAD_KEY ** (-0.5)).astype(jnp.bfloat16)
    segments = segment_ids.reshape(seqs, LENGTH)
    mixed = lax.map(
        lambda item: retention_forward(item[0], item[1], item[2], item[3], log_gamma),
        (query_rot, key_rot, values_seq, segments),
    )
    grouped, group_scale = norm_parts(mixed.reshape(count, heads, HEAD_VALUE), GROUP_EPSILON)
    grouped_flat = grouped.reshape(count, heads * HEAD_VALUE)
    sigmoid_gate = jax.nn.sigmoid(gate)
    swish = gate * sigmoid_gate
    gated = (swish * grouped_flat).astype(jnp.bfloat16)
    attention = lax.psum(dense(gated, full_out), "tensor")
    middle = inputs + attention
    normed_two, scale_two = norm_parts(middle, EPSILON)
    second_in = (normed_two * gain_two.astype(jnp.float32) + shift_two.astype(jnp.float32)).astype(
        jnp.bfloat16
    )
    ff_gate = dense(second_in, full_ffgate)
    ff_up = dense(second_in, full_ffup)
    normal_cdf = 0.5 * (1.0 + lax.erf(ff_gate * INV_ROOT2))
    activation = ff_gate * normal_cdf
    hidden = (activation * ff_up).astype(jnp.bfloat16)
    feed = lax.psum(dense(hidden, full_down).astype(jnp.bfloat16), "tensor").astype(jnp.float32)
    block_out = (middle + feed).astype(jnp.bfloat16)
    again = (
        lax.all_gather(w_query, "dp", axis=0, tiled=True),
        lax.all_gather(w_key, "dp", axis=0, tiled=True),
        lax.all_gather(w_value, "dp", axis=0, tiled=True),
        lax.all_gather(w_gate, "dp", axis=0, tiled=True),
        lax.all_gather(w_out, "dp", axis=1, tiled=True),
        lax.all_gather(w_ffgate, "dp", axis=0, tiled=True),
        lax.all_gather(w_ffup, "dp", axis=0, tiled=True),
        lax.all_gather(w_down, "dp", axis=1, tiled=True),
        lax.all_gather(norm1_gain, "dp", axis=0, tiled=True),
        lax.all_gather(norm1_shift, "dp", axis=0, tiled=True),
        lax.all_gather(norm2_gain, "dp", axis=0, tiled=True),
        lax.all_gather(norm2_shift, "dp", axis=0, tiled=True),
    )
    (
        back_query,
        back_key,
        back_value,
        back_gate,
        back_out,
        back_ffgate,
        back_ffup,
        back_down,
        back_gain_one,
        back_shift_one,
        back_gain_two,
        back_shift_two,
    ) = again
    grad_result = cotangent.astype(jnp.float32)
    grad_feed = grad_result.astype(jnp.bfloat16)
    grad_down = dense(hidden.T, grad_feed)
    grad_hidden = dense(grad_feed, back_down.T)
    density = jnp.exp(-0.5 * ff_gate * ff_gate) * INV_ROOT_TWO_PI
    grad_ffgate_in = (grad_hidden * ff_up * (normal_cdf + ff_gate * density)).astype(jnp.bfloat16)
    grad_ffup_in = (grad_hidden * activation).astype(jnp.bfloat16)
    grad_ffgate = dense(second_in.T, grad_ffgate_in)
    grad_ffup = dense(second_in.T, grad_ffup_in)
    grad_second = lax.psum(
        dense(grad_ffgate_in, back_ffgate.T) + dense(grad_ffup_in, back_ffup.T), "tensor"
    )
    grad_gain_two = jnp.sum(grad_second * normed_two, axis=0)
    grad_shift_two = jnp.sum(grad_second, axis=0)
    grad_middle = grad_result + norm_back(
        grad_second, normed_two, scale_two, back_gain_two.astype(jnp.float32)
    )
    grad_branch = grad_middle.astype(jnp.bfloat16)
    grad_out = dense(gated.T, grad_branch)
    grad_gated = dense(grad_branch, back_out.T)
    swish_slope = sigmoid_gate * (1.0 + gate * (1.0 - sigmoid_gate))
    grad_gate_in = (grad_gated * grouped_flat * swish_slope).astype(jnp.bfloat16)
    grad_grouped = (grad_gated * swish).reshape(count, heads, HEAD_VALUE)
    grad_mixed = norm_back(grad_grouped, grouped, group_scale, 1.0).astype(jnp.bfloat16)
    grad_mixed_seq = grad_mixed.reshape(seqs, LENGTH, heads, HEAD_VALUE)
    grad_qrot, grad_krot, grad_values = lax.map(
        lambda item: retention_backward(item[0], item[1], item[2], item[3], log_gamma, item[4]),
        (query_rot, key_rot, values_seq, segments, grad_mixed_seq),
    )
    grad_query_in = (
        unrotate(grad_qrot, cosine, sine, growth)
        .astype(jnp.bfloat16)
        .reshape(count, heads * HEAD_KEY)
    )
    grad_key_in = (
        (unrotate(grad_krot, cosine, sine, 1.0 / growth) * HEAD_KEY ** (-0.5))
        .astype(jnp.bfloat16)
        .reshape(count, heads * HEAD_KEY)
    )
    grad_value_in = grad_values.astype(jnp.bfloat16).reshape(count, heads * HEAD_VALUE)
    grad_query = dense(first_in.T, grad_query_in)
    grad_key = dense(first_in.T, grad_key_in)
    grad_value = dense(first_in.T, grad_value_in)
    grad_gate = dense(first_in.T, grad_gate_in)
    partial_first = (
        dense(grad_query_in, back_query.T)
        + dense(grad_key_in, back_key.T)
        + dense(grad_value_in, back_value.T)
        + dense(grad_gate_in, back_gate.T)
    )
    grad_first = lax.psum(partial_first.astype(jnp.bfloat16), "tensor").astype(jnp.float32)
    grad_gain_one = jnp.sum(grad_first * normed_one, axis=0)
    grad_shift_one = jnp.sum(grad_first, axis=0)
    grad_tokens = grad_middle + norm_back(
        grad_first, normed_one, scale_one, back_gain_one.astype(jnp.float32)
    )
    shares = tuple(
        (
            lax.psum_scatter(grad_query, "dp", scatter_dimension=0, tiled=True),
            lax.psum_scatter(grad_key, "dp", scatter_dimension=0, tiled=True),
            lax.psum_scatter(grad_value, "dp", scatter_dimension=0, tiled=True),
            lax.psum_scatter(grad_gate, "dp", scatter_dimension=0, tiled=True),
            lax.psum_scatter(grad_out, "dp", scatter_dimension=1, tiled=True),
            lax.psum_scatter(grad_ffgate, "dp", scatter_dimension=0, tiled=True),
            lax.psum_scatter(grad_ffup, "dp", scatter_dimension=0, tiled=True),
            lax.psum_scatter(grad_down, "dp", scatter_dimension=1, tiled=True),
            lax.psum_scatter(grad_gain_one, "dp", scatter_dimension=0, tiled=True),
            lax.psum_scatter(grad_shift_one, "dp", scatter_dimension=0, tiled=True),
            lax.psum_scatter(grad_gain_two, "dp", scatter_dimension=0, tiled=True),
            lax.psum_scatter(grad_shift_two, "dp", scatter_dimension=0, tiled=True),
        )
    )
    return (block_out, grad_tokens) + shares


def solution(mesh):
    placed = (
        P("dp", None),
        P("dp", "tensor"),
        P("dp", "tensor"),
        P("dp", "tensor"),
        P("dp", "tensor"),
        P("tensor", "dp"),
        P("dp", "tensor"),
        P("dp", "tensor"),
        P("tensor", "dp"),
        P("dp"),
        P("dp"),
        P("dp"),
        P("dp"),
        P("dp"),
        P("tensor"),
        P("dp", None),
    )
    return jax.shard_map(
        local,
        mesh=mesh,
        in_specs=placed,
        out_specs=(
            P("dp", None),
            P("dp", None),
            P("dp", "tensor"),
            P("dp", "tensor"),
            P("dp", "tensor"),
            P("dp", "tensor"),
            P("tensor", "dp"),
            P("dp", "tensor"),
            P("dp", "tensor"),
            P("tensor", "dp"),
            P("dp"),
            P("dp"),
            P("dp"),
            P("dp"),
        ),
        check_vma=False,
    )
```

profile of v0, /device:TPU:0, one launch (start us, length us, event | category | flops | bytes accessed | tf_op | source)
XLA Modules:
  0.0 2234.2 jit_solution(5405685063912232103)
XLA Ops:
  19.0 22.3 all-gather
  41.4 16.7 all-gather.1
  76.1 35.9 %all-gather.19.cloned.1.call-done = bf16[2048,512]{1,0:T(8,128)(2,1)} async-done(((bf16[256,512]{1,0:T(8,128)(2,1)}), bf16[2048,512]{1,0:T(8,128)(2,1)}) %all-gather.19.cloned.1.call-update) | async-done | bytes 2097168 | tf_op jit(solution)/shard_map/all_gather | solution.py:155
  132.1 53.3 %all-gather.15.cloned.1.call-done = bf16[2048,1024]{1,0:T(8,128)(2,1)} async-done(((bf16[256,1024]{1,0:T(8,128)(2,1)}), bf16[2048,1024]{1,0:T(8,128)(2,1)}) %all-gather.15.cloned.1.call-update) | async-done | bytes 4194320 | tf_op jit(solution)/shard_map/all_gather | solution.py:156
  185.4 8.6 convolution_convert_fusion.1
  199.1 59.7 %all-gather.13.cloned.1.call-done = bf16[2048,1024]{1,0:T(8,128)(2,1)} async-done(((bf16[256,1024]{1,0:T(8,128)(2,1)}), bf16[2048,1024]{1,0:T(8,128)(2,1)}) %all-gather.13.cloned.1.call-update) | async-done | bytes 4194320 | tf_op jit(solution)/shard_map/all_gather | solution.py:157
  258.8 12.2 multiply_convert_fusion.5
  270.9 62.9 %all-gather.21.cloned.1.call-done = bf16[1024,2048]{1,0:T(8,128)(2,1)} async-done(((bf16[1024,256]{1,0:T(8,128)(2,1)}), bf16[1024,2048]{1,0:T(8,128)(2,1)}) %all-gather.21.cloned.1.call-update) | async-done | bytes 4194320 | tf_op jit(solution)/shard_map/all_gather | solution.py:158
  333.9 11.0 fusion.63
  347.2 17.7 all-gather.2
  364.9 16.9 all-gather.3
  381.8 114.3 %all-reduce.10.cloned.1.call-done = f32[1024,2048]{1,0:T(8,128)} async-done(((f32[1024,2048]{1,0:T(8,128)}), f32[1024,2048]{1,0:T(8,128)}) %all-reduce.10.cloned.1.call-update) | async-done | bytes 8388624 | tf_op jit(solution)/shard_map/psum | solution.py:209
  508.0 63.2 %all-gather.23.cloned.1.call-done = bf16[2048,1024]{1,0:T(8,128)(2,1)} async-done(((bf16[256,1024]{1,0:T(8,128)(2,1)}), bf16[2048,1024]{1,0:T(8,128)(2,1)}) %all-gather.23.cloned.1.call-update) | async-done | bytes 4194320 | tf_op jit(solution)/shard_map/all_gather | solution.py:159
  571.2 10.0 fusion.64
  581.2 63.5 %all-gather.25.cloned.1.call-done = bf16[2048,1024]{1,0:T(8,128)(2,1)} async-done(((bf16[256,1024]{1,0:T(8,128)(2,1)}), bf16[2048,1024]{1,0:T(8,128)(2,1)}) %all-gather.25.cloned.1.call-update) | async-done | bytes 4194320 | tf_op jit(solution)/shard_map/all_gather | solution.py:160
  644.6 10.0 fusion.65
  654.7 65.2 %all-gather.27.cloned.1.call-done = bf16[1024,2048]{1,0:T(8,128)(2,1)} async-done(((bf16[1024,256]{1,0:T(8,128)(2,1)}), bf16[1024,2048]{1,0:T(8,128)(2,1)}) %all-gather.27.cloned.1.call-update) | async-done | bytes 4194320 | tf_op jit(solution)/shard_map/all_gather | solution.py:161
  719.9 12.5 multiply_convert_fusion.3
  737.0 6.9 convolution_add_fusion
  744.4 9.4 convolution_convert_fusion
  753.9 141.3 %all-reduce.12.cloned.1.call-done = f32[1024,2048]{1,0:T(8,128)} async-done(((f32[1024,2048]{1,0:T(8,128)}), f32[1024,2048]{1,0:T(8,128)}) %all-reduce.12.cloned.1.call-update) | async-done | bytes 8388624 | tf_op jit(solution)/shard_map/psum | solution.py:259
  895.2 8.3 multiply_reduce_fusion
  903.5 7.5 multiply_add_fusion
  911.2 13.1 multiply_convert_fusion
  958.5 6.9 fusion.68
  965.4 6.9 fusion.69
  972.2 11.4 add_convert_fusion
  984.1 6.6 fusion.71
  991.9 6.5 fusion.70
  1000.1 9.1 fusion.74
  1010.9 9.1 fusion.75
  1021.8 8.8 fusion.76
  1032.2 10.1 fusion.29
  1043.9 9.1 fusion.72
  1054.6 9.1 fusion.73
  1065.5 71.3 %all-reduce.14.cloned.1.call-done = (bf16[1024,2048]{1,0:T(8,128)(2,1)}, bf16[1024,2048]{1,0:T(8,128)(2,1)}) async-done(((bf16[1024,2048]{1,0:T(8,128)(2,1)}, bf16[1024,2048]{1,0:T(8,128)(2,1)}), (bf16[1024,2048]{1,0:T(8,128)(2,1)}, bf16[1024,2048]{1,0:T(8,128)(2,1)})) %all-reduce.14.cloned.1.call-update) | async-done | bytes 8388624 | tf_op jit(solution)/shard_map/psum | solution.py:220
  1136.8 6.2 fusion.14
  1143.1 39.4 %all-reduce.4 = (f32[2048]{0:T(1024)S(1)}, f32[2048]{0:T(1024)S(1)}, f32[2048]{0:T(1024)S(1)}, f32[2048]{0:T(1024)S(1)}) all-reduce(f32[2048]{0:T(1024)S(1)} %get-tuple-element.68, f32[2048]{0:T(1024)S(1)} %get-tuple-element.72, f32[2048]{0:T(1024)S(1)} %copy-done.48, ...), channel_id=10, replica_groups=mesh['dp'=8,'tensor'=4] {'dp'}, use_global_device_ids=true, to_apply=%region_25.26.clone | all-reduce | flops 8192 | bytes 65536
  1185.1 8.5 add_convert_fusion.1
  1193.6 7.4 fusion.11
  1201.0 29.0 %reduce-scatter.11.cloned.1.call-done = f32[256,512]{1,0:T(8,128)} async-done(((f32[2048,512]{1,0:T(8,128)}), f32[256,512]{1,0:T(8,128)}) %reduce-scatter.11.cloned.1.call-update) | async-done | bytes 524304 | tf_op jit(solution)/shard_map/reduce_scatter | solution.py:309
  1229.9 92.2 %reduce-scatter.9.cloned.1.call-done = f32[256,512]{1,0:T(8,128)} async-done(((f32[2048,512]{1,0:T(8,128)}), f32[256,512]{1,0:T(8,128)}) %reduce-scatter.9.cloned.1.call-update) | async-done | bytes 524304 | tf_op jit(solution)/shard_map/reduce_scatter | solution.py:308
  1322.1 151.2 %reduce-scatter.19.cloned.1.call-done = f32[256,1024]{1,0:T(8,128)} async-done(((f32[2048,1024]{1,0:T(8,128)}), f32[256,1024]{1,0:T(8,128)}) %reduce-scatter.19.cloned.1.call-update) | async-done | bytes 1048592 | tf_op jit(solution)/shard_map/reduce_scatter | solution.py:313
  1473.3 150.6 %reduce-scatter.21.cloned.1.call-done = f32[256,1024]{1,0:T(8,128)} async-done(((f32[2048,1024]{1,0:T(8,128)}), f32[256,1024]{1,0:T(8,128)}) %reduce-scatter.21.cloned.1.call-update) | async-done | bytes 1048592 | tf_op jit(solution)/shard_map/reduce_scatter | solution.py:314
  1623.9 151.1 %reduce-scatter.23.cloned.1.call-done = f32[1024,256]{1,0:T(8,128)} async-done(((f32[1024,2048]{1,0:T(8,128)}), f32[1024,256]{1,0:T(8,128)}) %reduce-scatter.23.cloned.1.call-update) | async-done | bytes 1048592 | tf_op jit(solution)/shard_map/reduce_scatter | solution.py:315
  1775.0 151.0 %reduce-scatter.17.cloned.1.call-done = f32[1024,256]{1,0:T(8,128)} async-done(((f32[1024,2048]{1,0:T(8,128)}), f32[1024,256]{1,0:T(8,128)}) %reduce-scatter.17.cloned.1.call-update) | async-done | bytes 1048592 | tf_op jit(solution)/shard_map/reduce_scatter | solution.py:312
  1926.0 150.7 %reduce-scatter.13.cloned.1.call-done = f32[256,1024]{1,0:T(8,128)} async-done(((f32[2048,1024]{1,0:T(8,128)}), f32[256,1024]{1,0:T(8,128)}) %reduce-scatter.13.cloned.1.call-update) | async-done | bytes 1048592 | tf_op jit(solution)/shard_map/reduce_scatter | solution.py:310
  2076.7 150.8 %reduce-scatter.15.cloned.1.call-done = f32[256,1024]{1,0:T(8,128)} async-done(((f32[2048,1024]{1,0:T(8,128)}), f32[256,1024]{1,0:T(8,128)}) %reduce-scatter.15.cloned.1.call-update) | async-done | bytes 1048592 | tf_op jit(solution)/shard_map/reduce_scatter | solution.py:311
  (251 shorter events, 123.2 us)
Async XLA Ops:
  7.2 58.0 %all-gather.17.cloned.1.call-start = ((), (), s32[]{:S(2)}) async-start(), calls=%async_computation.10 | async-start | bytes 2359296 | tf_op jit(solution)/shard_map/all_gather | solution.py:154
  7.9 104.0 %all-gather.19.cloned.1.call-start = ((), (), s32[]{:S(2)}) async-start(), calls=%async_computation.11 | async-start | bytes 2359296 | tf_op jit(solution)/shard_map/all_gather | solution.py:155
  8.7 176.8 %all-gather.15.cloned.1.call-start = ((), (), s32[]{:S(2)}) async-start(), calls=%async_computation.9 | async-start | bytes 4718592 | tf_op jit(solution)/shard_map/all_gather | solution.py:156
  9.4 249.4 %all-gather.13.cloned.1.call-start = ((), (), s32[]{:S(2)}) async-start(), calls=%async_computation.8 | async-start | bytes 4718592 | tf_op jit(solution)/shard_map/all_gather | solution.py:157
  10.0 323.9 %all-gather.21.cloned.1.call-start = ((), (), s32[]{:S(2)}) async-start(), calls=%async_computation.12 | async-start | bytes 4718592 | tf_op jit(solution)/shard_map/all_gather | solution.py:158
  10.6 485.5 %all-reduce.10.cloned.1.call-start = ((), (), s32[]{:S(2)}) async-start(), calls=%async_computation.13 | async-start | bytes 16777216 | tf_op jit(solution)/shard_map/psum | solution.py:209
  10.6 4.9 copy-start.1
  15.5 25.8 %copy-start.57 = (bf16[256]{0:T(256)(128)(2,1)S(1)}, bf16[256]{0:T(256)(128)(2,1)}, u32[]{:S(2)}) copy-start(bf16[256]{0:T(256)(128)(2,1)} %param.26) | copy-start | bytes 1540
  15.5 46.3 %copy-start.44 = (f32[1024]{0:T(1024)}, f32[1024]{0:T(1024)S(1)}, u32[]{:S(2)}) copy-start(f32[1024]{0:T(1024)S(1)} %broadcast_multiply_fusion.9) | copy-start | bytes 12292
  16.8 45.1 %copy-start.46 = (f32[1024]{0:T(1024)}, f32[1024]{0:T(1024)S(1)}, u32[]{:S(2)}) copy-start(f32[1024]{0:T(1024)S(1)} %add_rsqrt_fusion.2) | copy-start | bytes 12292
  17.0 106.9 %copy-start.14 = (f32[1024,128]{1,0:T(8,128)}, f32[1024,128]{1,0:T(8,128)S(1)}, u32[]{:S(2)}) copy-start(f32[1024,128]{1,0:T(8,128)S(1)} %get-tuple-element.103) | copy-start | bytes 1572868
  17.1 106.9 %copy-start.16 = (f32[1024,128]{1,0:T(8,128)}, f32[1024,128]{1,0:T(8,128)S(1)}, u32[]{:S(2)}) copy-start(f32[1024,128]{1,0:T(8,128)S(1)} %get-tuple-element.104) | copy-start | bytes 1572868
  19.0 105.0 %copy-start.18 = (f32[1024,128]{1,0:T(8,128)}, f32[1024,128]{1,0:T(8,128)S(1)}, u32[]{:S(2)}) copy-start(f32[1024,128]{1,0:T(8,128)S(1)} %get-tuple-element.105) | copy-start | bytes 1572868
  19.0 105.0 %copy-start.20 = (f32[1024,128]{1,0:T(8,128)}, f32[1024,128]{1,0:T(8,128)S(1)}, u32[]{:S(2)}) copy-start(f32[1024,128]{1,0:T(8,128)S(1)} %get-tuple-element.106) | copy-start | bytes 1572868
  41.3 20.5 copy-start.42
  185.4 8.6 copy-start.26
  344.8 20.1 copy-start.59
  344.9 226.3 %all-gather.23.cloned.1.call-start = ((), (), s32[]{:S(2)}) async-start(), calls=%async_computation.14 | async-start | bytes 4718592 | tf_op jit(solution)/shard_map/all_gather | solution.py:159
  345.6 299.0 %all-gather.25.cloned.1.call-start = ((), (), s32[]{:S(2)}) async-start(), calls=%async_computation.15 | async-start | bytes 4718592 | tf_op jit(solution)/shard_map/all_gather | solution.py:160
  346.4 373.5 %all-gather.27.cloned.1.call-start = ((), (), s32[]{:S(2)}) async-start(), calls=%async_computation.16 | async-start | bytes 4718592 | tf_op jit(solution)/shard_map/all_gather | solution.py:161
  347.1 548.1 %all-reduce.12.cloned.1.call-start = ((), (), s32[]{:S(2)}) async-start(), calls=%async_computation.17 | async-start | bytes 16777216 | tf_op jit(solution)/shard_map/psum | solution.py:259
  719.9 12.5 copy-start.52
  732.4 4.6 copy-start.64
  732.4 4.6 copy-start.53
  744.0 392.8 %all-reduce.14.cloned.1.call-start = ((), (), s32[]{:S(2)}) async-start(), calls=%async_computation.26 | async-start | bytes 16777216 | tf_op jit(solution)/shard_map/psum | solution.py:220
  895.2 8.3 copy-start.23
  903.5 7.5 copy-start.5
  903.5 7.7 copy-start.6
  911.0 13.2 copy-start.3
  930.1 6.4 copy-start.8
  943.9 7.4 copy-start.9
  958.5 6.9 copy-start.22
  958.5 6.9 copy-start.24
  983.6 246.3 %reduce-scatter.11.cloned.1.call-start = ((), (), s32[]{:S(2)}) async-start(), calls=%async_computation.19 | async-start | bytes 4718592 | tf_op jit(solution)/shard_map/reduce_scatter | solution.py:309
  990.7 331.4 %reduce-scatter.9.cloned.1.call-start = ((), (), s32[]{:S(2)}) async-start(), calls=%async_computation.18 | async-start | bytes 4718592 | tf_op jit(solution)/shard_map/reduce_scatter | solution.py:308
  998.5 474.8 %reduce-scatter.19.cloned.1.call-start = ((), (), s32[]{:S(2)}) async-start(), calls=%async_computation.23 | async-start | bytes 9437184 | tf_op jit(solution)/shard_map/reduce_scatter | solution.py:313
  1009.2 614.7 %reduce-scatter.21.cloned.1.call-start = ((), (), s32[]{:S(2)}) async-start(), calls=%async_computation.24 | async-start | bytes 9437184 | tf_op jit(solution)/shard_map/reduce_scatter | solution.py:314
  1020.0 755.0 %reduce-scatter.23.cloned.1.call-start = ((), (), s32[]{:S(2)}) async-start(), calls=%async_computation.25 | async-start | bytes 9437184 | tf_op jit(solution)/shard_map/reduce_scatter | solution.py:315
  1030.6 895.4 %reduce-scatter.17.cloned.1.call-start = ((), (), s32[]{:S(2)}) async-start(), calls=%async_computation.22 | async-start | bytes 9437184 | tf_op jit(solution)/shard_map/reduce_scatter | solution.py:312
  1042.3 1034.4 %reduce-scatter.13.cloned.1.call-start = ((), (), s32[]{:S(2)}) async-start(), calls=%async_computation.20 | async-start | bytes 9437184 | tf_op jit(solution)/shard_map/reduce_scatter | solution.py:310
  1053.0 1174.5 %reduce-scatter.15.cloned.1.call-start = ((), (), s32[]{:S(2)}) async-start(), calls=%async_computation.21 | async-start | bytes 9437184 | tf_op jit(solution)/shard_map/reduce_scatter | solution.py:311
  1063.7 73.1 %copy-start.43 = (f32[8,1,256]{2,1,0:T(1,128)S(1)}, f32[8,1,256]{2,1,0:T(1,128)}, u32[]{:S(2)}) copy-start(f32[8,1,256]{2,1,0:T(1,128)} %copy-done.42) | copy-start | bytes 24580
  1063.7 73.1 %copy-start.45 = (f32[1024]{0:T(1024)S(1)}, f32[1024]{0:T(1024)}, u32[]{:S(2)}) copy-start(f32[1024]{0:T(1024)} %copy-done.44) | copy-start | bytes 12292
  1063.7 73.1 %copy-start.47 = (f32[1024]{0:T(1024)S(1)}, f32[1024]{0:T(1024)}, u32[]{:S(2)}) copy-start(f32[1024]{0:T(1024)} %copy-done.46) | copy-start | bytes 12292
  1136.8 6.2 copy-start.48
  1136.8 6.2 copy-start.49
  1185.0 8.5 copy-start.2
  1185.1 8.5 copy-start.7
  (39 other events, 92.5 us)
Sparse Core Ops, SparseCore 0:
  10.1 52.0 all-gather.16
  64.3 47.5 all-gather.18
  114.1 71.3 all-gather.14
  187.4 71.3 all-gather.12
  260.6 73.1 all-gather.20
  345.0 151.0 all-reduce.9
  498.2 72.9 all-gather.22
  573.3 71.3 all-gather.24
  646.7 73.1 all-gather.26
  744.1 151.0 all-reduce.11
  983.7 153.0 all-reduce.13
  1140.9 89.0 reduce-scatter.10
  1234.1 87.9 reduce-scatter.8
  1326.2 147.0 reduce-scatter.18
  1477.3 146.5 reduce-scatter.20
  1628.0 146.9 reduce-scatter.22
  1779.0 146.9 reduce-scatter.16
  1930.1 146.5 reduce-scatter.12
  2080.9 146.5 reduce-scatter.14
where the time goes:
time: 2240 us; the launch traced here: 2230 us
  waiting for transfers between devices  1760 us (79%)
  matrix products  227 us (10%)
  blocking collectives  113 us (5%)
  other arithmetic  76.2 us (3%)
  local copies, waits for them, and re-layouts  38 us (2%)
    dot_general x24, matrix products, dense(): return jnp.dot(left, right, preferred_element_type=jnp.float32)  205 us
    reduce_scatter x1, waiting for transfers between devices, local(): lax.psum_scatter(grad_ffgate, 'dp', scatter_dimension=0, tiled=True)  151 us
    reduce_scatter x1, waiting for transfers between devices, local(): lax.psum_scatter(grad_down, 'dp', scatter_dimension=1, tiled=True)  151 us
    reduce_scatter x1, waiting for transfers between devices, local(): lax.psum_scatter(grad_out, 'dp', scatter_dimension=1, tiled=True)  151 us
    reduce_scatter x1, waiting for transfers between devices, local(): lax.psum_scatter(grad_gate, 'dp', scatter_dimension=0, tiled=True)  151 us
    reduce_scatter x1, waiting for transfers between devices, local(): lax.psum_scatter(grad_value, 'dp', scatter_dimension=0, tiled=True)  151 us
    reduce_scatter x1, waiting for transfers between devices, local(): lax.psum_scatter(grad_ffup, 'dp', scatter_dimension=0, tiled=True)  151 us
    psum x1, waiting for transfers between devices, local(): lax.psum(dense(grad_ffgate_in, back_ffgate.T) + dense(grad_ffup_in, back_...  141 us
  transfers between devices with their start and end apart: 19, of which 18 were waited for; matrix products, arithmetic and copies ran while one was open for 9% of the time, Pallas kernels for 0%

commit v1 on v0

v1 whole, which is shorter than its diff:
```python
import functools
import math

import jax
import jax.numpy as jnp
from jax import lax
from jax.sharding import PartitionSpec as P

HEAD_KEY = 256
HEAD_VALUE = 512
LENGTH = 1024


EPSILON = 1e-05
GROUP_EPSILON = 1.0
XPOS_SPAN = 512.0
INV_ROOT2 = 1.0 / math.sqrt(2.0)
INV_ROOT_TWO_PI = 1.0 / math.sqrt(2.0 * math.pi)

BOTH = ("dp", "tensor")


def xpos_tables(length, width):
    half = width // 2
    index = jnp.arange(half, dtype=jnp.float32)
    theta = jnp.exp(index * (-math.log(10000.0) / half))
    zeta = (2.0 * index + 0.4 * width) / (1.4 * width)
    position = jnp.arange(length, dtype=jnp.float32) - float(length // 2)
    angle = position[:, None] * theta[None, :]
    growth = jnp.exp(position[:, None] * (1.0 / XPOS_SPAN) * jnp.log(zeta)[None, :])
    return (jnp.cos(angle), jnp.sin(angle), growth)


def norm_parts(values, offset):
    centred = values - jnp.mean(values, axis=-1, keepdims=True)
    inv_scale = lax.rsqrt(jnp.mean(centred * centred, axis=-1, keepdims=True) + offset)
    return (centred * inv_scale, inv_scale)


def norm_back(grad_out, normed, inv_scale, gain):
    grad_norm = grad_out * gain
    return inv_scale * (
        grad_norm
        - jnp.mean(grad_norm, axis=-1, keepdims=True)
        - normed * jnp.mean(grad_norm * normed, axis=-1, keepdims=True)
    )


def dot_nn(left, right):
    return lax.dot_general(
        left, right, (((1,), (0,)), ((), ())), preferred_element_type=jnp.float32
    )


def dot_nt(left, right):
    return lax.dot_general(
        left, right, (((1,), (1,)), ((), ())), preferred_element_type=jnp.float32
    )


def dot_tn(left, right):
    return lax.dot_general(
        left, right, (((0,), (0,)), ((), ())), preferred_element_type=jnp.float32
    )


def together(*values):
    return lax.optimization_barrier(values)


def after(value, *others):
    return lax.optimization_barrier((value, *others))[0]


class Place:
    def __init__(self, ndp, nt):
        self.ndp, self.nt, self.na, self.ny = ndp, nt, ndp // 2, nt // 2
        index = lax.axis_index("dp")
        spot = lax.axis_index("tensor")
        self.a, self.b = index // 2, index % 2
        self.y, self.c = spot // 2, spot % 2
        self.keeper = self.b == self.c
        na, ny = self.na, self.ny
        self.ring = self.perm(lambda a, b, y, c: ((a + 1) % na, b, y, c))
        self.core = self.perm(lambda a, b, y, c: (a, b, y, 1 - c))
        self.across_x = self.perm(lambda a, b, y, c: (a, 1 - b, y, c))
        self.across_y = self.perm(lambda a, b, y, c: (a, b, 1 - y, c))
        self.across_both = self.perm(lambda a, b, y, c: (a, 1 - b, 1 - y, c))
        self.swap = self.perm(lambda a, b, y, c: (a, 1 - b, y, 1 - c) if b != c else None)
        self.home_x = self.perm(lambda a, b, y, c: (a, 1 - b, y, c) if b != c else None)
        self.home_y = self.perm(lambda a, b, y, c: (a, b, 1 - y, c) if b == c else None)
        self.home_core = self.perm(lambda a, b, y, c: (a, b, y, 1 - c) if b == c else None)
        self.group_ac = [
            [self.flat(a, b, y, c) for a in range(na) for c in range(2)]
            for b in range(2)
            for y in range(ny)
        ]
        self.group_a = [[2 * a + b for a in range(na)] for b in range(2)]

    def jump(self, step):
        return self.perm(lambda a, b, y, c: ((a + step) % self.na, b, y, c))

    def perm(self, move):
        pairs = []
        for a in range(self.na):
            for b in range(2):
                for y in range(self.ny):
                    for c in range(2):
                        to = move(a, b, y, c)
                        if to is not None:
                            pairs.append((self.flat(a, b, y, c), self.flat(*to)))
        return pairs

    def flat(self, a, b, y, c):
        return (2 * a + b) * self.nt + 2 * y + c


def send(value, pairs):
    return lax.ppermute(value, BOTH, pairs)


def rows_at(value, start, size):
    return lax.dynamic_slice_in_dim(value, start, size, axis=0)


def my_sequence(place, value):
    return jnp.where(place.keeper, value, send(value, place.swap))


def pick(keeper, value, received):
    return jnp.where(keeper, value, received)


def assemble(size, placed):
    first = placed[0][1]
    whole = jnp.zeros((size, *first.shape[1:]), first.dtype)
    for start, rows in placed:
        whole = lax.dynamic_update_slice_in_dim(whole, rows, start, axis=0)
    return whole


def row_starts(q, b, y):
    return (2 * y + b) * q, (4 + 2 * b + y) * q


def rows_of(value, b, y):
    q = value.shape[0] // 8
    first, second = row_starts(q, b, y)
    return rows_at(value, first, q), rows_at(value, second, q)


def my_rows(place, value):
    return jnp.concatenate(rows_of(value, place.b, place.y), axis=0)


def all_rows(place, pieces, others):
    width = pieces[0].shape[0]
    placed = []
    for j, (piece, other) in enumerate(zip(pieces, others)):
        at = 2 * ((place.a - j) % place.na)
        placed.append(((at + place.c) * width, piece))
        placed.append(((at + 1 - place.c) * width, other))
    return assemble(place.ndp * width, placed)


def queue_gather(place, own):
    return lax.all_gather(own, BOTH, axis=0, tiled=True, axis_index_groups=place.group_ac)


def core_halves(place, value):
    width = value.shape[1] // place.ndp

    def side(which):
        return jnp.concatenate(
            [
                lax.dynamic_slice_in_dim(value, (2 * j + which) * width, width, axis=1)
                for j in range(place.na)
            ],
            axis=1,
        )

    return side(place.c), side(1 - place.c)


def core_far(place, far, right):
    share = dot_tn(far, right).astype(jnp.bfloat16)
    return send(share, place.core), share


def core_near(near, right, got):
    return (dot_tn(near, right) + got.astype(jnp.float32)).astype(jnp.bfloat16)


def queue_scatter(place, value):
    return lax.psum_scatter(
        value, "dp", scatter_dimension=0, tiled=True, axis_index_groups=place.group_a
    )


def to_owner(place, value):
    return jnp.where(place.keeper, value, send(value, place.swap)).astype(jnp.float32)


def vector_grads(place, sums):
    parts = [send(sums, place.across_x), send(sums, place.across_y), send(sums, place.across_both)]
    sums = sums + parts[0] + (parts[1] + parts[2])
    sums = sums + send(sums, place.core)
    width = sums.shape[1] // place.ndp

    def block(a):
        return lax.dynamic_slice_in_dim(sums, (2 * a + place.b) * width, width, axis=1)

    total = block(place.a)
    for step in range(1, place.na):
        total = total + send(block((place.a + step) % place.na), place.jump(step))
    return total


def far_rows(place, value):
    y, b, q = place.y, place.b, value.shape[0] // 8
    return jnp.concatenate(
        [
            rows_at(value, (2 * (1 - y) + 1 - b) * q, q),
            rows_at(value, (2 * (1 - y) + b) * q, q),
            rows_at(value, (4 + 2 * (1 - b) + 1 - y) * q, q),
            rows_at(value, (4 + 2 * (1 - b) + y) * q, q),
        ],
        axis=0,
    )


def near_rows(place, value):
    y, b, q = place.y, place.b, value.shape[0] // 8
    return jnp.concatenate(
        [
            rows_at(value, (2 * y + 1 - b) * q, q),
            rows_at(value, (4 + 2 * b + 1 - y) * q, q),
            rows_at(value, (2 * y + b) * q, q),
            rows_at(value, (4 + 2 * b + y) * q, q),
        ],
        axis=0,
    )


def send_far(place, away):
    q = away.shape[0] // 4
    return (
        send(away[:q], place.across_y),
        send(away[2 * q : 3 * q], place.across_x),
        send(away[q : 2 * q], place.across_y),
        send(away[3 * q :], place.across_x),
    )


def sum_near(place, here, got):
    pass_a, pass_b, keep_a, keep_b = got
    q = pass_a.shape[0]
    share_a = (here[:q] + pass_a.astype(jnp.float32)).astype(jnp.bfloat16)
    share_b = (here[q : 2 * q] + pass_b.astype(jnp.float32)).astype(jnp.bfloat16)
    last_a = send(share_a, place.across_x)
    last_b = send(share_b, place.across_y)
    return (
        here[2 * q :]
        + jnp.concatenate([keep_a, keep_b], axis=0).astype(jnp.float32)
        + jnp.concatenate([last_a, last_b], axis=0).astype(jnp.float32)
    )


def gather_rows(place, own):
    q = own.shape[0] // 2
    y, b = place.y, place.b
    own_a, own_b = own[:q], own[q:]
    a_x = send(own_a, place.across_x)
    b_y = send(own_b, place.across_y)
    a_y = send(own_a, place.across_y)
    b_x = send(own_b, place.across_x)
    a_xy = send(a_x, place.across_y)
    b_xy = send(b_y, place.across_x)
    placed = []
    for first, second, bb, yy in (
        (own_a, own_b, b, y),
        (a_x, b_x, 1 - b, y),
        (a_y, b_y, b, 1 - y),
        (a_xy, b_xy, 1 - b, 1 - y),
    ):
        starts = row_starts(q, bb, yy)
        placed += [(starts[0], first), (starts[1], second)]
    return assemble(8 * q, placed)


def bring_home(place, own):
    q = own.shape[0] // 2
    y, b = place.y, place.b
    got = send(own, place.home_x)
    pieces = (
        (own, b, y),
        (got, 1 - b, y),
        (send(own, place.home_y), b, 1 - y),
        (send(got, place.home_y), 1 - b, 1 - y),
    )
    placed = []
    for rows, bb, yy in pieces:
        rows = jnp.where(place.keeper, rows, send(rows, place.home_core))
        starts = row_starts(q, bb, yy)
        placed += [(starts[0], rows[:q]), (starts[1], rows[q:])]
    return assemble(8 * q, placed)


def rotate(values, tables):
    cosine, sine, scale = tables
    half = values.shape[-1] // 2
    first, second = values[:, :half], values[:, half:]
    return jnp.concatenate(
        [(first * cosine - second * sine) * scale, (second * cosine + first * sine) * scale],
        axis=-1,
    )


def unrotate(grads, tables):
    cosine, sine, scale = tables
    half = grads.shape[-1] // 2
    first, second = grads[:, :half] * scale, grads[:, half:] * scale
    return jnp.concatenate(
        [first * cosine + second * sine, second * cosine - first * sine], axis=-1
    )


def decay_mask(row_start, row_segment, col_segment, log_gamma):
    row_pos = row_start + jnp.arange(row_segment.shape[0], dtype=jnp.int32)
    col_pos = jnp.arange(col_segment.shape[0], dtype=jnp.int32)
    gap = row_pos[:, None] - col_pos[None, :]
    keep = (gap >= 0) & (row_segment[:, None] == col_segment[None, :])
    distance = jnp.maximum(gap, 0).astype(jnp.float32)
    return jnp.where(keep, jnp.exp(distance * log_gamma), 0.0)


def retention_forward(query_rot, key_rot, values, segment, log_gamma):
    length = query_rot.shape[0]
    rows = min(512, length)
    outputs, kept = [], []
    for start in range(0, length, rows):
        stop = start + rows
        mask = decay_mask(start, segment[start:stop], segment[:stop], log_gamma)
        raw = dot_nt(query_rot[start:stop], key_rot[:stop])
        weighted = (raw * mask).astype(jnp.bfloat16)
        kept.append(weighted)
        outputs.append(dot_nn(weighted, values[:stop]))
    return jnp.concatenate(outputs, axis=0), kept


def retention_backward(query_rot, key_rot, values, segment, log_gamma, grad_mixed, kept):
    length = query_rot.shape[0]
    rows = min(512, length)
    grad_query, grad_key, grad_value = [], [], []
    for block, start in enumerate(range(0, length, rows)):
        stop = start + rows
        grad_block = grad_mixed[start:stop]
        mask = decay_mask(start, segment[start:stop], segment[:stop], log_gamma)
        grad_weighted = dot_nt(grad_block, values[:stop])
        grad_raw = (grad_weighted * mask).astype(jnp.bfloat16)
        grad_query.append(dot_nn(grad_raw, key_rot[:stop]))
        grad_key.append(dot_tn(grad_raw, query_rot[start:stop]))
        grad_value.append(dot_tn(kept[block], grad_block))

    def total(parts):
        out = []
        for start in range(0, length, rows):
            pieces = [p[start : start + rows] for p in parts if p.shape[0] > start]
            out.append(functools.reduce(jnp.add, pieces))
        return jnp.concatenate(out, axis=0)

    return jnp.concatenate(grad_query, axis=0), total(grad_key), total(grad_value)


def local(ndp, nt, *args):
    return layer(ndp, nt, *args)


def layer(
    ndp,
    nt,
    tokens,
    w_query,
    w_key,
    w_value,
    w_gate,
    w_out,
    w_ffgate,
    w_ffup,
    w_down,
    norm1_gain,
    norm1_shift,
    norm2_gain,
    norm2_shift,
    segment_ids,
    decay_index,
    cotangent,
):
    place = Place(ndp, nt)
    heads = w_query.shape[1] // HEAD_KEY
    split = heads * HEAD_KEY
    inner = heads * HEAD_VALUE
    units = w_ffgate.shape[1]

    width = norm1_gain.shape[0]
    norms = jnp.concatenate([norm1_gain, norm1_shift, norm2_gain, norm2_shift])
    across = w_value.shape[1]
    extra = -(-norms.shape[0] // across)
    norms = jnp.pad(norms, (0, 16 * across - norms.shape[0])).reshape(16, across)
    own_value = my_sequence(place, jnp.concatenate([w_value, norms], axis=0))
    own_qk = my_sequence(place, jnp.concatenate([w_query, w_key], axis=1))
    shard_og = jnp.concatenate([w_out.T, w_gate], axis=1)
    shard_ff = jnp.concatenate([w_ffgate, w_ffup], axis=1)
    shard_down = w_down.T
    got_tokens = send(tokens, place.swap)
    got_og = send(shard_og, place.swap)
    got_ff = send(shard_ff, place.swap)
    got_down = send(shard_down, place.swap)
    got_cotangent = send(cotangent, place.swap)
    value_pieces, qk_pieces = [own_value], [own_qk]
    for _ in range(1, place.na):
        value_pieces.append(send(value_pieces[-1], place.ring))
        qk_pieces.append(send(qk_pieces[-1], place.ring))
    value_others = [send(piece, place.core) for piece in value_pieces]
    qk_others = [send(piece, place.core) for piece in qk_pieces]
    norms = jnp.zeros((place.ndp, 4 * width), norms.dtype)
    for j in range(place.na):
        for piece, c in ((value_pieces[j], place.c), (value_others[j], 1 - place.c)):
            row = piece[width : width + extra].reshape(1, extra * across)[:, : 4 * width]
            at = 2 * ((place.a - j) % place.na) + c
            norms = lax.dynamic_update_slice_in_dim(norms, row, at, axis=0)
    norms = norms.reshape(place.ndp, 4, width).transpose(1, 0, 2).reshape(4, place.ndp * width)
    norms = norms.astype(jnp.float32)
    gain_one, shift_one, gain_two, shift_two = norms[0], norms[1], norms[2], norms[3]
    value_pieces = [piece[:width] for piece in value_pieces]
    value_others = [piece[:width] for piece in value_others]
    got_og, value_pieces[-2] = together(got_og, value_pieces[-2])
    got_tokens, qk_pieces[-2] = together(got_tokens, qk_pieces[-2])
    got_ff, got_down, value_pieces[-1] = together(got_ff, got_down, value_pieces[-1])
    own_og = pick(place.keeper, shard_og, got_og)
    own_ff = pick(place.keeper, shard_ff, got_ff)
    own_down = pick(place.keeper, shard_down, got_down)
    inputs = pick(place.keeper, tokens, got_tokens)
    full_value = all_rows(place, value_pieces, value_others)
    full_qk = all_rows(place, qk_pieces, qk_others)
    full_og = queue_gather(place, own_og)
    full_ff = queue_gather(place, own_ff)
    full_down = queue_gather(place, own_down)
    full_out, full_gate = full_og[:, :inner], full_og[:, inner:]
    segment = my_sequence(place, segment_ids)
    decay = jnp.where(place.keeper, decay_index, send(decay_index, place.core))
    log_gamma = jnp.log1p(-jnp.exp2(-5.0 - decay.astype(jnp.float32)))

    normed_all, _ = norm_parts(inputs.astype(jnp.float32), EPSILON)
    first_in = (normed_all * gain_one + shift_one).astype(jnp.bfloat16)
    qk = dot_nn(first_in, full_qk)
    values = dot_nn(first_in, full_value).astype(jnp.bfloat16)
    cosine, sine, growth = xpos_tables(LENGTH, HEAD_KEY)
    query_tables = (cosine, sine, growth)
    key_tables = (cosine, sine, 1.0 / growth)
    query_rot, key_rot = [], []
    for h in range(heads):
        query = qk[:, h * HEAD_KEY : (h + 1) * HEAD_KEY]
        keys = qk[:, split + h * HEAD_KEY : split + (h + 1) * HEAD_KEY]
        query_rot.append(rotate(query, query_tables).astype(jnp.bfloat16))
        key_rot.append((rotate(keys, key_tables) * HEAD_KEY ** (-0.5)).astype(jnp.bfloat16))
    grouped, group_scale, kept = [], [], []
    for h in range(heads):
        at = slice(h * HEAD_VALUE, (h + 1) * HEAD_VALUE)
        mixed, weighted = retention_forward(
            query_rot[h], key_rot[h], values[:, at], segment, log_gamma[h]
        )
        normed, scale = norm_parts(mixed, GROUP_EPSILON)
        grouped.append(normed)
        group_scale.append(scale)
        kept.append(weighted)
    grouped_flat = jnp.concatenate(grouped, axis=1)
    gate = dot_nn(first_in, full_gate)
    sigmoid_gate = jax.nn.sigmoid(gate)
    swish = gate * sigmoid_gate
    gated = (swish * grouped_flat).astype(jnp.bfloat16)
    got_cotangent, gated = together(got_cotangent, gated)
    grad_feed = pick(place.keeper, cotangent, got_cotangent)

    own_inputs = my_rows(place, inputs).astype(jnp.float32)
    away = dot_nt(far_rows(place, gated), full_out).astype(jnp.bfloat16)
    got = send_far(place, away)
    here = dot_nt(near_rows(place, after(gated, away)), full_out)
    middle = own_inputs + sum_near(place, here, got)
    normed_two, scale_two = norm_parts(middle, EPSILON)
    second_in = gather_rows(place, (normed_two * gain_two + shift_two).astype(jnp.bfloat16))

    ff_both = dot_nn(second_in, full_ff)
    ff_gate, ff_up = ff_both[:, :units], ff_both[:, units:]
    normal_cdf = 0.5 * (1.0 + lax.erf(ff_gate * INV_ROOT2))
    activation = ff_gate * normal_cdf
    hidden = (activation * ff_up).astype(jnp.bfloat16)
    feed_near, feed_far = core_halves(place, grad_feed)
    hidden, full_down = together(hidden, full_down)
    down_got, _ = core_far(place, feed_far, hidden)
    down_sum = core_near(feed_near, hidden, down_got)
    share_down = queue_scatter(place, down_sum)
    e_away = dot_nt(far_rows(place, hidden), full_down).astype(jnp.bfloat16)
    grad_hidden = dot_nn(grad_feed, full_down)
    density = jnp.exp(-0.5 * ff_gate * ff_gate) * INV_ROOT_TWO_PI
    grad_ff = jnp.concatenate(
        [
            (grad_hidden * ff_up * (normal_cdf + ff_gate * density)).astype(jnp.bfloat16),
            (grad_hidden * activation).astype(jnp.bfloat16),
        ],
        axis=1,
    )
    second_near, second_far = core_halves(place, second_in)
    ff_got, ff_far = core_far(place, second_far, grad_ff)
    away = dot_nt(far_rows(place, after(grad_ff, ff_far)), full_ff).astype(jnp.bfloat16)
    got = send_far(place, away)
    ff_sum = core_near(second_near, after(grad_ff, away), ff_got)
    ready, ff_sum = together(grad_ff, ff_sum)
    share_ff = queue_scatter(place, ff_sum)
    here = dot_nt(near_rows(place, ready), full_ff)
    grad_second = sum_near(place, here, got)
    grad_middle = my_rows(place, grad_feed).astype(jnp.float32) + norm_back(
        grad_second, normed_two, scale_two, gain_two
    )
    grad_branch = gather_rows(place, grad_middle.astype(jnp.bfloat16))
    e_got = send_far(place, e_away)
    branch_near, branch_far = core_halves(place, grad_branch)
    first_near, first_far = core_halves(place, first_in)
    out_got, out_far = core_far(place, branch_far, gated)
    grad_gated = dot_nn(after(grad_branch, out_far), full_out)
    swish_slope = sigmoid_gate * (1.0 + gate * (1.0 - sigmoid_gate))
    grad_gate_in = (grad_gated * grouped_flat * swish_slope).astype(jnp.bfloat16)
    grad_grouped = grad_gated * swish
    gate_got, gate_far = core_far(place, first_far, grad_gate_in)
    out_sum = core_near(branch_near, after(gated, gate_far), out_got)
    gate_sum = core_near(first_near, after(grad_gate_in, out_sum), gate_got)
    og_sum = jnp.concatenate([out_sum, gate_sum], axis=1)
    grad_grouped, og_sum, e_near = together(grad_grouped, og_sum, near_rows(place, hidden))
    share_og = queue_scatter(place, og_sum)
    here = dot_nt(e_near, full_down)
    feed = sum_near(place, here, e_got)
    block_out = bring_home(place, (middle + feed).astype(jnp.bfloat16))
    grad_qs, grad_ks, grad_vs = [], [], []
    for h in range(heads):
        at = slice(h * HEAD_VALUE, (h + 1) * HEAD_VALUE)
        grad_mixed = norm_back(grad_grouped[:, at], grouped[h], group_scale[h], 1.0).astype(
            jnp.bfloat16
        )
        grad_qrot, grad_krot, grad_value = retention_backward(
            query_rot[h], key_rot[h], values[:, at], segment, log_gamma[h], grad_mixed, kept[h]
        )
        grad_qs.append(unrotate(grad_qrot, query_tables).astype(jnp.bfloat16))
        grad_ks.append((unrotate(grad_krot, key_tables) * HEAD_KEY ** (-0.5)).astype(jnp.bfloat16))
        grad_vs.append(grad_value.astype(jnp.bfloat16))
    grad_vqk = jnp.concatenate(grad_vs + grad_qs + grad_ks, axis=1)

    def first_product(gate_rows, vqk_rows):
        return (
            dot_nt(gate_rows, full_gate)
            + dot_nt(vqk_rows[:, :inner], full_value)
            + dot_nt(vqk_rows[:, inner:], full_qk)
        )

    vqk_got, vqk_far = core_far(place, first_far, grad_vqk)
    ready = after(grad_vqk, vqk_far)
    away = first_product(far_rows(place, grad_gate_in), far_rows(place, ready)).astype(jnp.bfloat16)
    got = send_far(place, away)
    vqk_sum = core_near(first_near, after(grad_vqk, away), vqk_got)
    ready, vqk_sum = together(grad_vqk, vqk_sum)
    share_vqk = queue_scatter(place, vqk_sum)
    here = first_product(near_rows(place, grad_gate_in), near_rows(place, ready))
    grad_first = sum_near(place, here, got)
    normed_one, scale_one = norm_parts(own_inputs, EPSILON)
    grad_tokens = grad_middle + norm_back(grad_first, normed_one, scale_one, gain_one)
    grad_tokens = bring_home(place, grad_tokens.astype(jnp.bfloat16)).astype(jnp.float32)
    vectors = vector_grads(
        place,
        jnp.stack(
            [
                jnp.sum(grad_first * normed_one, axis=0),
                jnp.sum(grad_first, axis=0),
                jnp.sum(grad_second * normed_two, axis=0),
                jnp.sum(grad_second, axis=0),
            ]
        ),
    )
    share_down = to_owner(place, share_down).T
    share_ff = to_owner(place, share_ff)
    share_og = to_owner(place, share_og)
    share_vqk = to_owner(place, share_vqk)
    return (
        block_out,
        grad_tokens,
        share_vqk[:, inner : inner + split],
        share_vqk[:, inner + split :],
        share_vqk[:, :inner],
        share_og[:, inner:],
        share_og[:, :inner].T,
        share_ff[:, :units],
        share_ff[:, units:],
        share_down,
        vectors[0],
        vectors[1],
        vectors[2],
        vectors[3],
    )


def solution(mesh):
    placed = (
        P("dp", None),
        P("dp", "tensor"),
        P("dp", "tensor"),
        P("dp", "tensor"),
        P("dp", "tensor"),
        P("tensor", "dp"),
        P("dp", "tensor"),
        P("dp", "tensor"),
        P("tensor", "dp"),
        P("dp"),
        P("dp"),
        P("dp"),
        P("dp"),
        P("dp"),
        P("tensor"),
        P("dp", None),
    )
    return jax.shard_map(
        functools.partial(local, mesh.shape["dp"], mesh.shape["tensor"]),
        mesh=mesh,
        in_specs=placed,
        out_specs=(
            P("dp", None),
            P("dp", None),
            P("dp", "tensor"),
            P("dp", "tensor"),
            P("dp", "tensor"),
            P("dp", "tensor"),
            P("tensor", "dp"),
            P("dp", "tensor"),
            P("dp", "tensor"),
            P("tensor", "dp"),
            P("dp"),
            P("dp"),
            P("dp"),
            P("dp"),
        ),
        check_vma=False,
    )
```

time: 2240 us -> 839 us (0.37)
  the two profiles are of different devices: /device:TPU:0 before, /device:TPU:1 now
where the time goes in v1:
time: 839 us; the launch traced here: 829 us
  waiting for transfers between devices  251 us (30%)
  matrix products  202 us (24%)
  starting transfers between devices  145 us (17%)
  local copies, waits for them, and re-layouts  128 us (15%)
  other arithmetic  85.6 us (10%)
  between operations  17.9 us (2%)
    ppermute x89, waiting for transfers between devices, send(): return lax.ppermute(value, BOTH, pairs)  236 us
    ppermute x89, starting transfers between devices, send(): return lax.ppermute(value, BOTH, pairs)  145 us
    dot_general x20, matrix products, dot_nt(): lax.dot_general(left, right, (((1,), (1,)), ((), ())), preferred_element_...  70.3 us
    dot_general x14, matrix products, dot_nn(): lax.dot_general(left, right, (((1,), (0,)), ((), ())), preferred_element_...  67.2 us
    dot_general x18, matrix products, dot_tn(): lax.dot_general(left, right, (((0,), (0,)), ((), ())), preferred_element_...  64.3 us
    dynamic_update_slice x45, local copies, waits for them, and re-layouts, assemble(): whole = lax.dynamic_update_slice_in_dim(whole, rows, start, axis=0)  41.8 us
    unnamed x293, local copies, waits for them, and re-layouts  25.2 us
    another operation x10, local copies, waits for them, and re-layouts  19.6 us
  transfers between devices with their start and end apart: 96, of which 38 were waited for; matrix products, arithmetic and copies ran while one was open for 45% of the time, Pallas kernels for 0%

profile of v1, /device:TPU:1, one launch (start us, length us, event | category | flops | bytes accessed | tf_op | source)
XLA Modules:
  0.0 829.1 jit_solution(4599261539296812110)
XLA Ops:
  14.9 6.2 collective-permute-done.5
  26.4 8.3 %collective-permute-done.7 = bf16[272,1024]{1,0:T(8,128)(2,1)S(1)} collective-permute-done((bf16[272,1024]{1,0:T(8,128)(2,1)S(1)}, bf16[272,1024]{1,0:T(8,128)(2,1)S(1)}, u32[]{:S(2)}, u32[]{:S(2)}) %collective-permute-start.7) | collective-permute-done | bytes 557088 | tf_op jit(solution)/shard_map/ppermute | solution.py:119
  35.7 9.2 %collective-permute-done.9 = bf16[272,1024]{1,0:T(8,128)(2,1)S(1)} collective-permute-done((bf16[272,1024]{1,0:T(8,128)(2,1)S(1)}, bf16[272,1024]{1,0:T(8,128)(2,1)S(1)}, u32[]{:S(2)}, u32[]{:S(2)}) %collective-permute-start.9) | collective-permute-done | bytes 557088 | tf_op jit(solution)/shard_map/ppermute | solution.py:119
  47.3 10.5 %collective-permute-start.21 = (bf16[256,2048]{1,0:T(8,128)(2,1)S(1)}, bf16[256,2048]{1,0:T(8,128)(2,1)}, u32[]{:S(2)}, u32[]{:S(2)}) collective-permute-start(bf16[256,2048]{1,0:T(8,128)(2,1)S(1)} %constant_dynamic-update-slice_fusion.30), channel_id=1, source_target_pairs={{1,4},{3,6},{4,1},{6,3},{9,12},{11,14},{12,9},{14,11},{17,20},{19,... | collective-permute-start | bytes 3145736 | tf_op jit(solution)/shard_map/ppermute | solution.py:119
  61.1 13.6 %collective-permute-done.11 = bf16[272,1024]{1,0:T(8,128)(2,1)} collective-permute-done((bf16[272,1024]{1,0:T(8,128)(2,1)}, bf16[272,1024]{1,0:T(8,128)(2,1)}, u32[]{:S(2)}, u32[]{:S(2)}) %collective-permute-start.11) | collective-permute-done | bytes 557088 | tf_op jit(solution)/shard_map/ppermute | solution.py:119
  97.2 39.3 %collective-permute-done.19 = s32[1024]{0:T(1024)S(1)} collective-permute-done((s32[1024]{0:T(1024)S(1)}, s32[1024]{0:T(1024)S(1)}, u32[]{:S(2)}, u32[]{:S(2)}) %collective-permute-start.19) | collective-permute-done | bytes 4128 | tf_op jit(solution)/shard_map/ppermute | solution.py:119
  149.7 9.0 %collective-permute-done.3 = bf16[256,1024]{1,0:T(8,128)(2,1)S(1)} collective-permute-done((bf16[256,1024]{1,0:T(8,128)(2,1)}, bf16[256,1024]{1,0:T(8,128)(2,1)S(1)}, u32[]{:S(2)}, u32[]{:S(2)}) %collective-permute-start.3) | collective-permute-done | bytes 524320 | tf_op jit(solution)/shard_map/ppermute | solution.py:119
  166.6 17.1 %collective-permute-done.17 = bf16[256,1024]{1,0:T(8,128)(2,1)S(1)} collective-permute-done((bf16[256,1024]{1,0:T(8,128)(2,1)S(1)}, bf16[256,1024]{1,0:T(8,128)(2,1)S(1)}, u32[]{:S(2)}, u32[]{:S(2)}) %collective-permute-start.17) | collective-permute-done | bytes 524320 | tf_op jit(solution)/shard_map/ppermute | solution.py:119
  203.7 7.1 fusion.349
  222.2 7.7 convolution_convert_fusion.5
  238.3 11.0 %multiply_convert_fusion.3 = (bf16[1024,1024]{1,0:T(8,128)(2,1)S(1)}, f32[1024,1024]{1,0:T(8,128)}) fusion(f32[1024,512]{1,0:T(8,128)} %subtract_multiply_fusion.1, f32[1024,512]{1,0:T(8,128)S(1)} %subtract_multiply_fusion.2, bf16[1024,2048]{1,0:T(8,128)(2,1)} %copy-done.7, bf16[2048,2048]{1,0:T(8,128)(2,1)} %all-gather.4.cloned.1.call-done), kind=kOutput, calls=%fused_computation.29 | convolution fusion | flops 4302307328 | bytes 18874368 | tf_op jit(solution)/shard_map/dot_general | solution.py:50
  257.8 7.4 collective-permute-done.25
  271.1 5.3 collective-permute-done.23
  277.4 11.2 %collective-permute-done.26 = bf16[128,2048]{1,0:T(8,128)(2,1)S(1)} collective-permute-done((bf16[128,2048]{1,0:T(8,128)(2,1)S(1)}, bf16[128,2048]{1,0:T(8,128)(2,1)S(1)}, u32[]{:S(2)}, u32[]{:S(2)}) %collective-permute-start.26) | collective-permute-done | bytes 524320 | tf_op jit(solution)/shard_map/ppermute | solution.py:119
  296.0 6.9 collective-permute-done.29
  304.2 10.0 %collective-permute-done.30 = bf16[128,2048]{1,0:T(8,128)(2,1)S(1)} collective-permute-done((bf16[128,2048]{1,0:T(8,128)(2,1)S(1)}, bf16[128,2048]{1,0:T(8,128)(2,1)S(1)}, u32[]{:S(2)}, u32[]{:S(2)}) %collective-permute-start.30) | collective-permute-done | bytes 524320 | tf_op jit(solution)/shard_map/ppermute | solution.py:119
  314.4 11.1 %collective-permute-done.33 = bf16[128,2048]{1,0:T(8,128)(2,1)S(1)} collective-permute-done((bf16[128,2048]{1,0:T(8,128)(2,1)S(1)}, bf16[128,2048]{1,0:T(8,128)(2,1)S(1)}, u32[]{:S(2)}, u32[]{:S(2)}) %collective-permute-start.33) | collective-permute-done | bytes 524320 | tf_op jit(solution)/shard_map/ppermute | solution.py:119
  329.7 12.5 %fusion.350 = f32[1024,2048]{1,0:T(8,128)S(1)} fusion(bf16[1024,2048]{1,0:T(8,128)(2,1)} %copy-done.8, bf16[2048,2048]{1,0:T(8,128)(2,1)} %all-gather.6.cloned.1.call-done), kind=kOutput, calls=%fused_computation.643 | convolution fusion | flops 8589934592 | bytes 20971520 | tf_op jit(solution)/shard_map/dot_general | solution.py:50
  347.9 11.1 %fusion.11 = (bf16[1024,1024]{1,0:T(8,128)(2,1)S(1)}, bf16[1024,1024]{1,0:T(8,128)(2,1)S(1)}) fusion(f32[1024,2048]{1,0:T(8,128)} %copy-done.15, bf16[1024,2048]{1,0:T(8,128)(2,1)} %copy-done, bf16[2048,1024]{1,0:T(8,128)(2,1)} %all-gather.8.cloned.1.call-done), kind=kOutput, calls=%fused_computation.16 | convolution fusion | flops 4309647360 | bytes 20971520 | tf_op jit(solution)/shard_map/dot_general | solution.py:50
  359.0 6.7 convolution_convert_fusion.1
  374.6 9.8 %convolution_convert_fusion.3 = bf16[512,2048]{1,0:T(8,128)(2,1)S(1)} fusion(bf16[2048,2048]{1,0:T(8,128)(2,1)} %all-gather.6.cloned.1.call-done, bf16[128,2048]{1,0:T(8,128)(2,1)S(1)} %get-tuple-element.168, bf16[128,2048]{1,0:T(8,128)(2,1)S(1)} %get-tuple-element.169, bf16[128,2048]{1,0:T(8,128)(2,1)S(1)} %get-tuple-element.170, ...), kind=kOutput, calls=%fused_computation.54 | convolution fusion | flops 4304404480 | bytes 12582912 | tf_op jit(solution)/shard_map/dot_general | solution.py:56
  394.3 10.6 %add_convert_fusion.1 = bf16[1024,2048]{1,0:T(8,128)(2,1)} fusion(bf16[1024,2048]{1,0:T(8,128)(2,1)} %collective-permute-done.35, bf16[1024,2048]{1,0:T(8,128)(2,1)} %copy-done.9, bf16[1024,256]{1,0:T(8,128)(2,1)} %get-tuple-element.164, bf16[1024,256]{1,0:T(8,128)(2,1)} %get-tuple-element.165, bf16[1024,256]{1,0:T(8,128)(2,1)} %get-tuple-element.166, ...), kind=kOutput, calls=%fused_computation.9 | convolution fusion | flops 4309647360 | bytes 14680064 | tf_op jit(solution)/shard_map/dot_general | solution.py:62
  406.6 7.1 fusion.67
  421.9 5.6 collective-permute-done.39
  447.0 9.1 %collective-permute-done.43 = bf16[128,2048]{1,0:T(8,128)(2,1)S(1)} collective-permute-done((bf16[128,2048]{1,0:T(8,128)(2,1)}, bf16[128,2048]{1,0:T(8,128)(2,1)S(1)}, u32[]{:S(2)}, u32[]{:S(2)}) %collective-permute-start.43) | collective-permute-done | bytes 524320 | tf_op jit(solution)/shard_map/ppermute | solution.py:119
  462.8 7.3 collective-permute-done.46
  470.9 7.6 collective-permute-done.47
  487.0 5.6 collective-permute-start.48
  492.6 9.8 %multiply_convert_fusion = (bf16[1024,1024]{1,0:T(8,128)(2,1)S(1)}, f32[1024,1024]{1,0:T(8,128)}) fusion(f32[1024,1024]{1,0:T(8,128)S(1)} %copy-done.135, f32[1024,512]{1,0:T(8,128)S(1)} %copy-done.4, f32[1024,512]{1,0:T(8,128)S(1)} %copy-done.2, bf16[1024,2048]{1,0:T(8,128)(2,1)} %constant_dynamic-update-slice_fusion, bf16[2048,2048]{1,0:T(8,128)(2,1)S(1)} %bitcast.106), kind=kOutput, calls=%fused_computation.25 | convolution fusion | flops 4308598784 | bytes 23068672 | tf_op jit(solution)/shard_map/dot_general | solution.py:50
  515.0 6.7 fusion.21
  526.2 5.4 add_convert_fusion.5
  571.1 4.6 fusion.250
  601.2 6.6 convolution_convert_fusion
  614.2 4.6 fusion.134
  618.8 6.6 collective-permute-done.53
  632.4 4.6 add_convert_fusion.3
  652.1 5.8 collective-permute-done.58
  662.9 18.4 %collective-permute-start.65 = (bf16[128,2048]{1,0:T(8,128)(2,1)}, bf16[128,2048]{1,0:T(8,128)(2,1)}, u32[]{:S(2)}, u32[]{:S(2)}) collective-permute-start(bf16[128,2048]{1,0:T(8,128)(2,1)} %get-tuple-element.184), channel_id=1, source_target_pairs={{0,4},{1,5},{2,6},{3,7},{4,0},{5,1},{6,2},{7,3},{8,12},{9,13},{10,... | collective-permute-start | bytes 1572872 | tf_op jit(solution)/shard_map/ppermute | solution.py:119
  682.9 8.1 add_convert_fusion
  692.9 4.8 fusion.131
  697.7 4.7 add_add_fusion
  706.9 5.6 collective-permute-start.67
  714.6 10.4 %collective-permute-done.67 = bf16[128,2048]{1,0:T(8,128)(2,1)} collective-permute-done((bf16[128,2048]{1,0:T(8,128)(2,1)}, bf16[128,2048]{1,0:T(8,128)(2,1)}, u32[]{:S(2)}, u32[]{:S(2)}) %collective-permute-start.67) | collective-permute-done | bytes 524320 | tf_op jit(solution)/shard_map/ppermute | solution.py:119
  743.6 6.6 collective-permute-start.87
  753.1 5.4 collective-permute-start.79
  779.9 6.7 convert_element_type.337
  786.6 14.9 %reduce-scatter.5.cloned.1.call-done = bf16[256,2048]{1,0:T(8,128)(2,1)} async-done(((bf16[1024,2048]{1,0:T(8,128)(2,1)}), bf16[256,2048]{1,0:T(8,128)(2,1)}) %reduce-scatter.5.cloned.1.call-update) | async-done | bytes 1048592 | tf_op jit(solution)/shard_map/reduce_scatter | solution.py:195
  812.2 6.0 collective-permute-done.77
  (700 shorter events, 380.9 us)
Async XLA Ops:
  7.2 231.1 %all-gather.4.cloned.1.call-start = ((), (), s32[]{:S(2)}) async-start(), calls=%async_computation.4 | async-start | bytes 9437184 | tf_op jit(solution)/shard_map/all_gather | solution.py:167
  22.6 23.1 %collective-permute-start.13 = (bf16[256,2048]{1,0:T(8,128)(2,1)S(1)}, bf16[256,2048]{1,0:T(8,128)(2,1)S(1)}, u32[]{:S(2)}, u32[]{:S(2)}) collective-permute-start(bf16[256,2048]{1,0:T(8,128)(2,1)S(1)} %pad_maximum_fusion.10), channel_id=1, source_target_pairs={{1,4},{3,6},{4,1},{6,3},{9,12},{11,14},{12,9},{14,11},{17,20},{19,... | collective-permute-start | bytes 3145736 | tf_op jit(solution)/shard_map/ppermute | solution.py:119
  47.2 282.6 %all-gather.6.cloned.1.call-start = ((), (), s32[]{:S(2)}) async-start(), calls=%async_computation.5 | async-start | bytes 9437184 | tf_op jit(solution)/shard_map/all_gather | solution.py:167
  47.3 29.8 %collective-permute-start.21 = (bf16[256,2048]{1,0:T(8,128)(2,1)S(1)}, bf16[256,2048]{1,0:T(8,128)(2,1)}, u32[]{:S(2)}, u32[]{:S(2)}) collective-permute-start(bf16[256,2048]{1,0:T(8,128)(2,1)S(1)} %constant_dynamic-update-slice_fusion.30), channel_id=1, source_target_pairs={{1,4},{3,6},{4,1},{6,3},{9,12},{11,14},{12,9},{14,11},{17,20},{19,... | collective-permute-start | bytes 3145736 | tf_op jit(solution)/shard_map/ppermute | solution.py:119
  79.5 268.4 %all-gather.8.cloned.1.call-start = ((), (), s32[]{:S(2)}) async-start(), calls=%async_computation.6 | async-start | bytes 4718592 | tf_op jit(solution)/shard_map/all_gather | solution.py:167
  83.9 109.5 %collective-permute-start = (bf16[1024,2048]{1,0:T(8,128)(2,1)}, bf16[1024,2048]{1,0:T(8,128)(2,1)}, u32[]{:S(2)}, u32[]{:S(2)}) collective-permute-start(bf16[1024,2048]{1,0:T(8,128)(2,1)} %param.16), channel_id=1, source_target_pairs={{1,4},{3,6},{4,1},{6,3},{9,12},{11,14},{12,9},{14,11},{17,20},{19,... | collective-permute-start | bytes 12582920 | tf_op jit(solution)/shard_map/ppermute | solution.py:119
  86.2 50.3 %collective-permute-start.19 = (s32[1024]{0:T(1024)S(1)}, s32[1024]{0:T(1024)S(1)}, u32[]{:S(2)}, u32[]{:S(2)}) collective-permute-start(s32[1024]{0:T(1024)S(1)} %copy-done.122), channel_id=1, source_target_pairs={{1,4},{3,6},{4,1},{6,3},{9,12},{11,14},{12,9},{14,11},{17,20},{19,... | collective-permute-start | bytes 12296 | tf_op jit(solution)/shard_map/ppermute | solution.py:119
  89.6 159.8 %collective-permute-start.4 = (bf16[1024,2048]{1,0:T(8,128)(2,1)}, bf16[1024,2048]{1,0:T(8,128)(2,1)}, u32[]{:S(2)}, u32[]{:S(2)}) collective-permute-start(bf16[1024,2048]{1,0:T(8,128)(2,1)} %param.31), channel_id=1, source_target_pairs={{1,4},{3,6},{4,1},{6,3},{9,12},{11,14},{12,9},{14,11},{17,20},{19,... | collective-permute-start | bytes 12582920 | tf_op jit(solution)/shard_map/ppermute | solution.py:119
  96.8 43.8 %collective-permute-start.14 = (bf16[256,1024]{1,0:T(8,128)(2,1)}, bf16[256,1024]{1,0:T(8,128)(2,1)}, u32[]{:S(2)}, u32[]{:S(2)}) collective-permute-start(bf16[256,1024]{1,0:T(8,128)(2,1)} %get-tuple-element.99), channel_id=1, source_target_pairs={{0,1},{1,0},{2,3},{3,2},{4,5},{5,4},{6,7},{7,6},{8,9},{9,8},{10,11... | collective-permute-start | bytes 1572872 | tf_op jit(solution)/shard_map/ppermute | solution.py:119
  97.2 42.9 %collective-permute-start.2 = (bf16[256,1024]{1,0:T(8,128)(2,1)}, bf16[256,1024]{1,0:T(8,128)(2,1)}, u32[]{:S(2)}, u32[]{:S(2)}) collective-permute-start(bf16[256,1024]{1,0:T(8,128)(2,1)} %get-tuple-element.99), channel_id=1, source_target_pairs={{0,8},{1,9},{2,10},{3,11},{4,12},{5,13},{6,14},{7,15},{8,16},{9,17... | collective-permute-start | bytes 1572872 | tf_op jit(solution)/shard_map/ppermute | solution.py:119
  158.8 24.9 %collective-permute-start.17 = (bf16[256,1024]{1,0:T(8,128)(2,1)S(1)}, bf16[256,1024]{1,0:T(8,128)(2,1)S(1)}, u32[]{:S(2)}, u32[]{:S(2)}) collective-permute-start(bf16[256,1024]{1,0:T(8,128)(2,1)S(1)} %collective-permute-done.3), channel_id=1, source_target_pairs={{0,8},{1,9},{2,10},{3,11},{4,12},{5,13},{6,14},{7,15},{8,16},{9,17... | collective-permute-start | bytes 1572872 | tf_op jit(solution)/shard_map/ppermute | solution.py:119
  162.4 23.9 %collective-permute-start.10 = (bf16[272,1024]{1,0:T(8,128)(2,1)}, bf16[272,1024]{1,0:T(8,128)(2,1)}, u32[]{:S(2)}, u32[]{:S(2)}) collective-permute-start(bf16[272,1024]{1,0:T(8,128)(2,1)} %copy-done.95), channel_id=1, source_target_pairs={{0,1},{1,0},{2,3},{3,2},{4,5},{5,4},{6,7},{7,6},{8,9},{9,8},{10,11... | collective-permute-start | bytes 1671176 | tf_op jit(solution)/shard_map/ppermute | solution.py:119
  165.7 24.9 %collective-permute-start.12 = (bf16[272,1024]{1,0:T(8,128)(2,1)}, bf16[272,1024]{1,0:T(8,128)(2,1)}, u32[]{:S(2)}, u32[]{:S(2)}) collective-permute-start(bf16[272,1024]{1,0:T(8,128)(2,1)} %collective-permute-done.11), channel_id=1, source_target_pairs={{0,1},{1,0},{2,3},{3,2},{4,5},{5,4},{6,7},{7,6},{8,9},{9,8},{10,11... | collective-permute-start | bytes 1671176 | tf_op jit(solution)/shard_map/ppermute | solution.py:119
  166.5 346.2 %reduce-scatter.11.cloned.1.call-start = ((), (), s32[]{:S(2)}) async-start(), calls=%async_computation.10 | async-start | bytes 2621440 | tf_op jit(solution)/shard_map/reduce_scatter | solution.py:195
  253.7 22.8 %collective-permute-start.23 = (bf16[128,2048]{1,0:T(8,128)(2,1)S(1)}, bf16[128,2048]{1,0:T(8,128)(2,1)S(1)}, u32[]{:S(2)}, u32[]{:S(2)}) collective-permute-start(bf16[128,2048]{1,0:T(8,128)(2,1)S(1)} %get-tuple-element.209), channel_id=1, source_target_pairs={{0,2},{1,3},{2,0},{3,1},{4,6},{5,7},{6,4},{7,5},{8,10},{9,11},{10,... | collective-permute-start | bytes 1572872 | tf_op jit(solution)/shard_map/ppermute | solution.py:119
  254.0 23.4 %collective-permute-start.24 = (bf16[128,2048]{1,0:T(8,128)(2,1)S(1)}, bf16[128,2048]{1,0:T(8,128)(2,1)S(1)}, u32[]{:S(2)}, u32[]{:S(2)}) collective-permute-start(bf16[128,2048]{1,0:T(8,128)(2,1)S(1)} %get-tuple-element.212), channel_id=1, source_target_pairs={{0,4},{1,5},{2,6},{3,7},{4,0},{5,1},{6,2},{7,3},{8,12},{9,13},{10,... | collective-permute-start | bytes 1572872 | tf_op jit(solution)/shard_map/ppermute | solution.py:119
  266.5 22.1 %collective-permute-start.26 = (bf16[128,2048]{1,0:T(8,128)(2,1)S(1)}, bf16[128,2048]{1,0:T(8,128)(2,1)S(1)}, u32[]{:S(2)}, u32[]{:S(2)}) collective-permute-start(bf16[128,2048]{1,0:T(8,128)(2,1)S(1)} %get-tuple-element.173), channel_id=1, source_target_pairs={{0,4},{1,5},{2,6},{3,7},{4,0},{5,1},{6,2},{7,3},{8,12},{9,13},{10,... | collective-permute-start | bytes 1572872 | tf_op jit(solution)/shard_map/ppermute | solution.py:119
  266.8 21.8 %collective-permute-start.28 = (bf16[128,2048]{1,0:T(8,128)(2,1)S(1)}, bf16[128,2048]{1,0:T(8,128)(2,1)S(1)}, u32[]{:S(2)}, u32[]{:S(2)}) collective-permute-start(bf16[128,2048]{1,0:T(8,128)(2,1)S(1)} %get-tuple-element.174), channel_id=1, source_target_pairs={{0,2},{1,3},{2,0},{3,1},{4,6},{5,7},{6,4},{7,5},{8,10},{9,11},{10,... | collective-permute-start | bytes 1572872 | tf_op jit(solution)/shard_map/ppermute | solution.py:119
  293.7 20.5 %collective-permute-start.30 = (bf16[128,2048]{1,0:T(8,128)(2,1)S(1)}, bf16[128,2048]{1,0:T(8,128)(2,1)S(1)}, u32[]{:S(2)}, u32[]{:S(2)}) collective-permute-start(bf16[128,2048]{1,0:T(8,128)(2,1)S(1)} %get-tuple-element.233), channel_id=1, source_target_pairs={{0,4},{1,5},{2,6},{3,7},{4,0},{5,1},{6,2},{7,3},{8,12},{9,13},{10,... | collective-permute-start | bytes 1572872 | tf_op jit(solution)/shard_map/ppermute | solution.py:119
  302.9 22.6 %collective-permute-start.33 = (bf16[128,2048]{1,0:T(8,128)(2,1)S(1)}, bf16[128,2048]{1,0:T(8,128)(2,1)S(1)}, u32[]{:S(2)}, u32[]{:S(2)}) collective-permute-start(bf16[128,2048]{1,0:T(8,128)(2,1)S(1)} %collective-permute-done.29), channel_id=1, source_target_pairs={{0,2},{1,3},{2,0},{3,1},{4,6},{5,7},{6,4},{7,5},{8,10},{9,11},{10,... | collective-permute-start | bytes 1572872 | tf_op jit(solution)/shard_map/ppermute | solution.py:119
  303.3 22.3 %collective-permute-start.34 = (bf16[128,2048]{1,0:T(8,128)(2,1)S(1)}, bf16[128,2048]{1,0:T(8,128)(2,1)S(1)}, u32[]{:S(2)}, u32[]{:S(2)}) collective-permute-start(bf16[128,2048]{1,0:T(8,128)(2,1)S(1)} %collective-permute-done.32), channel_id=1, source_target_pairs={{0,4},{1,5},{2,6},{3,7},{4,0},{5,1},{6,2},{7,3},{8,12},{9,13},{10,... | collective-permute-start | bytes 1572872 | tf_op jit(solution)/shard_map/ppermute | solution.py:119
  365.7 28.7 %collective-permute-start.35 = (bf16[1024,2048]{1,0:T(8,128)(2,1)}, bf16[1024,2048]{1,0:T(8,128)(2,1)}, u32[]{:S(2)}, u32[]{:S(2)}) collective-permute-start(bf16[1024,2048]{1,0:T(8,128)(2,1)} %convolution_convert_fusion.1), channel_id=1, source_target_pairs={{0,1},{1,0},{2,3},{3,2},{4,5},{5,4},{6,7},{7,6},{8,9},{9,8},{10,11... | collective-permute-start | bytes 12582920 | tf_op jit(solution)/shard_map/ppermute | solution.py:119
  385.8 28.0 %collective-permute-start.38 = (bf16[128,2048]{1,0:T(8,128)(2,1)}, bf16[128,2048]{1,0:T(8,128)(2,1)}, u32[]{:S(2)}, u32[]{:S(2)}) collective-permute-start(bf16[128,2048]{1,0:T(8,128)(2,1)} %get-tuple-element.207), channel_id=1, source_target_pairs={{0,2},{1,3},{2,0},{3,1},{4,6},{5,7},{6,4},{7,5},{8,10},{9,11},{10,... | collective-permute-start | bytes 1572872 | tf_op jit(solution)/shard_map/ppermute | solution.py:119
  386.2 27.7 %collective-permute-start.40 = (bf16[128,2048]{1,0:T(8,128)(2,1)}, bf16[128,2048]{1,0:T(8,128)(2,1)}, u32[]{:S(2)}, u32[]{:S(2)}) collective-permute-start(bf16[128,2048]{1,0:T(8,128)(2,1)} %get-tuple-element.206), channel_id=1, source_target_pairs={{0,4},{1,5},{2,6},{3,7},{4,0},{5,1},{6,2},{7,3},{8,12},{9,13},{10,... | collective-permute-start | bytes 1572872 | tf_op jit(solution)/shard_map/ppermute | solution.py:119
  387.3 34.7 %collective-permute-start.36 = (bf16[128,2048]{1,0:T(8,128)(2,1)}, bf16[128,2048]{1,0:T(8,128)(2,1)S(1)}, u32[]{:S(2)}, u32[]{:S(2)}) collective-permute-start(bf16[128,2048]{1,0:T(8,128)(2,1)} %get-tuple-element.205), channel_id=1, source_target_pairs={{0,2},{1,3},{2,0},{3,1},{4,6},{5,7},{6,4},{7,5},{8,10},{9,11},{10,... | collective-permute-start | bytes 1572872 | tf_op jit(solution)/shard_map/ppermute | solution.py:119
  389.7 32.2 %collective-permute-start.37 = (bf16[128,2048]{1,0:T(8,128)(2,1)}, bf16[128,2048]{1,0:T(8,128)(2,1)S(1)}, u32[]{:S(2)}, u32[]{:S(2)}) collective-permute-start(bf16[128,2048]{1,0:T(8,128)(2,1)} %get-tuple-element.208), channel_id=1, source_target_pairs={{0,4},{1,5},{2,6},{3,7},{4,0},{5,1},{6,2},{7,3},{8,12},{9,13},{10,... | collective-permute-start | bytes 1572872 | tf_op jit(solution)/shard_map/ppermute | solution.py:119
  393.9 359.3 %reduce-scatter.9.cloned.1.call-start = ((), (), s32[]{:S(2)}) async-start(), calls=%async_computation.9 | async-start | bytes 5242880 | tf_op jit(solution)/shard_map/reduce_scatter | solution.py:195
  421.0 189.5 %collective-permute-start.52 = (bf16[128,2048]{1,0:T(8,128)(2,1)}, bf16[128,2048]{1,0:T(8,128)(2,1)}, u32[]{:S(2)}, u32[]{:S(2)}) collective-permute-start(bf16[128,2048]{1,0:T(8,128)(2,1)} %get-tuple-element.193), channel_id=1, source_target_pairs={{0,2},{1,3},{2,0},{3,1},{4,6},{5,7},{6,4},{7,5},{8,10},{9,11},{10,... | collective-permute-start | bytes 1572872 | tf_op jit(solution)/shard_map/ppermute | solution.py:119
  437.2 335.7 %reduce-scatter.7.cloned.1.call-start = ((), (), s32[]{:S(2)}) async-start(), calls=%async_computation.8 | async-start | bytes 5242880 | tf_op jit(solution)/shard_map/reduce_scatter | solution.py:195
  437.4 23.7 %collective-permute-start.44 = (bf16[128,2048]{1,0:T(8,128)(2,1)}, bf16[128,2048]{1,0:T(8,128)(2,1)S(1)}, u32[]{:S(2)}, u32[]{:S(2)}) collective-permute-start(bf16[128,2048]{1,0:T(8,128)(2,1)} %get-tuple-element.232), channel_id=1, source_target_pairs={{0,2},{1,3},{2,0},{3,1},{4,6},{5,7},{6,4},{7,5},{8,10},{9,11},{10,... | collective-permute-start | bytes 1572872 | tf_op jit(solution)/shard_map/ppermute | solution.py:119
  439.5 20.8 %collective-permute-start.45 = (bf16[128,2048]{1,0:T(8,128)(2,1)}, bf16[128,2048]{1,0:T(8,128)(2,1)S(1)}, u32[]{:S(2)}, u32[]{:S(2)}) collective-permute-start(bf16[128,2048]{1,0:T(8,128)(2,1)} %get-tuple-element.230), channel_id=1, source_target_pairs={{0,2},{1,3},{2,0},{3,1},{4,6},{5,7},{6,4},{7,5},{8,10},{9,11},{10,... | collective-permute-start | bytes 1572872 | tf_op jit(solution)/shard_map/ppermute | solution.py:119
  444.8 165.7 %collective-permute-start.54 = (bf16[128,2048]{1,0:T(8,128)(2,1)}, bf16[128,2048]{1,0:T(8,128)(2,1)}, u32[]{:S(2)}, u32[]{:S(2)}) collective-permute-start(bf16[128,2048]{1,0:T(8,128)(2,1)} %get-tuple-element.194), channel_id=1, source_target_pairs={{0,4},{1,5},{2,6},{3,7},{4,0},{5,1},{6,2},{7,3},{8,12},{9,13},{10,... | collective-permute-start | bytes 1572872 | tf_op jit(solution)/shard_map/ppermute | solution.py:119
  487.0 39.1 %collective-permute-start.48 = (bf16[1024,1024]{1,0:T(8,128)(2,1)}, bf16[1024,1024]{1,0:T(8,128)(2,1)}, u32[]{:S(2)}, u32[]{:S(2)}) collective-permute-start(bf16[1024,1024]{1,0:T(8,128)(2,1)} %fusion.113), channel_id=1, source_target_pairs={{0,1},{1,0},{2,3},{3,2},{4,5},{5,4},{6,7},{7,6},{8,9},{9,8},{10,11... | collective-permute-start | bytes 6291464 | tf_op jit(solution)/shard_map/ppermute | solution.py:119
  506.1 25.4 %collective-permute-start.49 = (bf16[1024,1024]{1,0:T(8,128)(2,1)}, bf16[1024,1024]{1,0:T(8,128)(2,1)}, u32[]{:S(2)}, u32[]{:S(2)}) collective-permute-start(bf16[1024,1024]{1,0:T(8,128)(2,1)} %convolution_convert_fusion.4), channel_id=1, source_target_pairs={{0,1},{1,0},{2,3},{3,2},{4,5},{5,4},{6,7},{7,6},{8,9},{9,8},{10,11... | collective-permute-start | bytes 6291464 | tf_op jit(solution)/shard_map/ppermute | solution.py:119
  523.8 94.9 %collective-permute-start.50 = (bf16[128,2048]{1,0:T(8,128)(2,1)}, bf16[128,2048]{1,0:T(8,128)(2,1)}, u32[]{:S(2)}, u32[]{:S(2)}) collective-permute-start(bf16[128,2048]{1,0:T(8,128)(2,1)} %get-tuple-element.196), channel_id=1, source_target_pairs={{0,2},{1,3},{2,0},{3,1},{4,6},{5,7},{6,4},{7,5},{8,10},{9,11},{10,... | collective-permute-start | bytes 1572872 | tf_op jit(solution)/shard_map/ppermute | solution.py:119
  526.1 92.7 %collective-permute-start.51 = (bf16[128,2048]{1,0:T(8,128)(2,1)}, bf16[128,2048]{1,0:T(8,128)(2,1)}, u32[]{:S(2)}, u32[]{:S(2)}) collective-permute-start(bf16[128,2048]{1,0:T(8,128)(2,1)} %get-tuple-element.195), channel_id=1, source_target_pairs={{0,4},{1,5},{2,6},{3,7},{4,0},{5,1},{6,2},{7,3},{8,12},{9,13},{10,... | collective-permute-start | bytes 1572872 | tf_op jit(solution)/shard_map/ppermute | solution.py:119
  607.8 73.5 %collective-permute-start.63 = (bf16[1024,2048]{1,0:T(8,128)(2,1)}, bf16[1024,2048]{1,0:T(8,128)(2,1)}, u32[]{:S(2)}, u32[]{:S(2)}) collective-permute-start(bf16[1024,2048]{1,0:T(8,128)(2,1)} %convolution_convert_fusion), channel_id=1, source_target_pairs={{0,1},{1,0},{2,3},{3,2},{4,5},{5,4},{6,7},{7,6},{8,9},{9,8},{10,11... | collective-permute-start | bytes 12582920 | tf_op jit(solution)/shard_map/ppermute | solution.py:119
  638.3 64.0 %collective-permute-start.66 = (bf16[128,2048]{1,0:T(8,128)(2,1)}, bf16[128,2048]{1,0:T(8,128)(2,1)}, u32[]{:S(2)}, u32[]{:S(2)}) collective-permute-start(bf16[128,2048]{1,0:T(8,128)(2,1)} %get-tuple-element.183), channel_id=1, source_target_pairs={{0,2},{1,3},{2,0},{3,1},{4,6},{5,7},{6,4},{7,5},{8,10},{9,11},{10,... | collective-permute-start | bytes 1572872 | tf_op jit(solution)/shard_map/ppermute | solution.py:119
  639.0 162.5 %reduce-scatter.5.cloned.1.call-start = ((), (), s32[]{:S(2)}) async-start(), calls=%async_computation.7 | async-start | bytes 5242880 | tf_op jit(solution)/shard_map/reduce_scatter | solution.py:195
  642.0 60.4 %collective-permute-start.68 = (bf16[128,2048]{1,0:T(8,128)(2,1)}, bf16[128,2048]{1,0:T(8,128)(2,1)}, u32[]{:S(2)}, u32[]{:S(2)}) collective-permute-start(bf16[128,2048]{1,0:T(8,128)(2,1)} %get-tuple-element.182), channel_id=1, source_target_pairs={{0,4},{1,5},{2,6},{3,7},{4,0},{5,1},{6,2},{7,3},{8,12},{9,13},{10,... | collective-permute-start | bytes 1572872 | tf_op jit(solution)/shard_map/ppermute | solution.py:119
  657.9 56.7 %collective-permute-start.64 = (bf16[128,2048]{1,0:T(8,128)(2,1)}, bf16[128,2048]{1,0:T(8,128)(2,1)}, u32[]{:S(2)}, u32[]{:S(2)}) collective-permute-start(bf16[128,2048]{1,0:T(8,128)(2,1)} %get-tuple-element.181), channel_id=1, source_target_pairs={{0,2},{1,3},{2,0},{3,1},{4,6},{5,7},{6,4},{7,5},{8,10},{9,11},{10,... | collective-permute-start | bytes 1572872 | tf_op jit(solution)/shard_map/ppermute | solution.py:119
  662.9 51.7 %collective-permute-start.65 = (bf16[128,2048]{1,0:T(8,128)(2,1)}, bf16[128,2048]{1,0:T(8,128)(2,1)}, u32[]{:S(2)}, u32[]{:S(2)}) collective-permute-start(bf16[128,2048]{1,0:T(8,128)(2,1)} %get-tuple-element.184), channel_id=1, source_target_pairs={{0,4},{1,5},{2,6},{3,7},{4,0},{5,1},{6,2},{7,3},{8,12},{9,13},{10,... | collective-permute-start | bytes 1572872 | tf_op jit(solution)/shard_map/ppermute | solution.py:119
  681.3 31.9 %collective-permute-start.62 = (bf16[256,2048]{1,0:T(8,128)(2,1)S(1)}, bf16[256,2048]{1,0:T(8,128)(2,1)}, u32[]{:S(2)}, u32[]{:S(2)}) collective-permute-start(bf16[256,2048]{1,0:T(8,128)(2,1)S(1)} %collective-permute-done.61), channel_id=1, source_target_pairs={{0,1},{2,3},{5,4},{7,6},{8,9},{10,11},{13,12},{15,14},{16,17},{18,... | collective-permute-start | bytes 3145736 | tf_op jit(solution)/shard_map/ppermute | solution.py:119
  736.7 22.5 %collective-permute-start.71 = (bf16[256,2048]{1,0:T(8,128)(2,1)S(1)}, bf16[256,2048]{1,0:T(8,128)(2,1)}, u32[]{:S(2)}, u32[]{:S(2)}) collective-permute-start(bf16[256,2048]{1,0:T(8,128)(2,1)S(1)} %fusion.37), channel_id=1, source_target_pairs={{1,5},{3,7},{4,0},{6,2},{9,13},{11,15},{12,8},{14,10},{17,21},{19,... | collective-permute-start | bytes 3145736 | tf_op jit(solution)/shard_map/ppermute | solution.py:119
  739.8 21.4 %collective-permute-start.73 = (bf16[256,2048]{1,0:T(8,128)(2,1)S(1)}, bf16[256,2048]{1,0:T(8,128)(2,1)}, u32[]{:S(2)}, u32[]{:S(2)}) collective-permute-start(bf16[256,2048]{1,0:T(8,128)(2,1)S(1)} %fusion.37), channel_id=1, source_target_pairs={{0,2},{2,0},{5,7},{7,5},{8,10},{10,8},{13,15},{15,13},{16,18},{18,... | collective-permute-start | bytes 3145736 | tf_op jit(solution)/shard_map/ppermute | solution.py:119
  741.4 21.1 %collective-permute-start.70 = (bf16[256,2048]{1,0:T(8,128)(2,1)S(1)}, bf16[256,2048]{1,0:T(8,128)(2,1)}, u32[]{:S(2)}, u32[]{:S(2)}) collective-permute-start(bf16[256,2048]{1,0:T(8,128)(2,1)S(1)} %fusion.37), channel_id=1, source_target_pairs={{0,1},{2,3},{5,4},{7,6},{8,9},{10,11},{13,12},{15,14},{16,17},{18,... | collective-permute-start | bytes 3145736 | tf_op jit(solution)/shard_map/ppermute | solution.py:119
  753.1 52.3 %collective-permute-start.79 = (bf16[256,2048]{1,0:T(8,128)(2,1)}, bf16[256,2048]{1,0:T(8,128)(2,1)S(1)}, u32[]{:S(2)}, u32[]{:S(2)}) collective-permute-start(bf16[256,2048]{1,0:T(8,128)(2,1)} %reduce-scatter.9.cloned.1.call-done), channel_id=1, source_target_pairs={{1,4},{3,6},{4,1},{6,3},{9,12},{11,14},{12,9},{14,11},{17,20},{19,... | collective-permute-start | bytes 3145736 | tf_op jit(solution)/shard_map/ppermute | solution.py:119
  772.9 33.5 %collective-permute-start.78 = (bf16[256,2048]{1,0:T(8,128)(2,1)}, bf16[256,2048]{1,0:T(8,128)(2,1)}, u32[]{:S(2)}, u32[]{:S(2)}) collective-permute-start(bf16[256,2048]{1,0:T(8,128)(2,1)} %reduce-scatter.7.cloned.1.call-done), channel_id=1, source_target_pairs={{1,4},{3,6},{4,1},{6,3},{9,12},{11,14},{12,9},{14,11},{17,20},{19,... | collective-permute-start | bytes 3145736 | tf_op jit(solution)/shard_map/ppermute | solution.py:119
  (186 other events, 2711.7 us)
Sparse Core Ops, SparseCore 0:
  47.3 104.4 all-gather.3
  153.9 90.1 all-gather.5
  246.3 44.3 all-gather.7
  394.0 47.5 reduce-scatter.10
  443.8 78.0 reduce-scatter.8
  639.1 82.4 reduce-scatter.6
  723.9 77.5 reduce-scatter.4

commit v2 on v1

--- a/solution.py
+++ b/solution.py
@@ -4,6 +4,8 @@
 import jax
 import jax.numpy as jnp
 from jax import lax
+from jax.experimental import pallas as pl
+from jax.experimental.pallas import tpu as pltpu
 from jax.sharding import PartitionSpec as P
 
 HEAD_KEY = 256
@@ -153,16 +155,6 @@
     return jnp.concatenate(rows_of(value, place.b, place.y), axis=0)
 
 
-def all_rows(place, pieces, others):
-    width = pieces[0].shape[0]
-    placed = []
-    for j, (piece, other) in enumerate(zip(pieces, others)):
-        at = 2 * ((place.a - j) % place.na)
-        placed.append(((at + place.c) * width, piece))
-        placed.append(((at + 1 - place.c) * width, other))
-    return assemble(place.ndp * width, placed)
-
-
 def queue_gather(place, own):
     return lax.all_gather(own, BOTH, axis=0, tiled=True, axis_index_groups=place.group_ac)
 
@@ -202,7 +194,8 @@
 
 
 def vector_grads(place, sums):
-    parts = [send(sums, place.across_x), send(sums, place.across_y), send(sums, place.across_both)]
+    ways = (place.across_x, place.across_y, place.across_both)
+    parts = [send(sums, way) for way in ways]
     sums = sums + parts[0] + (parts[1] + parts[2])
     sums = sums + send(sums, place.core)
     width = sums.shape[1] // place.ndp
@@ -306,70 +299,212 @@
     return assemble(8 * q, placed)
 
 
-def rotate(values, tables):
-    cosine, sine, scale = tables
-    half = values.shape[-1] // 2
-    first, second = values[:, :half], values[:, half:]
-    return jnp.concatenate(
-        [(first * cosine - second * sine) * scale, (second * cosine + first * sine) * scale],
-        axis=-1,
-    )
-
-
-def unrotate(grads, tables):
-    cosine, sine, scale = tables
-    half = grads.shape[-1] // 2
-    first, second = grads[:, :half] * scale, grads[:, half:] * scale
-    return jnp.concatenate(
-        [first * cosine + second * sine, second * cosine - first * sine], axis=-1
-    )
-
-
-def decay_mask(row_start, row_segment, col_segment, log_gamma):
-    row_pos = row_start + jnp.arange(row_segment.shape[0], dtype=jnp.int32)
-    col_pos = jnp.arange(col_segment.shape[0], dtype=jnp.int32)
-    gap = row_pos[:, None] - col_pos[None, :]
-    keep = (gap >= 0) & (row_segment[:, None] == col_segment[None, :])
+def decay_block(start, row_segment, col_segment, decay):
+    shape = (row_segment.shape[0], col_segment.shape[1])
+    gap = lax.broadcasted_iota(jnp.int32, shape, 0) - lax.broadcasted_iota(jnp.int32, shape, 1)
+    gap = gap + start
+    keep = (gap >= 0) & (row_segment == col_segment)
     distance = jnp.maximum(gap, 0).astype(jnp.float32)
-    return jnp.where(keep, jnp.exp(distance * log_gamma), 0.0)
-
-
-def retention_forward(query_rot, key_rot, values, segment, log_gamma):
-    length = query_rot.shape[0]
+    return jnp.where(keep, jnp.exp(distance * decay), 0.0)
+
+
+def forward_kernel(head, na, given, *refs):
+    log_gamma, row_segment, col_segment, cosine, sine, growth, tokens = refs[:7]
+    pieces = refs[7 : 7 + 2 * na]
+    full, parts, normed, scale, sems = refs[7 + 2 * na + given :]
+    width = full.shape[0] // (2 * na)
+    a, c = lax.axis_index("dp") // 2, lax.axis_index("tensor") % 2
+    copies = []
+    for j in range(na):
+        for side in range(2):
+            at = 2 * lax.rem(a - j + na, na) + (c if side == 0 else 1 - c)
+            at = pl.ds(pl.multiple_of(at * width, width), width)
+            piece = pieces[j + side * na].at[pl.ds(0, width), :]
+            copies.append(pltpu.make_async_copy(piece, full.at[at, :], sems.at[2 * j + side]))
+            copies[-1].start()
+    for copy in copies:
+        copy.wait()
+    length = tokens.shape[0]
     rows = min(512, length)
-    outputs, kept = [], []
-    for start in range(0, length, rows):
-        stop = start + rows
-        mask = decay_mask(start, segment[start:stop], segment[:stop], log_gamma)
-        raw = dot_nt(query_rot[start:stop], key_rot[:stop])
-        weighted = (raw * mask).astype(jnp.bfloat16)
-        kept.append(weighted)
-        outputs.append(dot_nn(weighted, values[:stop]))
-    return jnp.concatenate(outputs, axis=0), kept
-
-
-def retention_backward(query_rot, key_rot, values, segment, log_gamma, grad_mixed, kept):
-    length = query_rot.shape[0]
+    half = HEAD_KEY // 2
+
+    def project(r, carry):
+        at = pl.ds(pl.multiple_of(r * rows, rows), rows)
+        left = tokens[at, :]
+        for start in range(0, HEAD_VALUE, 256):
+            stop = start + 256
+            parts[at, start:stop] = dot_nn(left, full[:, start:stop]).astype(jnp.bfloat16)
+        cos, sin, grow = cosine[at, :], sine[at, :], growth[at, :]
+        for start, factor in (
+            (HEAD_VALUE, grow),
+            (HEAD_VALUE + HEAD_KEY, (1.0 / grow)),
+        ):
+            last = 1.0 if start == HEAD_VALUE else HEAD_KEY ** (-0.5)
+            part = dot_nn(left, full[:, start : start + HEAD_KEY])
+            first, second = part[:, :half], part[:, half:]
+            parts[at, start : start + half] = (
+                (first * cos - second * sin) * factor * last
+            ).astype(jnp.bfloat16)
+            parts[at, start + half : start + HEAD_KEY] = (
+                (second * cos + first * sin) * factor * last
+            ).astype(jnp.bfloat16)
+        return carry
+
+    lax.fori_loop(0, length // rows, project, 0)
+    decay = log_gamma[head]
+    query = slice(HEAD_VALUE, HEAD_VALUE + HEAD_KEY)
+    key = slice(HEAD_VALUE + HEAD_KEY, HEAD_VALUE + 2 * HEAD_KEY)
+    for i in range(length // rows):
+        to = slice(i * rows, (i + 1) * rows)
+        mixed = None
+        for j in range(i + 1):
+            of = slice(j * rows, (j + 1) * rows)
+            mask = decay_block((i - j) * rows, row_segment[to, :], col_segment[:, of], decay)
+            weighted = (dot_nt(parts[to, query], parts[of, key]) * mask).astype(jnp.bfloat16)
+            part = dot_nn(weighted, parts[of, :HEAD_VALUE])
+            mixed = part if mixed is None else mixed + part
+        unit, inverse = norm_parts(mixed, GROUP_EPSILON)
+        normed[to, :] = unit
+        scale[to, :] = inverse
+
+
+def retention_forward(place, head, shared, pieces, held):
+    log_gamma, row_segment, col_segment, *tables, tokens = shared
+    length, depth = tokens.shape
+    heads = log_gamma.shape[0]
+    width = HEAD_VALUE + 2 * HEAD_KEY
+    anywhere = pl.BlockSpec(memory_space=pl.ANY)
+    whole = lambda item: pl.BlockSpec(item.shape, lambda i: (0, 0))
+    return pl.pallas_call(
+        functools.partial(forward_kernel, head, place.na, len(held)),
+        grid=(1,),
+        in_specs=[
+            pl.BlockSpec(memory_space=pltpu.SMEM),
+            *[whole(item) for item in shared[1:]],
+            *[anywhere] * (len(pieces) + len(held)),
+        ],
+        out_specs=[
+            pl.BlockSpec((depth, width), lambda i: (0, 0)),
+            pl.BlockSpec((length, width), lambda i: (0, head)),
+            pl.BlockSpec((length, HEAD_VALUE), lambda i: (0, head)),
+            pl.BlockSpec((None, length, 1), lambda i: (head, 0, 0)),
+        ],
+        out_shape=[
+            jax.ShapeDtypeStruct((depth, width), jnp.bfloat16),
+            jax.ShapeDtypeStruct((length, heads * width), jnp.bfloat16),
+            jax.ShapeDtypeStruct((length, heads * HEAD_VALUE), jnp.float32),
+            jax.ShapeDtypeStruct((heads, length, 1), jnp.float32),
+        ],
+        scratch_shapes=[pltpu.SemaphoreType.DMA((len(pieces),))],
+        input_output_aliases={7 + len(pieces) + i: 1 + i for i in range(len(held))},
+        compiler_params=pltpu.CompilerParams(vmem_limit_bytes=56 << 20),
+        cost_estimate=pl.CostEstimate(
+            flops=2 * length * (depth * width + length * (HEAD_KEY + HEAD_VALUE)),
+            bytes_accessed=4 * length * width + 8 * depth * width,
+            transcendentals=length * length,
+        ),
+    )(log_gamma, row_segment, col_segment, *tables, tokens, *pieces, *held)
+
+
+def retention_kernel(
+    log_gamma,
+    row_segment,
+    col_segment,
+    cosine,
+    sine,
+    growth,
+    value,
+    query,
+    key,
+    grad,
+    normed,
+    scale,
+    out,
+    mixed,
+    grad_query,
+    grad_key,
+    grad_value,
+):
+    length = query.shape[0]
     rows = min(512, length)
-    grad_query, grad_key, grad_value = [], [], []
-    for block, start in enumerate(range(0, length, rows)):
-        stop = start + rows
-        grad_block = grad_mixed[start:stop]
-        mask = decay_mask(start, segment[start:stop], segment[:stop], log_gamma)
-        grad_weighted = dot_nt(grad_block, values[:stop])
-        grad_raw = (grad_weighted * mask).astype(jnp.bfloat16)
-        grad_query.append(dot_nn(grad_raw, key_rot[:stop]))
-        grad_key.append(dot_tn(grad_raw, query_rot[start:stop]))
-        grad_value.append(dot_tn(kept[block], grad_block))
-
-    def total(parts):
-        out = []
-        for start in range(0, length, rows):
-            pieces = [p[start : start + rows] for p in parts if p.shape[0] > start]
-            out.append(functools.reduce(jnp.add, pieces))
-        return jnp.concatenate(out, axis=0)
-
-    return jnp.concatenate(grad_query, axis=0), total(grad_key), total(grad_value)
+    decay = log_gamma[pl.program_id(0)]
+    grads, unit = grad[...], normed[...]
+    mixed[...] = (
+        scale[...]
+        * (
+            grads
+            - jnp.mean(grads, axis=-1, keepdims=True)
+            - unit * jnp.mean(grads * unit, axis=-1, keepdims=True)
+        )
+    ).astype(jnp.bfloat16)
+    for i in range(length // rows):
+        to = slice(i * rows, (i + 1) * rows)
+        for j in range(i + 1):
+            of = slice(j * rows, (j + 1) * rows)
+            mask = decay_block((i - j) * rows, row_segment[to, :], col_segment[:, of], decay)
+            weighted = (dot_nt(query[to, :], key[of, :]) * mask).astype(jnp.bfloat16)
+            raw = (dot_nt(mixed[to, :], value[of, :]) * mask).astype(jnp.bfloat16)
+            parts = (
+                (grad_query, to, dot_nn(raw, key[of, :]), j == 0),
+                (grad_key, of, dot_tn(raw, query[to, :]), i == j),
+                (grad_value, of, dot_tn(weighted, mixed[to, :]), i == j),
+            )
+            for total, at, part, first in parts:
+                if first:
+                    total[at, :] = part
+                else:
+                    total[at, :] += part
+    cos, sin, grow = cosine[...], sine[...], growth[...]
+    out[:, :HEAD_VALUE] = grad_value[...].astype(jnp.bfloat16)
+    half = HEAD_KEY // 2
+    for start, total, factor, last in (
+        (HEAD_VALUE, grad_query, grow, 1.0),
+        (HEAD_VALUE + HEAD_KEY, grad_key, 1.0 / grow, HEAD_KEY ** (-0.5)),
+    ):
+        first, second = total[:, :half] * factor, total[:, half:] * factor
+        out[:, start : start + half] = ((first * cos + second * sin) * last).astype(jnp.bfloat16)
+        out[:, start + half : start + HEAD_KEY] = ((second * cos - first * sin) * last).astype(
+            jnp.bfloat16
+        )
+
+
+def retention_backward(
+    log_gamma, row_segment, col_segment, cosine, sine, growth, vqk, grad, normed, scale
+):
+    length = vqk.shape[0]
+    heads = log_gamma.shape[0]
+    whole = lambda item: pl.BlockSpec(item.shape, lambda h: (0, 0))
+    width = HEAD_VALUE + 2 * HEAD_KEY
+    each, skip = width // HEAD_KEY, HEAD_VALUE // HEAD_KEY
+    shared = (row_segment, col_segment, cosine, sine, growth)
+    return pl.pallas_call(
+        retention_kernel,
+        grid=(heads,),
+        in_specs=[
+            pl.BlockSpec(memory_space=pltpu.SMEM),
+            *[whole(item) for item in shared],
+            pl.BlockSpec((length, HEAD_VALUE), lambda h: (0, h * (width // HEAD_VALUE))),
+            pl.BlockSpec((length, HEAD_KEY), lambda h: (0, h * each + skip)),
+            pl.BlockSpec((length, HEAD_KEY), lambda h: (0, h * each + skip + 1)),
+            pl.BlockSpec((length, HEAD_VALUE), lambda h: (0, h)),
+            pl.BlockSpec((length, HEAD_VALUE), lambda h: (0, h)),
+            pl.BlockSpec((None, length, 1), lambda h: (h, 0, 0)),
+        ],
+        out_specs=pl.BlockSpec((length, width), lambda h: (0, h)),
+        out_shape=jax.ShapeDtypeStruct((length, heads * width), jnp.bfloat16),
+        scratch_shapes=[
+            pltpu.VMEM((length, HEAD_VALUE), jnp.bfloat16),
+            pltpu.VMEM((length, HEAD_KEY), jnp.float32),
+            pltpu.VMEM((length, HEAD_KEY), jnp.float32),
+            pltpu.VMEM((length, HEAD_VALUE), jnp.float32),
+        ],
+        compiler_params=pltpu.CompilerParams(vmem_limit_bytes=48 << 20),
+        cost_estimate=pl.CostEstimate(
+            flops=heads * length * length * 2 * (2 * HEAD_VALUE + 3 * HEAD_KEY),
+            bytes_accessed=heads * length * (4 * width + 8 * HEAD_VALUE),
+            transcendentals=heads * length * length,
+        ),
+    )(log_gamma, *shared, vqk, vqk, vqk, grad, normed, scale)
 
 
 def local(ndp, nt, *args):
@@ -398,7 +533,6 @@
 ):
     place = Place(ndp, nt)
     heads = w_query.shape[1] // HEAD_KEY
-    split = heads * HEAD_KEY
     inner = heads * HEAD_VALUE
     units = w_ffgate.shape[1]
 
@@ -407,8 +541,19 @@
     across = w_value.shape[1]
     extra = -(-norms.shape[0] // across)
     norms = jnp.pad(norms, (0, 16 * across - norms.shape[0])).reshape(16, across)
-    own_value = my_sequence(place, jnp.concatenate([w_value, norms], axis=0))
-    own_qk = my_sequence(place, jnp.concatenate([w_query, w_key], axis=1))
+    shards = [
+        jnp.concatenate(
+            [
+                w_value[:, h * HEAD_VALUE : (h + 1) * HEAD_VALUE],
+                w_query[:, h * HEAD_KEY : (h + 1) * HEAD_KEY],
+                w_key[:, h * HEAD_KEY : (h + 1) * HEAD_KEY],
+            ],
+            axis=1,
+        )
+        for h in range(heads)
+    ]
+    own_value = my_sequence(place, jnp.concatenate([shards[0], norms], axis=0))
+    own_qk = my_sequence(place, shards[1])
     shard_og = jnp.concatenate([w_out.T, w_gate], axis=1)
     shard_ff = jnp.concatenate([w_ffgate, w_ffup], axis=1)
     shard_down = w_down.T
@@ -432,20 +577,11 @@
     norms = norms.reshape(place.ndp, 4, width).transpose(1, 0, 2).reshape(4, place.ndp * width)
     norms = norms.astype(jnp.float32)
     gain_one, shift_one, gain_two, shift_two = norms[0], norms[1], norms[2], norms[3]
-    value_pieces = [piece[:width] for piece in value_pieces]
-    value_others = [piece[:width] for piece in value_others]
     got_og, value_pieces[-2] = together(got_og, value_pieces[-2])
     got_tokens, qk_pieces[-2] = together(got_tokens, qk_pieces[-2])
-    got_ff, got_down, value_pieces[-1] = together(got_ff, got_down, value_pieces[-1])
     own_og = pick(place.keeper, shard_og, got_og)
-    own_ff = pick(place.keeper, shard_ff, got_ff)
-    own_down = pick(place.keeper, shard_down, got_down)
     inputs = pick(place.keeper, tokens, got_tokens)
-    full_value = all_rows(place, value_pieces, value_others)
-    full_qk = all_rows(place, qk_pieces, qk_others)
     full_og = queue_gather(place, own_og)
-    full_ff = queue_gather(place, own_ff)
-    full_down = queue_gather(place, own_down)
     full_out, full_gate = full_og[:, :inner], full_og[:, inner:]
     segment = my_sequence(place, segment_ids)
     decay = jnp.where(place.keeper, decay_index, send(decay_index, place.core))
@@ -453,28 +589,14 @@
 
     normed_all, _ = norm_parts(inputs.astype(jnp.float32), EPSILON)
     first_in = (normed_all * gain_one + shift_one).astype(jnp.bfloat16)
-    qk = dot_nn(first_in, full_qk)
-    values = dot_nn(first_in, full_value).astype(jnp.bfloat16)
-    cosine, sine, growth = xpos_tables(LENGTH, HEAD_KEY)
-    query_tables = (cosine, sine, growth)
-    key_tables = (cosine, sine, 1.0 / growth)
-    query_rot, key_rot = [], []
-    for h in range(heads):
-        query = qk[:, h * HEAD_KEY : (h + 1) * HEAD_KEY]
-        keys = qk[:, split + h * HEAD_KEY : split + (h + 1) * HEAD_KEY]
-        query_rot.append(rotate(query, query_tables).astype(jnp.bfloat16))
-        key_rot.append((rotate(keys, key_tables) * HEAD_KEY ** (-0.5)).astype(jnp.bfloat16))
-    grouped, group_scale, kept = [], [], []
-    for h in range(heads):
-        at = slice(h * HEAD_VALUE, (h + 1) * HEAD_VALUE)
-        mixed, weighted = retention_forward(
-            query_rot[h], key_rot[h], values[:, at], segment, log_gamma[h]
-        )
-        normed, scale = norm_parts(mixed, GROUP_EPSILON)
-        grouped.append(normed)
-        group_scale.append(scale)
-        kept.append(weighted)
-    grouped_flat = jnp.concatenate(grouped, axis=1)
+    tables = xpos_tables(LENGTH, HEAD_KEY)
+    shared = (log_gamma, segment[:, None], segment[None, :], *tables, first_in)
+    full_value, *held = retention_forward(place, 0, shared, value_pieces + value_others, ())
+    full_qk, *held = retention_forward(place, 1, shared, qk_pieces + qk_others, held)
+    vqk_rot, grouped_flat, group_scale = held
+    got_ff, got_down, full_value = together(got_ff, got_down, full_value)
+    full_ff = queue_gather(place, pick(place.keeper, shard_ff, got_ff))
+    full_down = queue_gather(place, pick(place.keeper, shard_down, got_down))
     gate = dot_nn(first_in, full_gate)
     sigmoid_gate = jax.nn.sigmoid(gate)
     swish = gate * sigmoid_gate
@@ -511,13 +633,12 @@
         axis=1,
     )
     second_near, second_far = core_halves(place, second_in)
-    ff_got, ff_far = core_far(place, second_far, grad_ff)
-    away = dot_nt(far_rows(place, after(grad_ff, ff_far)), full_ff).astype(jnp.bfloat16)
+    away = dot_nt(far_rows(place, grad_ff), full_ff).astype(jnp.bfloat16)
     got = send_far(place, away)
-    ff_sum = core_near(second_near, after(grad_ff, away), ff_got)
-    ready, ff_sum = together(grad_ff, ff_sum)
+    here = dot_nt(near_rows(place, after(grad_ff, away)), full_ff)
+    ff_got, _ = core_far(place, second_far, after(grad_ff, here))
+    ff_sum = core_near(second_near, grad_ff, ff_got)
     share_ff = queue_scatter(place, ff_sum)
-    here = dot_nt(near_rows(place, ready), full_ff)
     grad_second = sum_near(place, here, got)
     grad_middle = my_rows(place, grad_feed).astype(jnp.float32) + norm_back(
         grad_second, normed_two, scale_two, gain_two
@@ -526,33 +647,21 @@
     e_got = send_far(place, e_away)
     branch_near, branch_far = core_halves(place, grad_branch)
     first_near, first_far = core_halves(place, first_in)
-    out_got, out_far = core_far(place, branch_far, gated)
-    grad_gated = dot_nn(after(grad_branch, out_far), full_out)
+    grad_gated = dot_nn(grad_branch, full_out)
     swish_slope = sigmoid_gate * (1.0 + gate * (1.0 - sigmoid_gate))
     grad_gate_in = (grad_gated * grouped_flat * swish_slope).astype(jnp.bfloat16)
     grad_grouped = grad_gated * swish
     gate_got, gate_far = core_far(place, first_far, grad_gate_in)
-    out_sum = core_near(branch_near, after(gated, gate_far), out_got)
-    gate_sum = core_near(first_near, after(grad_gate_in, out_sum), gate_got)
+    out_got, out_far = core_far(place, branch_far, after(gated, gate_far))
+    gate_sum = core_near(first_near, after(grad_gate_in, out_far), gate_got)
+    out_sum = core_near(branch_near, after(gated, gate_sum), out_got)
     og_sum = jnp.concatenate([out_sum, gate_sum], axis=1)
     grad_grouped, og_sum, e_near = together(grad_grouped, og_sum, near_rows(place, hidden))
     share_og = queue_scatter(place, og_sum)
     here = dot_nt(e_near, full_down)
     feed = sum_near(place, here, e_got)
     block_out = bring_home(place, (middle + feed).astype(jnp.bfloat16))
-    grad_qs, grad_ks, grad_vs = [], [], []
-    for h in range(heads):
-        at = slice(h * HEAD_VALUE, (h + 1) * HEAD_VALUE)
-        grad_mixed = norm_back(grad_grouped[:, at], grouped[h], group_scale[h], 1.0).astype(
-            jnp.bfloat16
-        )
-        grad_qrot, grad_krot, grad_value = retention_backward(
-            query_rot[h], key_rot[h], values[:, at], segment, log_gamma[h], grad_mixed, kept[h]
-        )
-        grad_qs.append(unrotate(grad_qrot, query_tables).astype(jnp.bfloat16))
-        grad_ks.append((unrotate(grad_krot, key_tables) * HEAD_KEY ** (-0.5)).astype(jnp.bfloat16))
-        grad_vs.append(grad_value.astype(jnp.bfloat16))
-    grad_vqk = jnp.concatenate(grad_vs + grad_qs + grad_ks, axis=1)
+    grad_vqk = retention_backward(*shared[:-1], vqk_rot, grad_grouped, grouped_flat, group_scale)
 
     def first_product(gate_rows, vqk_rows):
         return (
@@ -588,12 +697,18 @@
     share_ff = to_owner(place, share_ff)
     share_og = to_owner(place, share_og)
     share_vqk = to_owner(place, share_vqk)
+    picks = []
+    for start, size in ((HEAD_VALUE, HEAD_KEY), (HEAD_VALUE + HEAD_KEY, HEAD_KEY), (0, HEAD_VALUE)):
+        each = HEAD_VALUE + 2 * HEAD_KEY
+        picks.append(
+            jnp.concatenate(
+                [share_vqk[:, h * each + start : h * each + start + size] for h in range(heads)], axis=1
+            )
+        )
     return (
         block_out,
         grad_tokens,
-        share_vqk[:, inner : inner + split],
-        share_vqk[:, inner + split :],
-        share_vqk[:, :inner],
+        *picks,
         share_og[:, inner:],
         share_og[:, :inner].T,
         share_ff[:, :units],

time: 839 us -> 768 us (0.915)
  matrix products: 202 us -> 152 us
  local copies, waits for them, and re-layouts: 128 us -> 84.7 us
  Pallas kernels: 0 us -> 38.9 us
  other arithmetic: 85.6 us -> 72.4 us
    pallas_call x0 -> x3, Pallas kernels: none -> 38.9 us  [the longest x2 26.7 us: retention_forward(): pl.pallas_call(functools.partial(forward_kernel, head, place.na, len(held...]
    dynamic_update_slice x45 -> x30, local copies, waits for them, and re-layouts: 41.8 us -> 21.6 us  [assemble(): whole = lax.dynamic_update_slice_in_dim(whole, rows, start, axis=0)]
    dot_general x14 -> x4, matrix products: 67.2 us -> 48.9 us  [dot_nn(): lax.dot_general(left, right, (((1,), (0,)), ((), ())), preferred_element_...]
    dot_general x20 -> x12, matrix products: 70.3 us -> 52.4 us  [dot_nt(): lax.dot_general(left, right, (((1,), (1,)), ((), ())), preferred_element_...]
    dot_general x18 -> x10, matrix products: 64.3 us -> 50.4 us  [dot_tn(): lax.dot_general(left, right, (((0,), (0,)), ((), ())), preferred_element_...]
    another operation x4 -> x0, other arithmetic: 12.9 us -> none
    another operation x10 -> x4, local copies, waits for them, and re-layouts: 19.6 us -> 8.16 us
    unnamed x293 -> x186, local copies, waits for them, and re-layouts: 25.2 us -> 20.4 us
  transfers between devices with their start and end apart: 96 -> 96, of which waited for: 38 -> 35; matrix products, arithmetic and copies ran while one was open for 45% -> 34% of each run, Pallas kernels for 0% -> 5%
where the time goes in v2:
time: 768 us; the launch traced here: 762 us
  waiting for transfers between devices  249 us (32%)
  matrix products  152 us (20%)
  starting transfers between devices  149 us (19%)
  local copies, waits for them, and re-layouts  84.7 us (11%)
  other arithmetic  72.4 us (9%)
  Pallas kernels  38.9 us (5%)
  between operations  16.7 us (2%)
    ppermute x89, waiting for transfers between devices, send(): return lax.ppermute(value, BOTH, pairs)  241 us
    ppermute x89, starting transfers between devices, send(): return lax.ppermute(value, BOTH, pairs)  148 us
    dot_general x12, matrix products, dot_nt(): lax.dot_general(left, right, (((1,), (1,)), ((), ())), preferred_element_...  52.4 us
    dot_general x10, matrix products, dot_tn(): lax.dot_general(left, right, (((0,), (0,)), ((), ())), preferred_element_...  50.4 us
    dot_general x4, matrix products, dot_nn(): lax.dot_general(left, right, (((1,), (0,)), ((), ())), preferred_element_...  48.9 us
    pallas_call x2, Pallas kernels, retention_forward(): pl.pallas_call(functools.partial(forward_kernel, head, place.na, len(held...  26.7 us
    dynamic_update_slice x30, local copies, waits for them, and re-layouts, assemble(): whole = lax.dynamic_update_slice_in_dim(whole, rows, start, axis=0)  21.6 us
    unnamed x186, local copies, waits for them, and re-layouts  20.4 us
  transfers between devices with their start and end apart: 96, of which 35 were waited for; matrix products, arithmetic and copies ran while one was open for 34% of the time, Pallas kernels for 5%

profile of v2, /device:TPU:1, one launch (start us, length us, event | category | flops | bytes accessed | tf_op | source)
XLA Modules:
  0.0 762.5 jit_solution(14553347252843813411)
XLA Ops:
  10.3 4.5 collective-permute-start.5
  16.1 6.2 collective-permute-done.5
  28.8 8.8 %collective-permute-done.7.refs_8_ = bf16[272,1024]{1,0:T(8,128)(2,1)S(1)} collective-permute-done((bf16[272,1024]{1,0:T(8,128)(2,1)S(1)}, bf16[272,1024]{1,0:T(8,128)(2,1)S(1)}, u32[]{:S(2)}, u32[]{:S(2)}) %collective-permute-start.7) | collective-permute-done | bytes 557088 | tf_op jit(solution)/shard_map/ppermute | solution.py:121
  41.3 6.6 collective-permute-done.9.refs_9_
  49.3 7.8 %collective-permute-start = (bf16[1024,2048]{1,0:T(8,128)(2,1)}, bf16[1024,2048]{1,0:T(8,128)(2,1)}, u32[]{:S(2)}, u32[]{:S(2)}) collective-permute-start(bf16[1024,2048]{1,0:T(8,128)(2,1)} %param.16), channel_id=1, source_target_pairs={{1,4},{3,6},{4,1},{6,3},{9,12},{11,14},{12,9},{14,11},{17,20},{19,... | collective-permute-start | bytes 12582920 | tf_op jit(solution)/shard_map/ppermute | solution.py:121
  59.3 50.2 %collective-permute-done.1 = bf16[256,1024]{1,0:T(8,128)(2,1)S(1)} collective-permute-done((bf16[256,1024]{1,0:T(8,128)(2,1)S(1)}, bf16[256,1024]{1,0:T(8,128)(2,1)S(1)}, u32[]{:S(2)}, u32[]{:S(2)}) %collective-permute-start.1) | collective-permute-done | bytes 524320 | tf_op jit(solution)/shard_map/ppermute | solution.py:121
  119.9 12.1 %collective-permute-done.2.refs_8_ = bf16[256,1024]{1,0:T(8,128)(2,1)} collective-permute-done((bf16[256,1024]{1,0:T(8,128)(2,1)}, bf16[256,1024]{1,0:T(8,128)(2,1)}, u32[]{:S(2)}, u32[]{:S(2)}) %collective-permute-start.2) | collective-permute-done | bytes 524320 | tf_op jit(solution)/shard_map/ppermute | solution.py:121
  132.0 17.9 %collective-permute-done.11.refs_10_ = bf16[272,1024]{1,0:T(8,128)(2,1)} collective-permute-done((bf16[272,1024]{1,0:T(8,128)(2,1)}, bf16[272,1024]{1,0:T(8,128)(2,1)}, u32[]{:S(2)}, u32[]{:S(2)}) %collective-permute-start.11) | collective-permute-done | bytes 557088 | tf_op jit(solution)/shard_map/ppermute | solution.py:121
  153.9 4.1 collective-permute-start.33
  175.4 13.3 %shard_map.263 = (bf16[2048,1024]{1,0:T(8,128)(2,1)}, bf16[1024,2048]{1,0:T(8,128)(2,1)}, f32[1024,1024]{1,0:T(8,128)}, f32[2,1024,1]{2,1,0:T(8,128)}) custom-call(f32[2]{0:T(128)} %negate_log-plus-one_fusion.refs_0_.log_gamma, s32[1024,1]{1,0:T(8,128)} %copy.43.refs_1_.row_segment, s32[1,1024]{1,0:T(1,128)} %bitcast.58, ...), custom_call_target="tpu_custom_call" | custom-call | flops 5905580032 | bytes 20971520 | tf_op jit(solution)/shard_map/pallas_call | solution.py:378
  189.8 5.0 collective-permute-start.4
  195.7 21.6 %collective-permute-done.16.refs_10_ = bf16[256,1024]{1,0:T(8,128)(2,1)S(1)} collective-permute-done((bf16[256,1024]{1,0:T(8,128)(2,1)}, bf16[256,1024]{1,0:T(8,128)(2,1)S(1)}, u32[]{:S(2)}, u32[]{:S(2)}) %collective-permute-start.16) | collective-permute-done | bytes 524320 | tf_op jit(solution)/shard_map/ppermute | solution.py:121
  220.0 4.3 constant_dynamic-slice_fusion.55
  225.1 13.5 %shard_map.264 = (bf16[2048,1024]{1,0:T(8,128)(2,1)}, bf16[1024,2048]{1,0:T(8,128)(2,1)}, f32[1024,1024]{1,0:T(8,128)}, f32[2,1024,1]{2,1,0:T(8,128)}) custom-call(f32[2]{0:T(128)} %negate_log-plus-one_fusion.refs_0_.log_gamma, s32[1024,1]{1,0:T(8,128)} %copy.43.refs_1_.row_segment, ...), custom_call_target="tpu_custom_call", output_to_operand_aliasing={{1}: (15, {}), {2}: (16, {}), {3}: (17, {})} | custom-call | flops 5905580032 | bytes 20971520 | tf_op jit(solution)/shard_map/pallas_call | solution.py:378
  238.6 11.7 %multiply_convert_fusion.3 = (bf16[1024,1024]{1,0:T(8,128)(2,1)S(1)}, f32[1024,1024]{1,0:T(8,128)}) fusion(f32[1024,1024]{1,0:T(8,128)} %get-tuple-element.53.normed, bf16[1024,2048]{1,0:T(8,128)(2,1)} %fusion.5.refs_6_, bf16[2048,2048]{1,0:T(8,128)(2,1)} %all-gather.4.cloned.1.call-done), kind=kOutput, calls=%fused_computation.36 | convolution fusion | flops 4301258752 | bytes 18874368 | tf_op jit(solution)/shard_map/dot_general | solution.py:52
  258.4 7.7 %collective-permute-done.23 = bf16[128,2048]{1,0:T(8,128)(2,1)S(1)} collective-permute-done((bf16[128,2048]{1,0:T(8,128)(2,1)S(1)}, bf16[128,2048]{1,0:T(8,128)(2,1)S(1)}, u32[]{:S(2)}, u32[]{:S(2)}) %collective-permute-start.23) | collective-permute-done | bytes 524320 | tf_op jit(solution)/shard_map/ppermute | solution.py:121
  278.3 11.2 %collective-permute-done.24 = bf16[128,2048]{1,0:T(8,128)(2,1)S(1)} collective-permute-done((bf16[128,2048]{1,0:T(8,128)(2,1)S(1)}, bf16[128,2048]{1,0:T(8,128)(2,1)S(1)}, u32[]{:S(2)}, u32[]{:S(2)}) %collective-permute-start.24) | collective-permute-done | bytes 524320 | tf_op jit(solution)/shard_map/ppermute | solution.py:121
  296.1 8.5 %collective-permute-done.27 = bf16[128,2048]{1,0:T(8,128)(2,1)S(1)} collective-permute-done((bf16[128,2048]{1,0:T(8,128)(2,1)S(1)}, bf16[128,2048]{1,0:T(8,128)(2,1)S(1)}, u32[]{:S(2)}, u32[]{:S(2)}) %collective-permute-start.27) | collective-permute-done | bytes 524320 | tf_op jit(solution)/shard_map/ppermute | solution.py:121
  304.9 11.7 %collective-permute-done.30 = bf16[128,2048]{1,0:T(8,128)(2,1)S(1)} collective-permute-done((bf16[128,2048]{1,0:T(8,128)(2,1)S(1)}, bf16[128,2048]{1,0:T(8,128)(2,1)S(1)}, u32[]{:S(2)}, u32[]{:S(2)}) %collective-permute-start.30) | collective-permute-done | bytes 524320 | tf_op jit(solution)/shard_map/ppermute | solution.py:121
  317.2 10.5 %collective-permute-done.31 = bf16[128,2048]{1,0:T(8,128)(2,1)S(1)} collective-permute-done((bf16[128,2048]{1,0:T(8,128)(2,1)S(1)}, bf16[128,2048]{1,0:T(8,128)(2,1)S(1)}, u32[]{:S(2)}, u32[]{:S(2)}) %collective-permute-start.31) | collective-permute-done | bytes 524320 | tf_op jit(solution)/shard_map/ppermute | solution.py:121
  332.0 12.5 %fusion.220 = f32[1024,2048]{1,0:T(8,128)S(1)} fusion(bf16[1024,2048]{1,0:T(8,128)(2,1)} %copy-done.10, bf16[2048,2048]{1,0:T(8,128)(2,1)} %all-gather.6.cloned.1.call-done), kind=kOutput, calls=%fused_computation.433 | convolution fusion | flops 8589934592 | bytes 20971520 | tf_op jit(solution)/shard_map/dot_general | solution.py:52
  350.2 10.9 %fusion.11 = (bf16[1024,1024]{1,0:T(8,128)(2,1)S(1)}, bf16[1024,1024]{1,0:T(8,128)(2,1)S(1)}) fusion(f32[1024,2048]{1,0:T(8,128)} %copy-done.18, bf16[1024,2048]{1,0:T(8,128)(2,1)} %copy-done.9, bf16[2048,1024]{1,0:T(8,128)(2,1)} %all-gather.8.cloned.1.call-done), kind=kOutput, calls=%fused_computation.25 | convolution fusion | flops 4309647360 | bytes 20971520 | tf_op jit(solution)/shard_map/dot_general | solution.py:52
  363.0 10.0 %convolution_convert_fusion.3 = bf16[512,2048]{1,0:T(8,128)(2,1)S(1)} fusion(bf16[2048,2048]{1,0:T(8,128)(2,1)} %all-gather.6.cloned.1.call-done, bf16[128,2048]{1,0:T(8,128)(2,1)S(1)} %get-tuple-element.181, bf16[128,2048]{1,0:T(8,128)(2,1)S(1)} %get-tuple-element.180, bf16[128,2048]{1,0:T(8,128)(2,1)S(1)} %get-tuple-element.179, ...), kind=kOutput, calls=%fused_computation.61 | convolution fusion | flops 4304404480 | bytes 12582912 | tf_op jit(solution)/shard_map/dot_general | solution.py:58
  376.5 7.1 fusion.53
  388.2 8.8 %collective-permute-start.80 = (bf16[1024,1024]{1,0:T(8,128)(2,1)S(1)}, bf16[1024,1024]{1,0:T(8,128)(2,1)S(1)}, u32[]{:S(2)}, u32[]{:S(2)}) collective-permute-start(bf16[1024,1024]{1,0:T(8,128)(2,1)S(1)} %fusion.107), channel_id=1, source_target_pairs={{0,1},{1,0},{2,3},{3,2},{4,5},{5,4},{6,7},{7,6},{8,9},{9,8},{10,11... | collective-permute-start | bytes 6291464 | tf_op jit(solution)/shard_map/ppermute | solution.py:121
  397.0 9.4 %collective-permute-done.38 = bf16[128,2048]{1,0:T(8,128)(2,1)S(1)} collective-permute-done((bf16[128,2048]{1,0:T(8,128)(2,1)S(1)}, bf16[128,2048]{1,0:T(8,128)(2,1)S(1)}, u32[]{:S(2)}, u32[]{:S(2)}) %collective-permute-start.38) | collective-permute-done | bytes 524320 | tf_op jit(solution)/shard_map/ppermute | solution.py:121
  414.9 6.6 convolution_convert_fusion
  426.2 9.3 %collective-permute-done.42 = bf16[128,2048]{1,0:T(8,128)(2,1)S(1)} collective-permute-done((bf16[128,2048]{1,0:T(8,128)(2,1)S(1)}, bf16[128,2048]{1,0:T(8,128)(2,1)S(1)}, u32[]{:S(2)}, u32[]{:S(2)}) %collective-permute-start.42) | collective-permute-done | bytes 524320 | tf_op jit(solution)/shard_map/ppermute | solution.py:121
  442.3 4.7 collective-permute-done.45
  450.8 13.8 %multiply_convert_fusion = (bf16[1024,1024]{1,0:T(8,128)(2,1)S(1)}, f32[1024,1024]{1,0:T(8,128)}) fusion(f32[1024,1024]{1,0:T(8,128)} %get-tuple-element.263, f32[1024,1024]{1,0:T(8,128)} %get-tuple-element.53.normed, bf16[1024,2048]{1,0:T(8,128)(2,1)} %constant_dynamic-update-slice_fusion, bf16[2048,2048]{1,0:T(8,128)(2,1)} %all-gather.4.cloned.1.call-done), kind=kOutput, calls=%fused_computation.32 | convolution fusion | flops 4307550208 | bytes 23068672 | tf_op jit(solution)/shard_map/dot_general | solution.py:52
  467.1 4.1 collective-permute-start.47
  494.0 5.0 fusion.19
  499.1 6.9 fusion.21
  506.0 12.1 %shard_map.265 = bf16[1024,2048]{1,0:T(8,128)(2,1)} custom-call(f32[2]{0:T(128)S(1)} %copy-done.7, s32[1024,1]{1,0:T(8,128)S(1)} %copy-done.1, s32[1,1024]{1,0:T(1,128)S(1)} %bitcast.60, f32[1024,128]{1,0:T(8,128)S(1)} %copy-done.3, f32[1024,128]{1,0:T(8,128)S(1)} %copy-done.2, f32[1024,128]{1,0:T(8,128)S(1)} %copy-done, ...), custom_call_target="tpu_custom_call" | custom-call | flops 7516192768 | bytes 16777216 | tf_op jit(solution)/shard_map/pallas_call | solution.py:480
  518.2 9.0 %convolution_convert_fusion.1 = bf16[1024,2048]{1,0:T(8,128)(2,1)} fusion(bf16[1024,2048]{1,0:T(8,128)(2,1)} %shard_map.265, bf16[1024,256]{1,0:T(8,128)(2,1)S(1)} %copy-done.43, bf16[1024,256]{1,0:T(8,128)(2,1)S(1)} %copy-done.45, bf16[1024,256]{1,0:T(8,128)(2,1)S(1)} %copy-done.47, bf16[1024,256]{1,0:T(8,128)(2,1)S(1)} %copy-done.49), kind=kOutput, calls=%fused_computation.42 | convolution fusion | flops 4305453056 | bytes 10485760 | tf_op jit(solution)/shard_map/dot_general | solution.py:64
  534.7 4.4 fusion.123
  539.1 4.8 add_convert_fusion.3
  553.6 8.3 %add_convert_fusion = bf16[1024,2048]{1,0:T(8,128)(2,1)} fusion(bf16[1024,2048]{1,0:T(8,128)(2,1)} %collective-permute-done.78, bf16[1024,256]{1,0:T(8,128)(2,1)S(1)} %copy-done.51, bf16[1024,256]{1,0:T(8,128)(2,1)S(1)} %copy-done.52, bf16[1024,256]{1,0:T(8,128)(2,1)S(1)} %copy-done.53, bf16[1024,256]{1,0:T(8,128)(2,1)S(1)} %copy-done.50, ...), kind=kOutput, calls=%fused_computation.8 | convolution fusion | flops 4318035968 | bytes 14680064 | tf_op jit(solution)/shard_map/dot_general | solution.py:64
  563.1 10.5 %fusion.171 = f32[1024,2048]{1,0:T(8,128)} fusion(bf16[1024,2048]{1,0:T(8,128)(2,1)} %shard_map.265, bf16[1024,256]{1,0:T(8,128)(2,1)S(1)} %copy-done.39, bf16[1024,256]{1,0:T(8,128)(2,1)} %get-tuple-element.168, bf16[1024,256]{1,0:T(8,128)(2,1)} %get-tuple-element.169, bf16[1024,256]{1,0:T(8,128)(2,1)S(1)} %copy-done.37), kind=kOutput, calls=%fused_computation.267 | convolution fusion | flops 4303355904 | bytes 14680064 | tf_op jit(solution)/shard_map/dot_general | solution.py:64
  586.1 6.9 collective-permute-start.67
  602.9 20.0 %collective-permute-start.64 = (bf16[128,2048]{1,0:T(8,128)(2,1)}, bf16[128,2048]{1,0:T(8,128)(2,1)}, u32[]{:S(2)}, u32[]{:S(2)}) collective-permute-start(bf16[128,2048]{1,0:T(8,128)(2,1)} %get-tuple-element.199), channel_id=1, source_target_pairs={{0,4},{1,5},{2,6},{3,7},{4,0},{5,1},{6,2},{7,3},{8,12},{9,13},{10,... | collective-permute-start | bytes 1572872 | tf_op jit(solution)/shard_map/ppermute | solution.py:121
  624.3 8.2 %add_convert_fusion.1 = bf16[1024,2048]{1,0:T(8,128)(2,1)} fusion(f32[1024,2048]{1,0:T(8,128)} %fusion.171, bf16[1024,2048]{1,0:T(8,128)(2,1)} %collective-permute-done.62), kind=kLoop, calls=%fused_computation.9 | loop fusion | flops 6291456 | bytes 16777216 | tf_op jit(solution)/shard_map/convert_element_type | solution.py:183
  649.8 9.8 %collective-permute-done.66 = bf16[128,2048]{1,0:T(8,128)(2,1)} collective-permute-done((bf16[128,2048]{1,0:T(8,128)(2,1)}, bf16[128,2048]{1,0:T(8,128)(2,1)}, u32[]{:S(2)}, u32[]{:S(2)}) %collective-permute-start.66) | collective-permute-done | bytes 524320 | tf_op jit(solution)/shard_map/ppermute | solution.py:121
  678.9 6.4 collective-permute-start.87
  706.3 8.2 %collective-permute-done.75 = bf16[256,2048]{1,0:T(8,128)(2,1)} collective-permute-done((bf16[256,2048]{1,0:T(8,128)(2,1)S(1)}, bf16[256,2048]{1,0:T(8,128)(2,1)}, u32[]{:S(2)}, u32[]{:S(2)}) %collective-permute-start.75) | collective-permute-done | bytes 1048608 | tf_op jit(solution)/shard_map/ppermute | solution.py:121
  719.5 6.7 convert_element_type.250
  726.4 7.8 %reduce-scatter.5.cloned.1.call-done = bf16[256,2048]{1,0:T(8,128)(2,1)} async-done(((bf16[1024,2048]{1,0:T(8,128)(2,1)}), bf16[256,2048]{1,0:T(8,128)(2,1)}) %reduce-scatter.5.cloned.1.call-update) | async-done | bytes 1048592 | tf_op jit(solution)/shard_map/reduce_scatter | solution.py:187
  743.6 7.4 collective-permute-done.76
  (520 shorter events, 268.8 us)
Async XLA Ops:
  7.2 231.4 %all-gather.4.cloned.1.call-start = ((), (), s32[]{:S(2)}) async-start(), calls=%async_computation.4 | async-start | bytes 9437184 | tf_op jit(solution)/shard_map/all_gather | solution.py:159
  49.3 282.8 %all-gather.6.cloned.1.call-start = ((), (), s32[]{:S(2)}) async-start(), calls=%async_computation.5 | async-start | bytes 9437184 | tf_op jit(solution)/shard_map/all_gather | solution.py:159
  49.3 118.1 %collective-permute-start = (bf16[1024,2048]{1,0:T(8,128)(2,1)}, bf16[1024,2048]{1,0:T(8,128)(2,1)}, u32[]{:S(2)}, u32[]{:S(2)}) collective-permute-start(bf16[1024,2048]{1,0:T(8,128)(2,1)} %param.16), channel_id=1, source_target_pairs={{1,4},{3,6},{4,1},{6,3},{9,12},{11,14},{12,9},{14,11},{17,20},{19,... | collective-permute-start | bytes 12582920 | tf_op jit(solution)/shard_map/ppermute | solution.py:121
  57.2 52.3 %collective-permute-start.1 = (bf16[256,1024]{1,0:T(8,128)(2,1)S(1)}, bf16[256,1024]{1,0:T(8,128)(2,1)S(1)}, u32[]{:S(2)}, u32[]{:S(2)}) collective-permute-start(bf16[256,1024]{1,0:T(8,128)(2,1)S(1)} %pad_maximum_fusion.11), channel_id=1, source_target_pairs={{1,4},{3,6},{4,1},{6,3},{9,12},{11,14},{12,9},{14,11},{17,20},{19,... | collective-permute-start | bytes 1572872 | tf_op jit(solution)/shard_map/ppermute | solution.py:121
  59.1 55.5 %collective-permute-start.14 = (s32[2]{0:T(128)S(1)}, s32[2]{0:T(128)S(1)}, u32[]{:S(2)}, u32[]{:S(2)}) collective-permute-start(s32[2]{0:T(128)S(1)} %copy-done.75), channel_id=1, source_target_pairs={{0,1},{1,0},{2,3},{3,2},{4,5},{5,4},{6,7},{7,6},{8,9},{9,8},{10,11... | collective-permute-start | bytes 32 | tf_op jit(solution)/shard_map/ppermute | solution.py:121
  110.5 39.4 %collective-permute-start.11 = (bf16[272,1024]{1,0:T(8,128)(2,1)}, bf16[272,1024]{1,0:T(8,128)(2,1)}, u32[]{:S(2)}, u32[]{:S(2)}) collective-permute-start(bf16[272,1024]{1,0:T(8,128)(2,1)} %collective-permute-done.9.refs_9_), channel_id=1, source_target_pairs={{0,8},{1,9},{2,10},{3,11},{4,12},{5,13},{6,14},{7,15},{8,16},{9,17... | collective-permute-start | bytes 1671176 | tf_op jit(solution)/shard_map/ppermute | solution.py:121
  113.6 37.9 %collective-permute-start.6 = (bf16[272,1024]{1,0:T(8,128)(2,1)S(1)}, bf16[272,1024]{1,0:T(8,128)(2,1)S(1)}, u32[]{:S(2)}, u32[]{:S(2)}) collective-permute-start(bf16[272,1024]{1,0:T(8,128)(2,1)S(1)} %broadcast_select_fusion.12.refs_7_), channel_id=1, source_target_pairs={{0,1},{1,0},{2,3},{3,2},{4,5},{5,4},{6,7},{7,6},{8,9},{9,8},{10,11... | collective-permute-start | bytes 1671176 | tf_op jit(solution)/shard_map/ppermute | solution.py:121
  119.9 34.0 %collective-permute-start.8 = (bf16[272,1024]{1,0:T(8,128)(2,1)}, bf16[272,1024]{1,0:T(8,128)(2,1)}, u32[]{:S(2)}, u32[]{:S(2)}) collective-permute-start(bf16[272,1024]{1,0:T(8,128)(2,1)} %copy-done.76), channel_id=1, source_target_pairs={{0,1},{1,0},{2,3},{3,2},{4,5},{5,4},{6,7},{7,6},{8,9},{9,8},{10,11... | collective-permute-start | bytes 1671176 | tf_op jit(solution)/shard_map/ppermute | solution.py:121
  132.0 27.5 %collective-permute-start.10 = (bf16[272,1024]{1,0:T(8,128)(2,1)}, bf16[272,1024]{1,0:T(8,128)(2,1)}, u32[]{:S(2)}, u32[]{:S(2)}) collective-permute-start(bf16[272,1024]{1,0:T(8,128)(2,1)} %collective-permute-done.9.refs_9_), channel_id=1, source_target_pairs={{0,1},{1,0},{2,3},{3,2},{4,5},{5,4},{6,7},{7,6},{8,9},{9,8},{10,11... | collective-permute-start | bytes 1671176 | tf_op jit(solution)/shard_map/ppermute | solution.py:121
  153.9 34.8 %collective-permute-start.33 = (bf16[256,2048]{1,0:T(8,128)(2,1)S(1)}, bf16[256,2048]{1,0:T(8,128)(2,1)S(1)}, u32[]{:S(2)}, u32[]{:S(2)}) collective-permute-start(bf16[256,2048]{1,0:T(8,128)(2,1)S(1)} %constant_dynamic-update-slice_fusion.16), channel_id=1, source_target_pairs={{1,4},{3,6},{4,1},{6,3},{9,12},{11,14},{12,9},{14,11},{17,20},{19,... | collective-permute-start | bytes 3145736 | tf_op jit(solution)/shard_map/ppermute | solution.py:121
  159.5 29.1 %collective-permute-start.34 = (bf16[256,1024]{1,0:T(8,128)(2,1)S(1)}, bf16[256,1024]{1,0:T(8,128)(2,1)S(1)}, u32[]{:S(2)}, u32[]{:S(2)}) collective-permute-start(bf16[256,1024]{1,0:T(8,128)(2,1)S(1)} %bitcast.63), channel_id=1, source_target_pairs={{1,4},{3,6},{4,1},{6,3},{9,12},{11,14},{12,9},{14,11},{17,20},{19,... | collective-permute-start | bytes 1572872 | tf_op jit(solution)/shard_map/ppermute | solution.py:121
  189.8 160.4 %all-gather.8.cloned.1.call-start = ((), (), s32[]{:S(2)}) async-start(), calls=%async_computation.6 | async-start | bytes 4718592 | tf_op jit(solution)/shard_map/all_gather | solution.py:159
  189.8 60.5 %collective-permute-start.4 = (bf16[1024,2048]{1,0:T(8,128)(2,1)}, bf16[1024,2048]{1,0:T(8,128)(2,1)}, u32[]{:S(2)}, u32[]{:S(2)}) collective-permute-start(bf16[1024,2048]{1,0:T(8,128)(2,1)} %param.31), channel_id=1, source_target_pairs={{1,4},{3,6},{4,1},{6,3},{9,12},{11,14},{12,9},{14,11},{17,20},{19,... | collective-permute-start | bytes 12582920 | tf_op jit(solution)/shard_map/ppermute | solution.py:121
  194.8 22.6 %collective-permute-start.16 = (bf16[256,1024]{1,0:T(8,128)(2,1)}, bf16[256,1024]{1,0:T(8,128)(2,1)S(1)}, u32[]{:S(2)}, u32[]{:S(2)}) collective-permute-start(bf16[256,1024]{1,0:T(8,128)(2,1)} %collective-permute-done.3.refs_9_), channel_id=1, source_target_pairs={{0,8},{1,9},{2,10},{3,11},{4,12},{5,13},{6,14},{7,15},{8,16},{9,17... | collective-permute-start | bytes 1572872 | tf_op jit(solution)/shard_map/ppermute | solution.py:121
  195.1 29.2 %collective-permute-start.17 = (bf16[256,1024]{1,0:T(8,128)(2,1)}, bf16[256,1024]{1,0:T(8,128)(2,1)S(1)}, u32[]{:S(2)}, u32[]{:S(2)}) collective-permute-start(bf16[256,1024]{1,0:T(8,128)(2,1)} %broadcast_select_fusion.14.refs_7_), channel_id=1, source_target_pairs={{0,1},{1,0},{2,3},{3,2},{4,5},{5,4},{6,7},{7,6},{8,9},{9,8},{10,11... | collective-permute-start | bytes 1572872 | tf_op jit(solution)/shard_map/ppermute | solution.py:121
  195.2 29.2 %collective-permute-start.18 = (bf16[256,1024]{1,0:T(8,128)(2,1)}, bf16[256,1024]{1,0:T(8,128)(2,1)}, u32[]{:S(2)}, u32[]{:S(2)}) collective-permute-start(bf16[256,1024]{1,0:T(8,128)(2,1)} %collective-permute-done.2.refs_8_), channel_id=1, source_target_pairs={{0,1},{1,0},{2,3},{3,2},{4,5},{5,4},{6,7},{7,6},{8,9},{9,8},{10,11... | collective-permute-start | bytes 1572872 | tf_op jit(solution)/shard_map/ppermute | solution.py:121
  195.7 28.7 %collective-permute-start.19 = (bf16[256,1024]{1,0:T(8,128)(2,1)}, bf16[256,1024]{1,0:T(8,128)(2,1)}, u32[]{:S(2)}, u32[]{:S(2)}) collective-permute-start(bf16[256,1024]{1,0:T(8,128)(2,1)} %collective-permute-done.3.refs_9_), channel_id=1, source_target_pairs={{0,1},{1,0},{2,3},{3,2},{4,5},{5,4},{6,7},{7,6},{8,9},{9,8},{10,11... | collective-permute-start | bytes 1572872 | tf_op jit(solution)/shard_map/ppermute | solution.py:121
  219.7 358.3 %reduce-scatter.11.cloned.1.call-start = ((), (), s32[]{:S(2)}) async-start(), calls=%async_computation.10 | async-start | bytes 2621440 | tf_op jit(solution)/shard_map/reduce_scatter | solution.py:187
  255.0 22.5 %collective-permute-start.21 = (bf16[128,2048]{1,0:T(8,128)(2,1)S(1)}, bf16[128,2048]{1,0:T(8,128)(2,1)S(1)}, u32[]{:S(2)}, u32[]{:S(2)}) collective-permute-start(bf16[128,2048]{1,0:T(8,128)(2,1)S(1)} %get-tuple-element.224), channel_id=1, source_target_pairs={{0,2},{1,3},{2,0},{3,1},{4,6},{5,7},{6,4},{7,5},{8,10},{9,11},{10,... | collective-permute-start | bytes 1572872 | tf_op jit(solution)/shard_map/ppermute | solution.py:121
  255.2 23.2 %collective-permute-start.22 = (bf16[128,2048]{1,0:T(8,128)(2,1)S(1)}, bf16[128,2048]{1,0:T(8,128)(2,1)S(1)}, u32[]{:S(2)}, u32[]{:S(2)}) collective-permute-start(bf16[128,2048]{1,0:T(8,128)(2,1)S(1)} %get-tuple-element.227), channel_id=1, source_target_pairs={{0,4},{1,5},{2,6},{3,7},{4,0},{5,1},{6,2},{7,3},{8,12},{9,13},{10,... | collective-permute-start | bytes 1572872 | tf_op jit(solution)/shard_map/ppermute | solution.py:121
  267.5 22.1 %collective-permute-start.24 = (bf16[128,2048]{1,0:T(8,128)(2,1)S(1)}, bf16[128,2048]{1,0:T(8,128)(2,1)S(1)}, u32[]{:S(2)}, u32[]{:S(2)}) collective-permute-start(bf16[128,2048]{1,0:T(8,128)(2,1)S(1)} %get-tuple-element.184), channel_id=1, source_target_pairs={{0,4},{1,5},{2,6},{3,7},{4,0},{5,1},{6,2},{7,3},{8,12},{9,13},{10,... | collective-permute-start | bytes 1572872 | tf_op jit(solution)/shard_map/ppermute | solution.py:121
  293.4 23.7 %collective-permute-start.29 = (bf16[128,2048]{1,0:T(8,128)(2,1)S(1)}, bf16[128,2048]{1,0:T(8,128)(2,1)S(1)}, u32[]{:S(2)}, u32[]{:S(2)}) collective-permute-start(bf16[128,2048]{1,0:T(8,128)(2,1)S(1)} %get-tuple-element.242), channel_id=1, source_target_pairs={{0,2},{1,3},{2,0},{3,1},{4,6},{5,7},{6,4},{7,5},{8,10},{9,11},{10,... | collective-permute-start | bytes 1572872 | tf_op jit(solution)/shard_map/ppermute | solution.py:121
  293.7 23.3 %collective-permute-start.28 = (bf16[128,2048]{1,0:T(8,128)(2,1)S(1)}, bf16[128,2048]{1,0:T(8,128)(2,1)S(1)}, u32[]{:S(2)}, u32[]{:S(2)}) collective-permute-start(bf16[128,2048]{1,0:T(8,128)(2,1)S(1)} %get-tuple-element.240), channel_id=1, source_target_pairs={{0,4},{1,5},{2,6},{3,7},{4,0},{5,1},{6,2},{7,3},{8,12},{9,13},{10,... | collective-permute-start | bytes 1572872 | tf_op jit(solution)/shard_map/ppermute | solution.py:121
  294.3 22.4 %collective-permute-start.30 = (bf16[128,2048]{1,0:T(8,128)(2,1)S(1)}, bf16[128,2048]{1,0:T(8,128)(2,1)S(1)}, u32[]{:S(2)}, u32[]{:S(2)}) collective-permute-start(bf16[128,2048]{1,0:T(8,128)(2,1)S(1)} %get-tuple-element.240), channel_id=1, source_target_pairs={{0,2},{1,3},{2,0},{3,1},{4,6},{5,7},{6,4},{7,5},{8,10},{9,11},{10,... | collective-permute-start | bytes 1572872 | tf_op jit(solution)/shard_map/ppermute | solution.py:121
  304.6 23.2 %collective-permute-start.31 = (bf16[128,2048]{1,0:T(8,128)(2,1)S(1)}, bf16[128,2048]{1,0:T(8,128)(2,1)S(1)}, u32[]{:S(2)}, u32[]{:S(2)}) collective-permute-start(bf16[128,2048]{1,0:T(8,128)(2,1)S(1)} %collective-permute-done.27), channel_id=1, source_target_pairs={{0,2},{1,3},{2,0},{3,1},{4,6},{5,7},{6,4},{7,5},{8,10},{9,11},{10,... | collective-permute-start | bytes 1572872 | tf_op jit(solution)/shard_map/ppermute | solution.py:121
  374.2 22.8 %collective-permute-start.35 = (bf16[128,2048]{1,0:T(8,128)(2,1)S(1)}, bf16[128,2048]{1,0:T(8,128)(2,1)S(1)}, u32[]{:S(2)}, u32[]{:S(2)}) collective-permute-start(bf16[128,2048]{1,0:T(8,128)(2,1)S(1)} %get-tuple-element.220), channel_id=1, source_target_pairs={{0,2},{1,3},{2,0},{3,1},{4,6},{5,7},{6,4},{7,5},{8,10},{9,11},{10,... | collective-permute-start | bytes 1572872 | tf_op jit(solution)/shard_map/ppermute | solution.py:121
  384.2 22.2 %collective-permute-start.38 = (bf16[128,2048]{1,0:T(8,128)(2,1)S(1)}, bf16[128,2048]{1,0:T(8,128)(2,1)S(1)}, u32[]{:S(2)}, u32[]{:S(2)}) collective-permute-start(bf16[128,2048]{1,0:T(8,128)(2,1)S(1)} %get-tuple-element.172), channel_id=1, source_target_pairs={{0,4},{1,5},{2,6},{3,7},{4,0},{5,1},{6,2},{7,3},{8,12},{9,13},{10,... | collective-permute-start | bytes 1572872 | tf_op jit(solution)/shard_map/ppermute | solution.py:121
  388.2 49.8 %collective-permute-start.80 = (bf16[1024,1024]{1,0:T(8,128)(2,1)S(1)}, bf16[1024,1024]{1,0:T(8,128)(2,1)S(1)}, u32[]{:S(2)}, u32[]{:S(2)}) collective-permute-start(bf16[1024,1024]{1,0:T(8,128)(2,1)S(1)} %fusion.107), channel_id=1, source_target_pairs={{0,1},{1,0},{2,3},{3,2},{4,5},{5,4},{6,7},{7,6},{8,9},{9,8},{10,11... | collective-permute-start | bytes 6291464 | tf_op jit(solution)/shard_map/ppermute | solution.py:121
  423.9 23.2 %collective-permute-start.45 = (bf16[128,2048]{1,0:T(8,128)(2,1)S(1)}, bf16[128,2048]{1,0:T(8,128)(2,1)}, u32[]{:S(2)}, u32[]{:S(2)}) collective-permute-start(bf16[128,2048]{1,0:T(8,128)(2,1)S(1)} %collective-permute-done.41), channel_id=1, source_target_pairs={{0,2},{1,3},{2,0},{3,1},{4,6},{5,7},{6,4},{7,5},{8,10},{9,11},{10,... | collective-permute-start | bytes 1572872 | tf_op jit(solution)/shard_map/ppermute | solution.py:121
  425.0 23.9 %collective-permute-start.46 = (bf16[128,2048]{1,0:T(8,128)(2,1)S(1)}, bf16[128,2048]{1,0:T(8,128)(2,1)}, u32[]{:S(2)}, u32[]{:S(2)}) collective-permute-start(bf16[128,2048]{1,0:T(8,128)(2,1)S(1)} %collective-permute-done.44), channel_id=1, source_target_pairs={{0,4},{1,5},{2,6},{3,7},{4,0},{5,1},{6,2},{7,3},{8,12},{9,13},{10,... | collective-permute-start | bytes 1572872 | tf_op jit(solution)/shard_map/ppermute | solution.py:121
  441.9 262.5 %reduce-scatter.7.cloned.1.call-start = ((), (), s32[]{:S(2)}) async-start(), calls=%async_computation.8 | async-start | bytes 5242880 | tf_op jit(solution)/shard_map/reduce_scatter | solution.py:187
  476.8 76.8 %collective-permute-start.78 = (bf16[1024,2048]{1,0:T(8,128)(2,1)}, bf16[1024,2048]{1,0:T(8,128)(2,1)}, u32[]{:S(2)}, u32[]{:S(2)}) collective-permute-start(bf16[1024,2048]{1,0:T(8,128)(2,1)} %convolution_convert_fusion), channel_id=1, source_target_pairs={{0,1},{1,0},{2,3},{3,2},{4,5},{5,4},{6,7},{7,6},{8,9},{9,8},{10,11... | collective-permute-start | bytes 12582920 | tf_op jit(solution)/shard_map/ppermute | solution.py:121
  482.1 47.5 %collective-permute-start.51 = (bf16[128,2048]{1,0:T(8,128)(2,1)}, bf16[128,2048]{1,0:T(8,128)(2,1)}, u32[]{:S(2)}, u32[]{:S(2)}) collective-permute-start(bf16[128,2048]{1,0:T(8,128)(2,1)} %get-tuple-element.208), channel_id=1, source_target_pairs={{0,2},{1,3},{2,0},{3,1},{4,6},{5,7},{6,4},{7,5},{8,10},{9,11},{10,... | collective-permute-start | bytes 1572872 | tf_op jit(solution)/shard_map/ppermute | solution.py:121
  483.3 46.3 %collective-permute-start.53 = (bf16[128,2048]{1,0:T(8,128)(2,1)}, bf16[128,2048]{1,0:T(8,128)(2,1)}, u32[]{:S(2)}, u32[]{:S(2)}) collective-permute-start(bf16[128,2048]{1,0:T(8,128)(2,1)} %get-tuple-element.209), channel_id=1, source_target_pairs={{0,4},{1,5},{2,6},{3,7},{4,0},{5,1},{6,2},{7,3},{8,12},{9,13},{10,... | collective-permute-start | bytes 1572872 | tf_op jit(solution)/shard_map/ppermute | solution.py:121
  485.8 59.6 %collective-permute-start.49 = (bf16[128,2048]{1,0:T(8,128)(2,1)}, bf16[128,2048]{1,0:T(8,128)(2,1)}, u32[]{:S(2)}, u32[]{:S(2)}) collective-permute-start(bf16[128,2048]{1,0:T(8,128)(2,1)} %get-tuple-element.211), channel_id=1, source_target_pairs={{0,2},{1,3},{2,0},{3,1},{4,6},{5,7},{6,4},{7,5},{8,10},{9,11},{10,... | collective-permute-start | bytes 1572872 | tf_op jit(solution)/shard_map/ppermute | solution.py:121
  488.6 58.2 %collective-permute-start.50 = (bf16[128,2048]{1,0:T(8,128)(2,1)}, bf16[128,2048]{1,0:T(8,128)(2,1)}, u32[]{:S(2)}, u32[]{:S(2)}) collective-permute-start(bf16[128,2048]{1,0:T(8,128)(2,1)} %get-tuple-element.210), channel_id=1, source_target_pairs={{0,4},{1,5},{2,6},{3,7},{4,0},{5,1},{6,2},{7,3},{8,12},{9,13},{10,... | collective-permute-start | bytes 1572872 | tf_op jit(solution)/shard_map/ppermute | solution.py:121
  493.9 222.8 %reduce-scatter.9.cloned.1.call-start = ((), (), s32[]{:S(2)}) async-start(), calls=%async_computation.9 | async-start | bytes 5242880 | tf_op jit(solution)/shard_map/reduce_scatter | solution.py:187
  545.3 77.5 %collective-permute-start.62 = (bf16[1024,2048]{1,0:T(8,128)(2,1)}, bf16[1024,2048]{1,0:T(8,128)(2,1)}, u32[]{:S(2)}, u32[]{:S(2)}) collective-permute-start(bf16[1024,2048]{1,0:T(8,128)(2,1)} %convolution_convert_fusion.1), channel_id=1, source_target_pairs={{0,1},{1,0},{2,3},{3,2},{4,5},{5,4},{6,7},{7,6},{8,9},{9,8},{10,11... | collective-permute-start | bytes 12582920 | tf_op jit(solution)/shard_map/ppermute | solution.py:121
  546.8 94.6 %collective-permute-start.65 = (bf16[128,2048]{1,0:T(8,128)(2,1)}, bf16[128,2048]{1,0:T(8,128)(2,1)}, u32[]{:S(2)}, u32[]{:S(2)}) collective-permute-start(bf16[128,2048]{1,0:T(8,128)(2,1)} %get-tuple-element.198), channel_id=1, source_target_pairs={{0,2},{1,3},{2,0},{3,1},{4,6},{5,7},{6,4},{7,5},{8,10},{9,11},{10,... | collective-permute-start | bytes 1572872 | tf_op jit(solution)/shard_map/ppermute | solution.py:121
  549.9 25.5 %collective-permute-start.56 = (bf16[256,2048]{1,0:T(8,128)(2,1)S(1)}, bf16[256,2048]{1,0:T(8,128)(2,1)S(1)}, u32[]{:S(2)}, u32[]{:S(2)}) collective-permute-start(bf16[256,2048]{1,0:T(8,128)(2,1)S(1)} %fusion.43), channel_id=1, source_target_pairs={{1,5},{3,7},{4,0},{6,2},{9,13},{11,15},{12,8},{14,10},{17,21},{19,... | collective-permute-start | bytes 3145736 | tf_op jit(solution)/shard_map/ppermute | solution.py:121
  552.2 24.4 %collective-permute-start.55 = (bf16[256,2048]{1,0:T(8,128)(2,1)S(1)}, bf16[256,2048]{1,0:T(8,128)(2,1)}, u32[]{:S(2)}, u32[]{:S(2)}) collective-permute-start(bf16[256,2048]{1,0:T(8,128)(2,1)S(1)} %fusion.43), channel_id=1, source_target_pairs={{0,1},{2,3},{5,4},{7,6},{8,9},{10,11},{13,12},{15,14},{16,17},{18,... | collective-permute-start | bytes 3145736 | tf_op jit(solution)/shard_map/ppermute | solution.py:121
  561.9 172.3 %reduce-scatter.5.cloned.1.call-start = ((), (), s32[]{:S(2)}) async-start(), calls=%async_computation.7 | async-start | bytes 5242880 | tf_op jit(solution)/shard_map/reduce_scatter | solution.py:187
  586.1 55.3 %collective-permute-start.67 = (bf16[128,2048]{1,0:T(8,128)(2,1)}, bf16[128,2048]{1,0:T(8,128)(2,1)}, u32[]{:S(2)}, u32[]{:S(2)}) collective-permute-start(bf16[128,2048]{1,0:T(8,128)(2,1)} %get-tuple-element.197), channel_id=1, source_target_pairs={{0,4},{1,5},{2,6},{3,7},{4,0},{5,1},{6,2},{7,3},{8,12},{9,13},{10,... | collective-permute-start | bytes 1572872 | tf_op jit(solution)/shard_map/ppermute | solution.py:121
  595.7 54.1 %collective-permute-start.63 = (bf16[128,2048]{1,0:T(8,128)(2,1)}, bf16[128,2048]{1,0:T(8,128)(2,1)}, u32[]{:S(2)}, u32[]{:S(2)}) collective-permute-start(bf16[128,2048]{1,0:T(8,128)(2,1)} %get-tuple-element.196), channel_id=1, source_target_pairs={{0,2},{1,3},{2,0},{3,1},{4,6},{5,7},{6,4},{7,5},{8,10},{9,11},{10,... | collective-permute-start | bytes 1572872 | tf_op jit(solution)/shard_map/ppermute | solution.py:121
  602.9 46.9 %collective-permute-start.64 = (bf16[128,2048]{1,0:T(8,128)(2,1)}, bf16[128,2048]{1,0:T(8,128)(2,1)}, u32[]{:S(2)}, u32[]{:S(2)}) collective-permute-start(bf16[128,2048]{1,0:T(8,128)(2,1)} %get-tuple-element.199), channel_id=1, source_target_pairs={{0,4},{1,5},{2,6},{3,7},{4,0},{5,1},{6,2},{7,3},{8,12},{9,13},{10,... | collective-permute-start | bytes 1572872 | tf_op jit(solution)/shard_map/ppermute | solution.py:121
  622.9 25.5 %collective-permute-start.61 = (bf16[256,2048]{1,0:T(8,128)(2,1)S(1)}, bf16[256,2048]{1,0:T(8,128)(2,1)}, u32[]{:S(2)}, u32[]{:S(2)}) collective-permute-start(bf16[256,2048]{1,0:T(8,128)(2,1)S(1)} %collective-permute-done.60), channel_id=1, source_target_pairs={{0,1},{2,3},{5,4},{7,6},{8,9},{10,11},{13,12},{15,14},{16,17},{18,... | collective-permute-start | bytes 3145736 | tf_op jit(solution)/shard_map/ppermute | solution.py:121
  704.4 21.8 %collective-permute-start.77 = (bf16[256,2048]{1,0:T(8,128)(2,1)}, bf16[256,2048]{1,0:T(8,128)(2,1)S(1)}, u32[]{:S(2)}, u32[]{:S(2)}) collective-permute-start(bf16[256,2048]{1,0:T(8,128)(2,1)} %reduce-scatter.7.cloned.1.call-done), channel_id=1, source_target_pairs={{1,4},{3,6},{4,1},{6,3},{9,12},{11,14},{12,9},{14,11},{17,20},{19,... | collective-permute-start | bytes 3145736 | tf_op jit(solution)/shard_map/ppermute | solution.py:121
  716.7 24.0 %collective-permute-start.79 = (bf16[256,2048]{1,0:T(8,128)(2,1)}, bf16[256,2048]{1,0:T(8,128)(2,1)}, u32[]{:S(2)}, u32[]{:S(2)}) collective-permute-start(bf16[256,2048]{1,0:T(8,128)(2,1)} %reduce-scatter.9.cloned.1.call-done), channel_id=1, source_target_pairs={{1,4},{3,6},{4,1},{6,3},{9,12},{11,14},{12,9},{14,11},{17,20},{19,... | collective-permute-start | bytes 3145736 | tf_op jit(solution)/shard_map/ppermute | solution.py:121
  (136 other events, 1750.8 us)
Sparse Core Ops, SparseCore 0:
  49.4 107.5 all-gather.3
  189.9 89.6 all-gather.5
  281.2 44.6 all-gather.7
  442.0 53.0 reduce-scatter.10
  497.2 77.5 reduce-scatter.6
  577.0 77.2 reduce-scatter.8
  656.6 77.5 reduce-scatter.4

commit v3 on v2

--- a/solution.py
+++ b/solution.py
@@ -614,14 +614,16 @@
 
     ff_both = dot_nn(second_in, full_ff)
     ff_gate, ff_up = ff_both[:, :units], ff_both[:, units:]
+    hidden = (ff_gate * (0.5 * (1.0 + lax.erf(ff_gate * INV_ROOT2))) * ff_up).astype(jnp.bfloat16)
+    hidden, ff_both = together(hidden, ff_both)
+    feed_near, feed_far = core_halves(place, grad_feed)
+    down_got, _ = core_far(place, feed_far, hidden)
+    down_sum = core_near(feed_near, hidden, down_got)
+    down_sum, full_down = together(down_sum, full_down)
+    share_down = queue_scatter(place, down_sum)
+    ff_gate, ff_up = ff_both[:, :units], ff_both[:, units:]
     normal_cdf = 0.5 * (1.0 + lax.erf(ff_gate * INV_ROOT2))
     activation = ff_gate * normal_cdf
-    hidden = (activation * ff_up).astype(jnp.bfloat16)
-    feed_near, feed_far = core_halves(place, grad_feed)
-    hidden, full_down = together(hidden, full_down)
-    down_got, _ = core_far(place, feed_far, hidden)
-    down_sum = core_near(feed_near, hidden, down_got)
-    share_down = queue_scatter(place, down_sum)
     e_away = dot_nt(far_rows(place, hidden), full_down).astype(jnp.bfloat16)
     grad_hidden = dot_nn(grad_feed, full_down)
     density = jnp.exp(-0.5 * ff_gate * ff_gate) * INV_ROOT_TWO_PI
@@ -696,6 +698,7 @@
     share_down = to_owner(place, share_down).T
     share_ff = to_owner(place, share_ff)
     share_og = to_owner(place, share_og)
+    share_vqk, grad_tokens = together(share_vqk, grad_tokens)
     share_vqk = to_owner(place, share_vqk)
     picks = []
     for start, size in ((HEAD_VALUE, HEAD_KEY), (HEAD_VALUE + HEAD_KEY, HEAD_KEY), (0, HEAD_VALUE)):

time: 768 us -> 795 us (1.035)
  the two profiles are of different devices: /device:TPU:1 before, /device:TPU:0 now
where the time goes in v3:
time: 795 us; the launch traced here: 779 us
  starting transfers between devices  203 us (26%)
  waiting for transfers between devices  203 us (26%)
  matrix products  157 us (20%)
  local copies, waits for them, and re-layouts  97.3 us (12%)
  other arithmetic  63.2 us (8%)
  Pallas kernels  39.3 us (5%)
  between operations  16.5 us (2%)
    ppermute x89, starting transfers between devices, send(): return lax.ppermute(value, BOTH, pairs)  202 us
    ppermute x89, waiting for transfers between devices, send(): return lax.ppermute(value, BOTH, pairs)  185 us
    dot_general x12, matrix products, dot_nt(): lax.dot_general(left, right, (((1,), (1,)), ((), ())), preferred_element_...  60 us
    dot_general x10, matrix products, dot_tn(): lax.dot_general(left, right, (((0,), (0,)), ((), ())), preferred_element_...  49.9 us
    dot_general x4, matrix products, dot_nn(): lax.dot_general(left, right, (((1,), (0,)), ((), ())), preferred_element_...  47 us
    dynamic_update_slice x30, local copies, waits for them, and re-layouts, assemble(): whole = lax.dynamic_update_slice_in_dim(whole, rows, start, axis=0)  27 us
    pallas_call x2, Pallas kernels, retention_forward(): pl.pallas_call(functools.partial(forward_kernel, head, place.na, len(held...  26.7 us
    unnamed x216, local copies, waits for them, and re-layouts  20.4 us
  transfers between devices with their start and end apart: 96, of which 33 were waited for; matrix products, arithmetic and copies ran while one was open for 34% of the time, Pallas kernels for 5%

profile of v3, /device:TPU:0, one launch (start us, length us, event | category | flops | bytes accessed | tf_op | source)
XLA Modules:
  0.0 779.4 jit_solution(18352275873351368209)
XLA Ops:
  17.2 8.7 %collective-permute-done.7.refs_8_ = bf16[272,1024]{1,0:T(8,128)(2,1)S(1)} collective-permute-done((bf16[272,1024]{1,0:T(8,128)(2,1)S(1)}, bf16[272,1024]{1,0:T(8,128)(2,1)S(1)}, u32[]{:S(2)}, u32[]{:S(2)}) %collective-permute-start.7) | collective-permute-done | bytes 557088 | tf_op jit(solution)/shard_map/ppermute | solution.py:121
  26.7 13.9 %collective-permute-done.9.refs_9_ = bf16[272,1024]{1,0:T(8,128)(2,1)} collective-permute-done((bf16[272,1024]{1,0:T(8,128)(2,1)S(1)}, bf16[272,1024]{1,0:T(8,128)(2,1)}, u32[]{:S(2)}, u32[]{:S(2)}) %collective-permute-start.9) | collective-permute-done | bytes 557088 | tf_op jit(solution)/shard_map/ppermute | solution.py:121
  45.6 14.1 %collective-permute-start.14 = (s32[2]{0:T(128)S(1)}, s32[2]{0:T(128)S(1)}, u32[]{:S(2)}, u32[]{:S(2)}) collective-permute-start(s32[2]{0:T(128)S(1)} %copy-done.88), channel_id=1, source_target_pairs={{0,1},{1,0},{2,3},{3,2},{4,5},{5,4},{6,7},{7,6},{8,9},{9,8},{10,11... | collective-permute-start | bytes 32 | tf_op jit(solution)/shard_map/ppermute | solution.py:121
  63.8 50.2 %collective-permute-start.6 = (bf16[272,1024]{1,0:T(8,128)(2,1)S(1)}, bf16[272,1024]{1,0:T(8,128)(2,1)S(1)}, u32[]{:S(2)}, u32[]{:S(2)}) collective-permute-start(bf16[272,1024]{1,0:T(8,128)(2,1)S(1)} %broadcast_select_fusion.12.refs_7_), channel_id=1, source_target_pairs={{0,1},{1,0},{2,3},{3,2},{4,5},{5,4},{6,7},{7,6},{8,9},{9,8},{10,11... | collective-permute-start | bytes 1671176 | tf_op jit(solution)/shard_map/ppermute | solution.py:121
  120.4 12.1 %collective-permute-start.10 = (bf16[272,1024]{1,0:T(8,128)(2,1)}, bf16[272,1024]{1,0:T(8,128)(2,1)}, u32[]{:S(2)}, u32[]{:S(2)}) collective-permute-start(bf16[272,1024]{1,0:T(8,128)(2,1)} %collective-permute-done.9.refs_9_), channel_id=1, source_target_pairs={{0,1},{1,0},{2,3},{3,2},{4,5},{5,4},{6,7},{7,6},{8,9},{9,8},{10,11... | collective-permute-start | bytes 1671176 | tf_op jit(solution)/shard_map/ppermute | solution.py:121
  132.5 17.9 %collective-permute-start.12 = (bf16[272,1024]{1,0:T(8,128)(2,1)}, bf16[272,1024]{1,0:T(8,128)(2,1)}, u32[]{:S(2)}, u32[]{:S(2)}) collective-permute-start(bf16[272,1024]{1,0:T(8,128)(2,1)} %collective-permute-done.11.refs_10_), channel_id=1, source_target_pairs={{0,1},{1,0},{2,3},{3,2},{4,5},{5,4},{6,7},{7,6},{8,9},{9,8},{10,11... | collective-permute-start | bytes 1671176 | tf_op jit(solution)/shard_map/ppermute | solution.py:121
  160.5 8.0 %collective-permute-done.3.refs_9_ = bf16[256,1024]{1,0:T(8,128)(2,1)} collective-permute-done((bf16[256,1024]{1,0:T(8,128)(2,1)}, bf16[256,1024]{1,0:T(8,128)(2,1)}, u32[]{:S(2)}, u32[]{:S(2)}) %collective-permute-start.3) | collective-permute-done | bytes 524320 | tf_op jit(solution)/shard_map/ppermute | solution.py:121
  176.4 13.2 %shard_map.263 = (bf16[2048,1024]{1,0:T(8,128)(2,1)}, bf16[1024,2048]{1,0:T(8,128)(2,1)}, f32[1024,1024]{1,0:T(8,128)}, f32[2,1024,1]{2,1,0:T(8,128)}) custom-call(f32[2]{0:T(128)} %negate_log-plus-one_fusion.refs_0_.log_gamma, s32[1024,1]{1,0:T(8,128)} %copy.43.refs_1_.row_segment, s32[1,1024]{1,0:T(1,128)} %bitcast.58, ...), custom_call_target="tpu_custom_call" | custom-call | flops 5905580032 | bytes 20971520 | tf_op jit(solution)/shard_map/pallas_call | solution.py:378
  196.0 19.4 %collective-permute-done.16.refs_10_ = bf16[256,1024]{1,0:T(8,128)(2,1)S(1)} collective-permute-done((bf16[256,1024]{1,0:T(8,128)(2,1)}, bf16[256,1024]{1,0:T(8,128)(2,1)S(1)}, u32[]{:S(2)}, u32[]{:S(2)}) %collective-permute-start.16) | collective-permute-done | bytes 524320 | tf_op jit(solution)/shard_map/ppermute | solution.py:121
  221.2 13.5 %shard_map.264 = (bf16[2048,1024]{1,0:T(8,128)(2,1)}, bf16[1024,2048]{1,0:T(8,128)(2,1)}, f32[1024,1024]{1,0:T(8,128)}, f32[2,1024,1]{2,1,0:T(8,128)}) custom-call(f32[2]{0:T(128)} %negate_log-plus-one_fusion.refs_0_.log_gamma, s32[1024,1]{1,0:T(8,128)} %copy.43.refs_1_.row_segment, ...), custom_call_target="tpu_custom_call", output_to_operand_aliasing={{1}: (15, {}), {2}: (16, {}), {3}: (17, {})} | custom-call | flops 5905580032 | bytes 20971520 | tf_op jit(solution)/shard_map/pallas_call | solution.py:378
  234.7 11.7 %multiply_convert_fusion.2 = (bf16[1024,1024]{1,0:T(8,128)(2,1)S(1)}, f32[1024,1024]{1,0:T(8,128)}) fusion(f32[1024,1024]{1,0:T(8,128)} %get-tuple-element.57.normed, bf16[1024,2048]{1,0:T(8,128)(2,1)} %fusion.5.refs_6_, bf16[2048,2048]{1,0:T(8,128)(2,1)} %all-gather.4.cloned.1.call-done), kind=kOutput, calls=%fused_computation.37 | convolution fusion | flops 4301258752 | bytes 18874368 | tf_op jit(solution)/shard_map/dot_general | solution.py:52
  255.6 8.2 %collective-permute-done.23 = bf16[128,2048]{1,0:T(8,128)(2,1)S(1)} collective-permute-done((bf16[128,2048]{1,0:T(8,128)(2,1)S(1)}, bf16[128,2048]{1,0:T(8,128)(2,1)S(1)}, u32[]{:S(2)}, u32[]{:S(2)}) %collective-permute-start.23) | collective-permute-done | bytes 524320 | tf_op jit(solution)/shard_map/ppermute | solution.py:121
  267.5 7.6 collective-permute-done.21
  276.7 10.1 %collective-permute-done.24 = bf16[128,2048]{1,0:T(8,128)(2,1)S(1)} collective-permute-done((bf16[128,2048]{1,0:T(8,128)(2,1)S(1)}, bf16[128,2048]{1,0:T(8,128)(2,1)S(1)}, u32[]{:S(2)}, u32[]{:S(2)}) %collective-permute-start.24) | collective-permute-done | bytes 524320 | tf_op jit(solution)/shard_map/ppermute | solution.py:121
  299.1 8.0 %collective-permute-done.27 = bf16[128,2048]{1,0:T(8,128)(2,1)S(1)} collective-permute-done((bf16[128,2048]{1,0:T(8,128)(2,1)S(1)}, bf16[128,2048]{1,0:T(8,128)(2,1)S(1)}, u32[]{:S(2)}, u32[]{:S(2)}) %collective-permute-start.27) | collective-permute-done | bytes 524320 | tf_op jit(solution)/shard_map/ppermute | solution.py:121
  309.9 8.4 %collective-permute-done.28 = bf16[128,2048]{1,0:T(8,128)(2,1)S(1)} collective-permute-done((bf16[128,2048]{1,0:T(8,128)(2,1)S(1)}, bf16[128,2048]{1,0:T(8,128)(2,1)S(1)}, u32[]{:S(2)}, u32[]{:S(2)}) %collective-permute-start.28) | collective-permute-done | bytes 524320 | tf_op jit(solution)/shard_map/ppermute | solution.py:121
  320.8 7.6 collective-permute-done.31
  330.1 12.5 %fusion.221 = f32[1024,2048]{1,0:T(8,128)S(1)} fusion(bf16[1024,2048]{1,0:T(8,128)(2,1)} %constant_dynamic-update-slice_fusion.8, bf16[2048,2048]{1,0:T(8,128)(2,1)} %all-gather.6.cloned.1.call-done), kind=kOutput, calls=%fused_computation.433 | convolution fusion | flops 8589934592 | bytes 20971520 | tf_op jit(solution)/shard_map/dot_general | solution.py:52
  349.9 4.4 constant_dynamic-slice_fusion.47
  356.6 5.3 add_convert_fusion.5
  361.8 11.3 %fusion.11 = (bf16[1024,1024]{1,0:T(8,128)(2,1)S(1)}, bf16[1024,1024]{1,0:T(8,128)(2,1)S(1)}) fusion(f32[1024,2048]{1,0:T(8,128)} %copy-done.21, bf16[1024,2048]{1,0:T(8,128)(2,1)} %copy-done.9, bf16[2048,1024]{1,0:T(8,128)(2,1)} %all-gather.8.cloned.1.call-done), kind=kOutput, calls=%fused_computation.25 | convolution fusion | flops 4309647360 | bytes 20971520 | tf_op jit(solution)/shard_map/dot_general | solution.py:52
  375.2 11.3 %convolution_convert_fusion.3 = bf16[512,2048]{1,0:T(8,128)(2,1)S(1)} fusion(bf16[2048,2048]{1,0:T(8,128)(2,1)} %all-gather.6.cloned.1.call-done, bf16[128,2048]{1,0:T(8,128)(2,1)S(1)} %get-tuple-element.181, bf16[128,2048]{1,0:T(8,128)(2,1)S(1)} %get-tuple-element.180, bf16[128,2048]{1,0:T(8,128)(2,1)S(1)} %get-tuple-element.179, ...), kind=kOutput, calls=%fused_computation.61 | convolution fusion | flops 4304404480 | bytes 12582912 | tf_op jit(solution)/shard_map/dot_general | solution.py:58
  390.9 7.0 fusion.70
  397.8 3.8 collective-permute-done.38
  404.9 4.4 constant_dynamic-slice_fusion.11
  413.4 10.4 %collective-permute-done.39 = bf16[128,2048]{1,0:T(8,128)(2,1)S(1)} collective-permute-done((bf16[128,2048]{1,0:T(8,128)(2,1)S(1)}, bf16[128,2048]{1,0:T(8,128)(2,1)S(1)}, u32[]{:S(2)}, u32[]{:S(2)}) %collective-permute-start.39) | collective-permute-done | bytes 524320 | tf_op jit(solution)/shard_map/ppermute | solution.py:121
  437.5 8.9 %collective-permute-done.42 = bf16[128,2048]{1,0:T(8,128)(2,1)} collective-permute-done((bf16[128,2048]{1,0:T(8,128)(2,1)}, bf16[128,2048]{1,0:T(8,128)(2,1)}, u32[]{:S(2)}, u32[]{:S(2)}) %collective-permute-start.42) | collective-permute-done | bytes 524320 | tf_op jit(solution)/shard_map/ppermute | solution.py:121
  450.6 6.9 collective-permute-done.43
  461.1 6.6 collective-permute-done.46
  474.2 11.5 %multiply_convert_fusion = (bf16[1024,1024]{1,0:T(8,128)(2,1)S(1)}, f32[1024,1024]{1,0:T(8,128)}) fusion(f32[1024,1024]{1,0:T(8,128)S(1)} %copy-done.100, f32[1024,1024]{1,0:T(8,128)S(1)} %copy-done.30, bf16[1024,2048]{1,0:T(8,128)(2,1)} %constant_dynamic-update-slice_fusion, bf16[2048,2048]{1,0:T(8,128)(2,1)} %all-gather.4.cloned.1.call-done), kind=kOutput, calls=%fused_computation.33 | convolution fusion | flops 4307550208 | bytes 23068672 | tf_op jit(solution)/shard_map/dot_general | solution.py:52
  491.4 6.8 convolution_convert_fusion
  515.0 6.9 fusion.22
  522.0 7.3 fusion.20
  529.4 12.6 %shard_map.265 = bf16[1024,2048]{1,0:T(8,128)(2,1)} custom-call(f32[2]{0:T(128)S(1)} %copy-done.7, s32[1024,1]{1,0:T(8,128)S(1)} %copy-done.1, s32[1,1024]{1,0:T(1,128)S(1)} %bitcast.60, f32[1024,128]{1,0:T(8,128)S(1)} %copy-done.3, f32[1024,128]{1,0:T(8,128)S(1)} %copy-done.2, f32[1024,128]{1,0:T(8,128)S(1)} %copy-done, ...), custom_call_target="tpu_custom_call" | custom-call | flops 7516192768 | bytes 16777216 | tf_op jit(solution)/shard_map/pallas_call | solution.py:480
  542.0 8.8 %convolution_convert_fusion.1 = bf16[1024,2048]{1,0:T(8,128)(2,1)} fusion(bf16[1024,2048]{1,0:T(8,128)(2,1)} %shard_map.265, bf16[1024,256]{1,0:T(8,128)(2,1)S(1)} %copy-done.56, bf16[1024,256]{1,0:T(8,128)(2,1)S(1)} %copy-done.58, bf16[1024,256]{1,0:T(8,128)(2,1)S(1)} %copy-done.60, bf16[1024,256]{1,0:T(8,128)(2,1)S(1)} %copy-done.62), kind=kOutput, calls=%fused_computation.43 | convolution fusion | flops 4305453056 | bytes 10485760 | tf_op jit(solution)/shard_map/dot_general | solution.py:64
  553.3 3.7 fusion.127
  559.5 4.4 fusion.124
  564.9 8.4 %add_convert_fusion = bf16[1024,2048]{1,0:T(8,128)(2,1)} fusion(bf16[1024,2048]{1,0:T(8,128)(2,1)} %collective-permute-done.79, bf16[1024,256]{1,0:T(8,128)(2,1)S(1)} %copy-done.64, bf16[1024,256]{1,0:T(8,128)(2,1)S(1)} %copy-done.65, bf16[1024,256]{1,0:T(8,128)(2,1)S(1)} %copy-done.66, bf16[1024,256]{1,0:T(8,128)(2,1)S(1)} %copy-done.63, ...), kind=kOutput, calls=%fused_computation.8 | convolution fusion | flops 4318035968 | bytes 14680064 | tf_op jit(solution)/shard_map/dot_general | solution.py:64
  573.3 8.8 %add_convert_fusion.2 = bf16[512,2048]{1,0:T(8,128)(2,1)} fusion(f32[512,2048]{1,0:T(8,128)} %fusion.22, f32[512,2048]{1,0:T(8,128)} %fusion.124, bf16[2048,1024]{1,0:T(8,128)(2,1)} %get-tuple-element.77, bf16[512,2048]{1,0:T(8,128)(2,1)} %copy-done.34), kind=kOutput, calls=%fused_computation.30 | convolution fusion | flops 2150629376 | bytes 15728640 | tf_op jit(solution)/shard_map/dot_general | solution.py:58
  591.6 4.2 collective-permute-start.56
  595.9 7.2 fusion.172
  627.5 15.6 %collective-permute-done.61 = bf16[256,2048]{1,0:T(8,128)(2,1)S(1)} collective-permute-done((bf16[256,2048]{1,0:T(8,128)(2,1)}, bf16[256,2048]{1,0:T(8,128)(2,1)S(1)}, u32[]{:S(2)}, u32[]{:S(2)}) %collective-permute-start.61) | collective-permute-done | bytes 1048608 | tf_op jit(solution)/shard_map/ppermute | solution.py:121
  646.8 5.9 add_convert_fusion.1
  666.5 12.7 %collective-permute-done.67 = bf16[128,2048]{1,0:T(8,128)(2,1)} collective-permute-done((bf16[128,2048]{1,0:T(8,128)(2,1)}, bf16[128,2048]{1,0:T(8,128)(2,1)}, u32[]{:S(2)}, u32[]{:S(2)}) %collective-permute-start.67) | collective-permute-done | bytes 524320 | tf_op jit(solution)/shard_map/ppermute | solution.py:121
  697.6 6.8 collective-permute-start.87
  720.4 6.0 collective-permute-done.75
  736.4 6.8 convert_element_type.253
  743.4 18.6 %reduce-scatter.5.cloned.1.call-done = bf16[256,2048]{1,0:T(8,128)(2,1)} async-done(((bf16[1024,2048]{1,0:T(8,128)(2,1)}), bf16[256,2048]{1,0:T(8,128)(2,1)}) %reduce-scatter.5.cloned.1.call-update) | async-done | bytes 1048592 | tf_op jit(solution)/shard_map/reduce_scatter | solution.py:187
  (551 shorter events, 274.4 us)
Async XLA Ops:
  7.2 227.5 %all-gather.4.cloned.1.call-start = ((), (), s32[]{:S(2)}) async-start(), calls=%async_computation.4 | async-start | bytes 9437184 | tf_op jit(solution)/shard_map/all_gather | solution.py:159
  42.0 288.1 %all-gather.6.cloned.1.call-start = ((), (), s32[]{:S(2)}) async-start(), calls=%async_computation.5 | async-start | bytes 9437184 | tf_op jit(solution)/shard_map/all_gather | solution.py:159
  42.1 126.4 %collective-permute-start = (bf16[1024,2048]{1,0:T(8,128)(2,1)}, bf16[1024,2048]{1,0:T(8,128)(2,1)}, u32[]{:S(2)}, u32[]{:S(2)}) collective-permute-start(bf16[1024,2048]{1,0:T(8,128)(2,1)} %param.16), channel_id=1, source_target_pairs={{1,4},{3,6},{4,1},{6,3},{9,12},{11,14},{12,9},{14,11},{17,20},{19,... | collective-permute-start | bytes 12582920 | tf_op jit(solution)/shard_map/ppermute | solution.py:121
  45.6 69.5 %collective-permute-start.14 = (s32[2]{0:T(128)S(1)}, s32[2]{0:T(128)S(1)}, u32[]{:S(2)}, u32[]{:S(2)}) collective-permute-start(s32[2]{0:T(128)S(1)} %copy-done.88), channel_id=1, source_target_pairs={{0,1},{1,0},{2,3},{3,2},{4,5},{5,4},{6,7},{7,6},{8,9},{9,8},{10,11... | collective-permute-start | bytes 32 | tf_op jit(solution)/shard_map/ppermute | solution.py:121
  60.7 59.7 %collective-permute-start.2 = (bf16[256,1024]{1,0:T(8,128)(2,1)}, bf16[256,1024]{1,0:T(8,128)(2,1)}, u32[]{:S(2)}, u32[]{:S(2)}) collective-permute-start(bf16[256,1024]{1,0:T(8,128)(2,1)} %broadcast_select_fusion.14.refs_7_), channel_id=1, source_target_pairs={{0,8},{1,9},{2,10},{3,11},{4,12},{5,13},{6,14},{7,15},{8,16},{9,17... | collective-permute-start | bytes 1572872 | tf_op jit(solution)/shard_map/ppermute | solution.py:121
  60.7 71.7 %collective-permute-start.11 = (bf16[272,1024]{1,0:T(8,128)(2,1)}, bf16[272,1024]{1,0:T(8,128)(2,1)}, u32[]{:S(2)}, u32[]{:S(2)}) collective-permute-start(bf16[272,1024]{1,0:T(8,128)(2,1)} %collective-permute-done.9.refs_9_), channel_id=1, source_target_pairs={{0,8},{1,9},{2,10},{3,11},{4,12},{5,13},{6,14},{7,15},{8,16},{9,17... | collective-permute-start | bytes 1671176 | tf_op jit(solution)/shard_map/ppermute | solution.py:121
  63.8 88.2 %collective-permute-start.6 = (bf16[272,1024]{1,0:T(8,128)(2,1)S(1)}, bf16[272,1024]{1,0:T(8,128)(2,1)S(1)}, u32[]{:S(2)}, u32[]{:S(2)}) collective-permute-start(bf16[272,1024]{1,0:T(8,128)(2,1)S(1)} %broadcast_select_fusion.12.refs_7_), channel_id=1, source_target_pairs={{0,1},{1,0},{2,3},{3,2},{4,5},{5,4},{6,7},{7,6},{8,9},{9,8},{10,11... | collective-permute-start | bytes 1671176 | tf_op jit(solution)/shard_map/ppermute | solution.py:121
  117.2 37.5 %collective-permute-start.8 = (bf16[272,1024]{1,0:T(8,128)(2,1)}, bf16[272,1024]{1,0:T(8,128)(2,1)}, u32[]{:S(2)}, u32[]{:S(2)}) collective-permute-start(bf16[272,1024]{1,0:T(8,128)(2,1)} %copy-done.89), channel_id=1, source_target_pairs={{0,1},{1,0},{2,3},{3,2},{4,5},{5,4},{6,7},{7,6},{8,9},{9,8},{10,11... | collective-permute-start | bytes 1671176 | tf_op jit(solution)/shard_map/ppermute | solution.py:121
  120.4 36.5 %collective-permute-start.10 = (bf16[272,1024]{1,0:T(8,128)(2,1)}, bf16[272,1024]{1,0:T(8,128)(2,1)}, u32[]{:S(2)}, u32[]{:S(2)}) collective-permute-start(bf16[272,1024]{1,0:T(8,128)(2,1)} %collective-permute-done.9.refs_9_), channel_id=1, source_target_pairs={{0,1},{1,0},{2,3},{3,2},{4,5},{5,4},{6,7},{7,6},{8,9},{9,8},{10,11... | collective-permute-start | bytes 1671176 | tf_op jit(solution)/shard_map/ppermute | solution.py:121
  132.5 26.7 %collective-permute-start.12 = (bf16[272,1024]{1,0:T(8,128)(2,1)}, bf16[272,1024]{1,0:T(8,128)(2,1)}, u32[]{:S(2)}, u32[]{:S(2)}) collective-permute-start(bf16[272,1024]{1,0:T(8,128)(2,1)} %collective-permute-done.11.refs_10_), channel_id=1, source_target_pairs={{0,1},{1,0},{2,3},{3,2},{4,5},{5,4},{6,7},{7,6},{8,9},{9,8},{10,11... | collective-permute-start | bytes 1671176 | tf_op jit(solution)/shard_map/ppermute | solution.py:121
  154.6 35.1 %collective-permute-start.33 = (bf16[256,2048]{1,0:T(8,128)(2,1)S(1)}, bf16[256,2048]{1,0:T(8,128)(2,1)S(1)}, u32[]{:S(2)}, u32[]{:S(2)}) collective-permute-start(bf16[256,2048]{1,0:T(8,128)(2,1)S(1)} %constant_dynamic-update-slice_fusion.16), channel_id=1, source_target_pairs={{1,4},{3,6},{4,1},{6,3},{9,12},{11,14},{12,9},{14,11},{17,20},{19,... | collective-permute-start | bytes 3145736 | tf_op jit(solution)/shard_map/ppermute | solution.py:121
  156.9 32.8 %collective-permute-start.34 = (bf16[256,1024]{1,0:T(8,128)(2,1)S(1)}, bf16[256,1024]{1,0:T(8,128)(2,1)S(1)}, u32[]{:S(2)}, u32[]{:S(2)}) collective-permute-start(bf16[256,1024]{1,0:T(8,128)(2,1)S(1)} %bitcast.65), channel_id=1, source_target_pairs={{1,4},{3,6},{4,1},{6,3},{9,12},{11,14},{12,9},{14,11},{17,20},{19,... | collective-permute-start | bytes 1572872 | tf_op jit(solution)/shard_map/ppermute | solution.py:121
  190.8 171.0 %all-gather.8.cloned.1.call-start = ((), (), s32[]{:S(2)}) async-start(), calls=%async_computation.6 | async-start | bytes 4718592 | tf_op jit(solution)/shard_map/all_gather | solution.py:159
  190.9 55.5 %collective-permute-start.4 = (bf16[1024,2048]{1,0:T(8,128)(2,1)}, bf16[1024,2048]{1,0:T(8,128)(2,1)}, u32[]{:S(2)}, u32[]{:S(2)}) collective-permute-start(bf16[1024,2048]{1,0:T(8,128)(2,1)} %param.31), channel_id=1, source_target_pairs={{1,4},{3,6},{4,1},{6,3},{9,12},{11,14},{12,9},{14,11},{17,20},{19,... | collective-permute-start | bytes 12582920 | tf_op jit(solution)/shard_map/ppermute | solution.py:121
  193.5 21.9 %collective-permute-start.16 = (bf16[256,1024]{1,0:T(8,128)(2,1)}, bf16[256,1024]{1,0:T(8,128)(2,1)S(1)}, u32[]{:S(2)}, u32[]{:S(2)}) collective-permute-start(bf16[256,1024]{1,0:T(8,128)(2,1)} %collective-permute-done.3.refs_9_), channel_id=1, source_target_pairs={{0,8},{1,9},{2,10},{3,11},{4,12},{5,13},{6,14},{7,15},{8,16},{9,17... | collective-permute-start | bytes 1572872 | tf_op jit(solution)/shard_map/ppermute | solution.py:121
  193.5 26.8 %collective-permute-start.17 = (bf16[256,1024]{1,0:T(8,128)(2,1)}, bf16[256,1024]{1,0:T(8,128)(2,1)S(1)}, u32[]{:S(2)}, u32[]{:S(2)}) collective-permute-start(bf16[256,1024]{1,0:T(8,128)(2,1)} %broadcast_select_fusion.14.refs_7_), channel_id=1, source_target_pairs={{0,1},{1,0},{2,3},{3,2},{4,5},{5,4},{6,7},{7,6},{8,9},{9,8},{10,11... | collective-permute-start | bytes 1572872 | tf_op jit(solution)/shard_map/ppermute | solution.py:121
  195.5 24.8 %collective-permute-start.18 = (bf16[256,1024]{1,0:T(8,128)(2,1)}, bf16[256,1024]{1,0:T(8,128)(2,1)}, u32[]{:S(2)}, u32[]{:S(2)}) collective-permute-start(bf16[256,1024]{1,0:T(8,128)(2,1)} %collective-permute-done.2.refs_8_), channel_id=1, source_target_pairs={{0,1},{1,0},{2,3},{3,2},{4,5},{5,4},{6,7},{7,6},{8,9},{9,8},{10,11... | collective-permute-start | bytes 1572872 | tf_op jit(solution)/shard_map/ppermute | solution.py:121
  195.6 24.8 %collective-permute-start.19 = (bf16[256,1024]{1,0:T(8,128)(2,1)}, bf16[256,1024]{1,0:T(8,128)(2,1)}, u32[]{:S(2)}, u32[]{:S(2)}) collective-permute-start(bf16[256,1024]{1,0:T(8,128)(2,1)} %collective-permute-done.3.refs_9_), channel_id=1, source_target_pairs={{0,1},{1,0},{2,3},{3,2},{4,5},{5,4},{6,7},{7,6},{8,9},{9,8},{10,11... | collective-permute-start | bytes 1572872 | tf_op jit(solution)/shard_map/ppermute | solution.py:121
  218.7 363.4 %reduce-scatter.11.cloned.1.call-start = ((), (), s32[]{:S(2)}) async-start(), calls=%async_computation.10 | async-start | bytes 2621440 | tf_op jit(solution)/shard_map/reduce_scatter | solution.py:187
  251.3 23.8 %collective-permute-start.21 = (bf16[128,2048]{1,0:T(8,128)(2,1)S(1)}, bf16[128,2048]{1,0:T(8,128)(2,1)S(1)}, u32[]{:S(2)}, u32[]{:S(2)}) collective-permute-start(bf16[128,2048]{1,0:T(8,128)(2,1)S(1)} %get-tuple-element.232), channel_id=1, source_target_pairs={{0,2},{1,3},{2,0},{3,1},{4,6},{5,7},{6,4},{7,5},{8,10},{9,11},{10,... | collective-permute-start | bytes 1572872 | tf_op jit(solution)/shard_map/ppermute | solution.py:121
  251.8 24.9 %collective-permute-start.22 = (bf16[128,2048]{1,0:T(8,128)(2,1)S(1)}, bf16[128,2048]{1,0:T(8,128)(2,1)S(1)}, u32[]{:S(2)}, u32[]{:S(2)}) collective-permute-start(bf16[128,2048]{1,0:T(8,128)(2,1)S(1)} %get-tuple-element.235), channel_id=1, source_target_pairs={{0,4},{1,5},{2,6},{3,7},{4,0},{5,1},{6,2},{7,3},{8,12},{9,13},{10,... | collective-permute-start | bytes 1572872 | tf_op jit(solution)/shard_map/ppermute | solution.py:121
  295.5 22.8 %collective-permute-start.28 = (bf16[128,2048]{1,0:T(8,128)(2,1)S(1)}, bf16[128,2048]{1,0:T(8,128)(2,1)S(1)}, u32[]{:S(2)}, u32[]{:S(2)}) collective-permute-start(bf16[128,2048]{1,0:T(8,128)(2,1)S(1)} %get-tuple-element.248), channel_id=1, source_target_pairs={{0,4},{1,5},{2,6},{3,7},{4,0},{5,1},{6,2},{7,3},{8,12},{9,13},{10,... | collective-permute-start | bytes 1572872 | tf_op jit(solution)/shard_map/ppermute | solution.py:121
  296.6 22.6 %collective-permute-start.29 = (bf16[128,2048]{1,0:T(8,128)(2,1)S(1)}, bf16[128,2048]{1,0:T(8,128)(2,1)S(1)}, u32[]{:S(2)}, u32[]{:S(2)}) collective-permute-start(bf16[128,2048]{1,0:T(8,128)(2,1)S(1)} %get-tuple-element.250), channel_id=1, source_target_pairs={{0,2},{1,3},{2,0},{3,1},{4,6},{5,7},{6,4},{7,5},{8,10},{9,11},{10,... | collective-permute-start | bytes 1572872 | tf_op jit(solution)/shard_map/ppermute | solution.py:121
  307.1 21.4 %collective-permute-start.31 = (bf16[128,2048]{1,0:T(8,128)(2,1)S(1)}, bf16[128,2048]{1,0:T(8,128)(2,1)S(1)}, u32[]{:S(2)}, u32[]{:S(2)}) collective-permute-start(bf16[128,2048]{1,0:T(8,128)(2,1)S(1)} %collective-permute-done.27), channel_id=1, source_target_pairs={{0,2},{1,3},{2,0},{3,1},{4,6},{5,7},{6,4},{7,5},{8,10},{9,11},{10,... | collective-permute-start | bytes 1572872 | tf_op jit(solution)/shard_map/ppermute | solution.py:121
  388.3 24.6 %collective-permute-start.36 = (bf16[128,2048]{1,0:T(8,128)(2,1)S(1)}, bf16[128,2048]{1,0:T(8,128)(2,1)S(1)}, u32[]{:S(2)}, u32[]{:S(2)}) collective-permute-start(bf16[128,2048]{1,0:T(8,128)(2,1)S(1)} %get-tuple-element.228), channel_id=1, source_target_pairs={{0,2},{1,3},{2,0},{3,1},{4,6},{5,7},{6,4},{7,5},{8,10},{9,11},{10,... | collective-permute-start | bytes 1572872 | tf_op jit(solution)/shard_map/ppermute | solution.py:121
  389.7 23.7 %collective-permute-start.37 = (bf16[128,2048]{1,0:T(8,128)(2,1)S(1)}, bf16[128,2048]{1,0:T(8,128)(2,1)S(1)}, u32[]{:S(2)}, u32[]{:S(2)}) collective-permute-start(bf16[128,2048]{1,0:T(8,128)(2,1)S(1)} %get-tuple-element.231), channel_id=1, source_target_pairs={{0,4},{1,5},{2,6},{3,7},{4,0},{5,1},{6,2},{7,3},{8,12},{9,13},{10,... | collective-permute-start | bytes 1572872 | tf_op jit(solution)/shard_map/ppermute | solution.py:121
  402.5 21.4 %collective-permute-start.39 = (bf16[128,2048]{1,0:T(8,128)(2,1)S(1)}, bf16[128,2048]{1,0:T(8,128)(2,1)S(1)}, u32[]{:S(2)}, u32[]{:S(2)}) collective-permute-start(bf16[128,2048]{1,0:T(8,128)(2,1)S(1)} %get-tuple-element.172), channel_id=1, source_target_pairs={{0,4},{1,5},{2,6},{3,7},{4,0},{5,1},{6,2},{7,3},{8,12},{9,13},{10,... | collective-permute-start | bytes 1572872 | tf_op jit(solution)/shard_map/ppermute | solution.py:121
  434.7 297.6 %reduce-scatter.7.cloned.1.call-start = ((), (), s32[]{:S(2)}) async-start(), calls=%async_computation.8 | async-start | bytes 5242880 | tf_op jit(solution)/shard_map/reduce_scatter | solution.py:187
  434.9 22.6 %collective-permute-start.43 = (bf16[128,2048]{1,0:T(8,128)(2,1)}, bf16[128,2048]{1,0:T(8,128)(2,1)S(1)}, u32[]{:S(2)}, u32[]{:S(2)}) collective-permute-start(bf16[128,2048]{1,0:T(8,128)(2,1)} %get-tuple-element.245), channel_id=1, source_target_pairs={{0,4},{1,5},{2,6},{3,7},{4,0},{5,1},{6,2},{7,3},{8,12},{9,13},{10,... | collective-permute-start | bytes 1572872 | tf_op jit(solution)/shard_map/ppermute | solution.py:121
  436.1 22.3 %collective-permute-start.44 = (bf16[128,2048]{1,0:T(8,128)(2,1)}, bf16[128,2048]{1,0:T(8,128)(2,1)S(1)}, u32[]{:S(2)}, u32[]{:S(2)}) collective-permute-start(bf16[128,2048]{1,0:T(8,128)(2,1)} %get-tuple-element.247), channel_id=1, source_target_pairs={{0,2},{1,3},{2,0},{3,1},{4,6},{5,7},{6,4},{7,5},{8,10},{9,11},{10,... | collective-permute-start | bytes 1572872 | tf_op jit(solution)/shard_map/ppermute | solution.py:121
  498.2 65.7 %collective-permute-start.79 = (bf16[1024,2048]{1,0:T(8,128)(2,1)}, bf16[1024,2048]{1,0:T(8,128)(2,1)}, u32[]{:S(2)}, u32[]{:S(2)}) collective-permute-start(bf16[1024,2048]{1,0:T(8,128)(2,1)} %convolution_convert_fusion), channel_id=1, source_target_pairs={{0,1},{1,0},{2,3},{3,2},{4,5},{5,4},{6,7},{7,6},{8,9},{9,8},{10,11... | collective-permute-start | bytes 12582920 | tf_op jit(solution)/shard_map/ppermute | solution.py:121
  502.2 51.0 %collective-permute-start.52 = (bf16[128,2048]{1,0:T(8,128)(2,1)}, bf16[128,2048]{1,0:T(8,128)(2,1)}, u32[]{:S(2)}, u32[]{:S(2)}) collective-permute-start(bf16[128,2048]{1,0:T(8,128)(2,1)} %get-tuple-element.216), channel_id=1, source_target_pairs={{0,2},{1,3},{2,0},{3,1},{4,6},{5,7},{6,4},{7,5},{8,10},{9,11},{10,... | collective-permute-start | bytes 1572872 | tf_op jit(solution)/shard_map/ppermute | solution.py:121
  503.6 49.7 %collective-permute-start.54 = (bf16[128,2048]{1,0:T(8,128)(2,1)}, bf16[128,2048]{1,0:T(8,128)(2,1)}, u32[]{:S(2)}, u32[]{:S(2)}) collective-permute-start(bf16[128,2048]{1,0:T(8,128)(2,1)} %get-tuple-element.217), channel_id=1, source_target_pairs={{0,4},{1,5},{2,6},{3,7},{4,0},{5,1},{6,2},{7,3},{8,12},{9,13},{10,... | collective-permute-start | bytes 1572872 | tf_op jit(solution)/shard_map/ppermute | solution.py:121
  506.0 76.1 %collective-permute-start.50 = (bf16[128,2048]{1,0:T(8,128)(2,1)}, bf16[128,2048]{1,0:T(8,128)(2,1)S(1)}, u32[]{:S(2)}, u32[]{:S(2)}) collective-permute-start(bf16[128,2048]{1,0:T(8,128)(2,1)} %get-tuple-element.219), channel_id=1, source_target_pairs={{0,2},{1,3},{2,0},{3,1},{4,6},{5,7},{6,4},{7,5},{8,10},{9,11},{10,... | collective-permute-start | bytes 1572872 | tf_op jit(solution)/shard_map/ppermute | solution.py:121
  509.1 74.7 %collective-permute-start.51 = (bf16[128,2048]{1,0:T(8,128)(2,1)}, bf16[128,2048]{1,0:T(8,128)(2,1)S(1)}, u32[]{:S(2)}, u32[]{:S(2)}) collective-permute-start(bf16[128,2048]{1,0:T(8,128)(2,1)} %get-tuple-element.218), channel_id=1, source_target_pairs={{0,4},{1,5},{2,6},{3,7},{4,0},{5,1},{6,2},{7,3},{8,12},{9,13},{10,... | collective-permute-start | bytes 1572872 | tf_op jit(solution)/shard_map/ppermute | solution.py:121
  514.9 219.0 %reduce-scatter.9.cloned.1.call-start = ((), (), s32[]{:S(2)}) async-start(), calls=%async_computation.9 | async-start | bytes 5242880 | tf_op jit(solution)/shard_map/reduce_scatter | solution.py:187
  553.2 89.9 %collective-permute-start.63 = (bf16[1024,2048]{1,0:T(8,128)(2,1)}, bf16[1024,2048]{1,0:T(8,128)(2,1)}, u32[]{:S(2)}, u32[]{:S(2)}) collective-permute-start(bf16[1024,2048]{1,0:T(8,128)(2,1)} %convolution_convert_fusion.1), channel_id=1, source_target_pairs={{0,1},{1,0},{2,3},{3,2},{4,5},{5,4},{6,7},{7,6},{8,9},{9,8},{10,11... | collective-permute-start | bytes 12582920 | tf_op jit(solution)/shard_map/ppermute | solution.py:121
  557.0 26.8 %collective-permute-start.53 = (bf16[128,2048]{1,0:T(8,128)(2,1)}, bf16[128,2048]{1,0:T(8,128)(2,1)}, u32[]{:S(2)}, u32[]{:S(2)}) collective-permute-start(bf16[128,2048]{1,0:T(8,128)(2,1)} %get-tuple-element.152), channel_id=1, source_target_pairs={{0,4},{1,5},{2,6},{3,7},{4,0},{5,1},{6,2},{7,3},{8,12},{9,13},{10,... | collective-permute-start | bytes 1572872 | tf_op jit(solution)/shard_map/ppermute | solution.py:121
  582.2 23.8 %collective-permute-start.81 = (bf16[256,1024]{1,0:T(8,128)(2,1)}, bf16[256,1024]{1,0:T(8,128)(2,1)}, u32[]{:S(2)}, u32[]{:S(2)}) collective-permute-start(bf16[256,1024]{1,0:T(8,128)(2,1)} %reduce-scatter.11.cloned.1.call-done), channel_id=1, source_target_pairs={{1,4},{3,6},{4,1},{6,3},{9,12},{11,14},{12,9},{14,11},{17,20},{19,... | collective-permute-start | bytes 1572872 | tf_op jit(solution)/shard_map/ppermute | solution.py:121
  603.1 158.9 %reduce-scatter.5.cloned.1.call-start = ((), (), s32[]{:S(2)}) async-start(), calls=%async_computation.7 | async-start | bytes 5242880 | tf_op jit(solution)/shard_map/reduce_scatter | solution.py:187
  606.0 55.4 %collective-permute-start.66 = (bf16[128,2048]{1,0:T(8,128)(2,1)}, bf16[128,2048]{1,0:T(8,128)(2,1)S(1)}, u32[]{:S(2)}, u32[]{:S(2)}) collective-permute-start(bf16[128,2048]{1,0:T(8,128)(2,1)} %get-tuple-element.206), channel_id=1, source_target_pairs={{0,2},{1,3},{2,0},{3,1},{4,6},{5,7},{6,4},{7,5},{8,10},{9,11},{10,... | collective-permute-start | bytes 1572872 | tf_op jit(solution)/shard_map/ppermute | solution.py:121
  608.1 53.4 %collective-permute-start.68 = (bf16[128,2048]{1,0:T(8,128)(2,1)S(1)}, bf16[128,2048]{1,0:T(8,128)(2,1)S(1)}, u32[]{:S(2)}, u32[]{:S(2)}) collective-permute-start(bf16[128,2048]{1,0:T(8,128)(2,1)S(1)} %copy-done.46), channel_id=1, source_target_pairs={{0,4},{1,5},{2,6},{3,7},{4,0},{5,1},{6,2},{7,3},{8,12},{9,13},{10,... | collective-permute-start | bytes 1572872 | tf_op jit(solution)/shard_map/ppermute | solution.py:121
  617.2 49.2 %collective-permute-start.64 = (bf16[128,2048]{1,0:T(8,128)(2,1)}, bf16[128,2048]{1,0:T(8,128)(2,1)}, u32[]{:S(2)}, u32[]{:S(2)}) collective-permute-start(bf16[128,2048]{1,0:T(8,128)(2,1)} %get-tuple-element.204), channel_id=1, source_target_pairs={{0,2},{1,3},{2,0},{3,1},{4,6},{5,7},{6,4},{7,5},{8,10},{9,11},{10,... | collective-permute-start | bytes 1572872 | tf_op jit(solution)/shard_map/ppermute | solution.py:121
  620.7 22.4 %collective-permute-start.61 = (bf16[256,2048]{1,0:T(8,128)(2,1)}, bf16[256,2048]{1,0:T(8,128)(2,1)S(1)}, u32[]{:S(2)}, u32[]{:S(2)}) collective-permute-start(bf16[256,2048]{1,0:T(8,128)(2,1)} %collective-permute-done.57), channel_id=1, source_target_pairs={{0,2},{2,0},{5,7},{7,5},{8,10},{10,8},{13,15},{15,13},{16,18},{18,... | collective-permute-start | bytes 3145736 | tf_op jit(solution)/shard_map/ppermute | solution.py:121
  643.1 23.4 %collective-permute-start.65 = (bf16[128,2048]{1,0:T(8,128)(2,1)}, bf16[128,2048]{1,0:T(8,128)(2,1)}, u32[]{:S(2)}, u32[]{:S(2)}) collective-permute-start(bf16[128,2048]{1,0:T(8,128)(2,1)} %get-tuple-element.207), channel_id=1, source_target_pairs={{0,4},{1,5},{2,6},{3,7},{4,0},{5,1},{6,2},{7,3},{8,12},{9,13},{10,... | collective-permute-start | bytes 1572872 | tf_op jit(solution)/shard_map/ppermute | solution.py:121
  643.1 23.3 %collective-permute-start.62 = (bf16[256,2048]{1,0:T(8,128)(2,1)S(1)}, bf16[256,2048]{1,0:T(8,128)(2,1)}, u32[]{:S(2)}, u32[]{:S(2)}) collective-permute-start(bf16[256,2048]{1,0:T(8,128)(2,1)S(1)} %collective-permute-done.61), channel_id=1, source_target_pairs={{0,1},{2,3},{5,4},{7,6},{8,9},{10,11},{13,12},{15,14},{16,17},{18,... | collective-permute-start | bytes 3145736 | tf_op jit(solution)/shard_map/ppermute | solution.py:121
  692.3 22.3 %collective-permute-start.73 = (bf16[256,2048]{1,0:T(8,128)(2,1)S(1)}, bf16[256,2048]{1,0:T(8,128)(2,1)S(1)}, u32[]{:S(2)}, u32[]{:S(2)}) collective-permute-start(bf16[256,2048]{1,0:T(8,128)(2,1)S(1)} %fusion.38), channel_id=1, source_target_pairs={{0,2},{2,0},{5,7},{7,5},{8,10},{10,8},{13,15},{15,13},{16,18},{18,... | collective-permute-start | bytes 3145736 | tf_op jit(solution)/shard_map/ppermute | solution.py:121
  734.0 32.2 %collective-permute-start.80 = (bf16[256,2048]{1,0:T(8,128)(2,1)}, bf16[256,2048]{1,0:T(8,128)(2,1)}, u32[]{:S(2)}, u32[]{:S(2)}) collective-permute-start(bf16[256,2048]{1,0:T(8,128)(2,1)} %reduce-scatter.9.cloned.1.call-done), channel_id=1, source_target_pairs={{1,4},{3,6},{4,1},{6,3},{9,12},{11,14},{12,9},{14,11},{17,20},{19,... | collective-permute-start | bytes 3145736 | tf_op jit(solution)/shard_map/ppermute | solution.py:121
  (151 other events, 1921.7 us)
Sparse Core Ops, SparseCore 0:
  42.2 115.0 all-gather.3
  191.0 88.8 all-gather.5
  281.5 44.6 all-gather.7
  434.8 45.4 reduce-scatter.10
  515.0 79.5 reduce-scatter.6
  603.2 78.8 reduce-scatter.8
  684.4 77.5 reduce-scatter.4

commit v4 on v3

--- a/solution.py
+++ b/solution.py
@@ -637,9 +637,9 @@
     second_near, second_far = core_halves(place, second_in)
     away = dot_nt(far_rows(place, grad_ff), full_ff).astype(jnp.bfloat16)
     got = send_far(place, away)
-    here = dot_nt(near_rows(place, after(grad_ff, away)), full_ff)
-    ff_got, _ = core_far(place, second_far, after(grad_ff, here))
-    ff_sum = core_near(second_near, grad_ff, ff_got)
+    ff_got, ff_far = core_far(place, second_far, after(grad_ff, away))
+    here = dot_nt(near_rows(place, after(grad_ff, ff_far)), full_ff)
+    ff_sum = core_near(second_near, after(grad_ff, here), ff_got)
     share_ff = queue_scatter(place, ff_sum)
     grad_second = sum_near(place, here, got)
     grad_middle = my_rows(place, grad_feed).astype(jnp.float32) + norm_back(
@@ -649,14 +649,14 @@
     e_got = send_far(place, e_away)
     branch_near, branch_far = core_halves(place, grad_branch)
     first_near, first_far = core_halves(place, first_in)
-    grad_gated = dot_nn(grad_branch, full_out)
+    out_got, out_far = core_far(place, branch_far, gated)
+    grad_gated = dot_nn(after(grad_branch, out_far), full_out)
     swish_slope = sigmoid_gate * (1.0 + gate * (1.0 - sigmoid_gate))
     grad_gate_in = (grad_gated * grouped_flat * swish_slope).astype(jnp.bfloat16)
     grad_grouped = grad_gated * swish
     gate_got, gate_far = core_far(place, first_far, grad_gate_in)
-    out_got, out_far = core_far(place, branch_far, after(gated, gate_far))
-    gate_sum = core_near(first_near, after(grad_gate_in, out_far), gate_got)
-    out_sum = core_near(branch_near, after(gated, gate_sum), out_got)
+    out_sum = core_near(branch_near, after(gated, gate_far), out_got)
+    gate_sum = core_near(first_near, after(grad_gate_in, out_sum), gate_got)
     og_sum = jnp.concatenate([out_sum, gate_sum], axis=1)
     grad_grouped, og_sum, e_near = together(grad_grouped, og_sum, near_rows(place, hidden))
     share_og = queue_scatter(place, og_sum)

time: 795 us -> 792 us (level)
  the two profiles are of different devices: /device:TPU:0 before, /device:TPU:1 now
where the time goes in v4:
time: 792 us; the launch traced here: 786 us
  waiting for transfers between devices  272 us (34%)
  matrix products  154 us (19%)
  starting transfers between devices  141 us (18%)
  local copies, waits for them, and re-layouts  93.5 us (12%)
  other arithmetic  69.9 us (9%)
  Pallas kernels  39.3 us (5%)
  between operations  16.6 us (2%)
    ppermute x89, waiting for transfers between devices, send(): return lax.ppermute(value, BOTH, pairs)  252 us
    ppermute x89, starting transfers between devices, send(): return lax.ppermute(value, BOTH, pairs)  140 us
    dot_general x12, matrix products, dot_nt(): lax.dot_general(left, right, (((1,), (1,)), ((), ())), preferred_element_...  59.6 us
    dot_general x10, matrix products, dot_tn(): lax.dot_general(left, right, (((0,), (0,)), ((), ())), preferred_element_...  47.8 us
    dot_general x4, matrix products, dot_nn(): lax.dot_general(left, right, (((1,), (0,)), ((), ())), preferred_element_...  46.2 us
    dynamic_update_slice x30, local copies, waits for them, and re-layouts, assemble(): whole = lax.dynamic_update_slice_in_dim(whole, rows, start, axis=0)  27.1 us
    pallas_call x2, Pallas kernels, retention_forward(): pl.pallas_call(functools.partial(forward_kernel, head, place.na, len(held...  26.8 us
    reduce_scatter x4, waiting for transfers between devices, queue_scatter(): lax.psum_scatter(value, 'dp', scatter_dimension=0, tiled=True, axis_index...  19.3 us
  transfers between devices with their start and end apart: 96, of which 36 were waited for; matrix products, arithmetic and copies ran while one was open for 32% of the time, Pallas kernels for 5%

profile of v4, /device:TPU:1, one launch (start us, length us, event | category | flops | bytes accessed | tf_op | source)
XLA Modules:
  0.0 785.6 jit_solution(16526909317320756784)
XLA Ops:
  10.3 4.5 collective-permute-start.5
  16.1 6.2 collective-permute-done.5
  28.8 8.8 %collective-permute-done.7.refs_8_ = bf16[272,1024]{1,0:T(8,128)(2,1)S(1)} collective-permute-done((bf16[272,1024]{1,0:T(8,128)(2,1)S(1)}, bf16[272,1024]{1,0:T(8,128)(2,1)S(1)}, u32[]{:S(2)}, u32[]{:S(2)}) %collective-permute-start.7) | collective-permute-done | bytes 557088 | tf_op jit(solution)/shard_map/ppermute | solution.py:121
  41.3 6.6 collective-permute-done.9.refs_9_
  49.3 7.8 collective-permute-start
  59.3 50.2 %collective-permute-done.1 = bf16[256,1024]{1,0:T(8,128)(2,1)S(1)} collective-permute-done((bf16[256,1024]{1,0:T(8,128)(2,1)S(1)}, bf16[256,1024]{1,0:T(8,128)(2,1)S(1)}, u32[]{:S(2)}, u32[]{:S(2)}) %collective-permute-start.1) | collective-permute-done | bytes 524320 | tf_op jit(solution)/shard_map/ppermute | solution.py:121
  119.9 12.1 %collective-permute-done.2.refs_8_ = bf16[256,1024]{1,0:T(8,128)(2,1)} collective-permute-done((bf16[256,1024]{1,0:T(8,128)(2,1)}, bf16[256,1024]{1,0:T(8,128)(2,1)}, u32[]{:S(2)}, u32[]{:S(2)}) %collective-permute-start.2) | collective-permute-done | bytes 524320 | tf_op jit(solution)/shard_map/ppermute | solution.py:121
  132.0 17.9 %collective-permute-done.11.refs_10_ = bf16[272,1024]{1,0:T(8,128)(2,1)} collective-permute-done((bf16[272,1024]{1,0:T(8,128)(2,1)}, bf16[272,1024]{1,0:T(8,128)(2,1)}, u32[]{:S(2)}, u32[]{:S(2)}) %collective-permute-start.11) | collective-permute-done | bytes 557088 | tf_op jit(solution)/shard_map/ppermute | solution.py:121
  175.4 13.3 %shard_map.263 = (bf16[2048,1024]{1,0:T(8,128)(2,1)}, bf16[1024,2048]{1,0:T(8,128)(2,1)}, f32[1024,1024]{1,0:T(8,128)}, f32[2,1024,1]{2,1,0:T(8,128)}) custom-call(f32[2]{0:T(128)} %negate_log-plus-one_fusion.refs_0_.log_gamma, s32[1024,1]{1,0:T(8,128)} %copy.43.refs_1_.row_segment, s32[1,1024]{1,0:T(1,128)} %bitcast.59, ...), custom_call_target="tpu_custom_call" | custom-call | flops 5905580032 | bytes 20971520 | tf_op jit(solution)/shard_map/pallas_call | solution.py:378
  189.8 5.0 collective-permute-start.4
  195.6 21.7 %collective-permute-done.16.refs_10_ = bf16[256,1024]{1,0:T(8,128)(2,1)S(1)} collective-permute-done((bf16[256,1024]{1,0:T(8,128)(2,1)}, bf16[256,1024]{1,0:T(8,128)(2,1)S(1)}, u32[]{:S(2)}, u32[]{:S(2)}) %collective-permute-start.16) | collective-permute-done | bytes 524320 | tf_op jit(solution)/shard_map/ppermute | solution.py:121
  220.8 13.5 %shard_map.264 = (bf16[2048,1024]{1,0:T(8,128)(2,1)}, bf16[1024,2048]{1,0:T(8,128)(2,1)}, f32[1024,1024]{1,0:T(8,128)}, f32[2,1024,1]{2,1,0:T(8,128)}) custom-call(f32[2]{0:T(128)} %negate_log-plus-one_fusion.refs_0_.log_gamma, s32[1024,1]{1,0:T(8,128)} %copy.43.refs_1_.row_segment, ...), custom_call_target="tpu_custom_call", output_to_operand_aliasing={{1}: (15, {}), {2}: (16, {}), {3}: (17, {})} | custom-call | flops 5905580032 | bytes 20971520 | tf_op jit(solution)/shard_map/pallas_call | solution.py:378
  234.4 11.6 %multiply_convert_fusion.2 = (bf16[1024,1024]{1,0:T(8,128)(2,1)S(1)}, f32[1024,1024]{1,0:T(8,128)}) fusion(f32[1024,1024]{1,0:T(8,128)} %get-tuple-element.58.normed, bf16[1024,2048]{1,0:T(8,128)(2,1)} %fusion.5.refs_6_, bf16[2048,2048]{1,0:T(8,128)(2,1)} %all-gather.4.cloned.1.call-done), kind=kOutput, calls=%fused_computation.37 | convolution fusion | flops 4301258752 | bytes 18874368 | tf_op jit(solution)/shard_map/dot_general | solution.py:52
  254.2 7.8 collective-permute-done.23
  267.4 5.8 collective-permute-done.21
  274.2 11.1 %collective-permute-done.24 = bf16[128,2048]{1,0:T(8,128)(2,1)S(1)} collective-permute-done((bf16[128,2048]{1,0:T(8,128)(2,1)S(1)}, bf16[128,2048]{1,0:T(8,128)(2,1)S(1)}, u32[]{:S(2)}, u32[]{:S(2)}) %collective-permute-start.24) | collective-permute-done | bytes 524320 | tf_op jit(solution)/shard_map/ppermute | solution.py:121
  296.4 6.4 collective-permute-done.27
  305.3 8.7 %collective-permute-done.28 = bf16[128,2048]{1,0:T(8,128)(2,1)S(1)} collective-permute-done((bf16[128,2048]{1,0:T(8,128)(2,1)S(1)}, bf16[128,2048]{1,0:T(8,128)(2,1)S(1)}, u32[]{:S(2)}, u32[]{:S(2)}) %collective-permute-start.28) | collective-permute-done | bytes 524320 | tf_op jit(solution)/shard_map/ppermute | solution.py:121
  316.7 9.5 %collective-permute-done.31 = bf16[128,2048]{1,0:T(8,128)(2,1)S(1)} collective-permute-done((bf16[128,2048]{1,0:T(8,128)(2,1)S(1)}, bf16[128,2048]{1,0:T(8,128)(2,1)S(1)}, u32[]{:S(2)}, u32[]{:S(2)}) %collective-permute-start.31) | collective-permute-done | bytes 524320 | tf_op jit(solution)/shard_map/ppermute | solution.py:121
  327.9 12.5 %fusion.221 = f32[1024,2048]{1,0:T(8,128)S(1)} fusion(bf16[1024,2048]{1,0:T(8,128)(2,1)} %constant_dynamic-update-slice_fusion.8, bf16[2048,2048]{1,0:T(8,128)(2,1)} %all-gather.6.cloned.1.call-done), kind=kOutput, calls=%fused_computation.433 | convolution fusion | flops 8589934592 | bytes 20971520 | tf_op jit(solution)/shard_map/dot_general | solution.py:52
  348.8 4.3 constant_dynamic-slice_fusion.7
  356.7 11.3 %fusion.11 = (bf16[1024,1024]{1,0:T(8,128)(2,1)S(1)}, bf16[1024,1024]{1,0:T(8,128)(2,1)S(1)}) fusion(f32[1024,2048]{1,0:T(8,128)} %copy-done.20, bf16[1024,2048]{1,0:T(8,128)(2,1)} %copy-done.9, bf16[2048,1024]{1,0:T(8,128)(2,1)} %all-gather.8.cloned.1.call-done), kind=kOutput, calls=%fused_computation.25 | convolution fusion | flops 4309647360 | bytes 20971520 | tf_op jit(solution)/shard_map/dot_general | solution.py:52
  368.7 11.3 %convolution_convert_fusion.3 = bf16[512,2048]{1,0:T(8,128)(2,1)S(1)} fusion(bf16[2048,2048]{1,0:T(8,128)(2,1)} %all-gather.6.cloned.1.call-done, bf16[128,2048]{1,0:T(8,128)(2,1)S(1)} %get-tuple-element.183, bf16[128,2048]{1,0:T(8,128)(2,1)S(1)} %get-tuple-element.182, bf16[128,2048]{1,0:T(8,128)(2,1)S(1)} %get-tuple-element.181, ...), kind=kOutput, calls=%fused_computation.61 | convolution fusion | flops 4304404480 | bytes 12582912 | tf_op jit(solution)/shard_map/dot_general | solution.py:58
  381.9 6.5 convolution_convert_fusion.1
  391.7 7.3 fusion.77
  405.0 4.5 constant_dynamic-slice_fusion.35
  413.4 11.3 %collective-permute-done.39 = bf16[128,2048]{1,0:T(8,128)(2,1)} collective-permute-done((bf16[128,2048]{1,0:T(8,128)(2,1)}, bf16[128,2048]{1,0:T(8,128)(2,1)}, u32[]{:S(2)}, u32[]{:S(2)}) %collective-permute-start.39) | collective-permute-done | bytes 524320 | tf_op jit(solution)/shard_map/ppermute | solution.py:121
  437.1 8.7 %collective-permute-done.42 = bf16[128,2048]{1,0:T(8,128)(2,1)} collective-permute-done((bf16[128,2048]{1,0:T(8,128)(2,1)}, bf16[128,2048]{1,0:T(8,128)(2,1)}, u32[]{:S(2)}, u32[]{:S(2)}) %collective-permute-start.42) | collective-permute-done | bytes 524320 | tf_op jit(solution)/shard_map/ppermute | solution.py:121
  449.3 7.8 collective-permute-done.43
  460.6 7.8 collective-permute-done.46
  479.1 10.8 %multiply_convert_fusion = (bf16[1024,1024]{1,0:T(8,128)(2,1)S(1)}, f32[1024,1024]{1,0:T(8,128)}) fusion(f32[1024,1024]{1,0:T(8,128)} %get-tuple-element.273, f32[1024,1024]{1,0:T(8,128)S(1)} %copy-done.27, bf16[1024,2048]{1,0:T(8,128)(2,1)} %constant_dynamic-update-slice_fusion, bf16[2048,2048]{1,0:T(8,128)(2,1)S(1)} %bitcast.89), kind=kOutput, calls=%fused_computation.33 | convolution fusion | flops 4307550208 | bytes 23068672 | tf_op jit(solution)/shard_map/dot_general | solution.py:52
  509.9 7.0 fusion.22
  517.0 6.7 fusion.20
  523.8 12.5 %shard_map.265 = bf16[1024,2048]{1,0:T(8,128)(2,1)} custom-call(f32[2]{0:T(128)S(1)} %copy-done.7, s32[1024,1]{1,0:T(8,128)S(1)} %copy-done.1, s32[1,1024]{1,0:T(1,128)S(1)} %bitcast.61, f32[1024,128]{1,0:T(8,128)S(1)} %copy-done.3, f32[1024,128]{1,0:T(8,128)S(1)} %copy-done.2, f32[1024,128]{1,0:T(8,128)S(1)} %copy-done, ...), custom_call_target="tpu_custom_call" | custom-call | flops 7516192768 | bytes 16777216 | tf_op jit(solution)/shard_map/pallas_call | solution.py:480
  536.4 8.8 %convolution_convert_fusion = bf16[1024,2048]{1,0:T(8,128)(2,1)} fusion(bf16[1024,2048]{1,0:T(8,128)(2,1)} %shard_map.265, bf16[1024,256]{1,0:T(8,128)(2,1)S(1)} %copy-done.53, bf16[1024,256]{1,0:T(8,128)(2,1)S(1)} %copy-done.55, bf16[1024,256]{1,0:T(8,128)(2,1)S(1)} %copy-done.57, bf16[1024,256]{1,0:T(8,128)(2,1)S(1)} %copy-done.59), kind=kOutput, calls=%fused_computation.42 | convolution fusion | flops 4305453056 | bytes 10485760 | tf_op jit(solution)/shard_map/dot_general | solution.py:64
  554.9 4.4 fusion.124
  560.5 8.2 %add_convert_fusion = bf16[1024,2048]{1,0:T(8,128)(2,1)} fusion(bf16[1024,2048]{1,0:T(8,128)(2,1)} %collective-permute-done.79, bf16[1024,2048]{1,0:T(8,128)(2,1)S(1)} %copy-done.17, bf16[1024,256]{1,0:T(8,128)(2,1)S(1)} %copy-done.41, bf16[1024,256]{1,0:T(8,128)(2,1)S(1)} %copy-done.42, bf16[1024,256]{1,0:T(8,128)(2,1)S(1)} %copy-done.43, ...), kind=kOutput, calls=%fused_computation.8 | convolution fusion | flops 4309647360 | bytes 14680064 | tf_op jit(solution)/shard_map/dot_general | solution.py:64
  568.6 8.6 %add_convert_fusion.2 = bf16[512,2048]{1,0:T(8,128)(2,1)} fusion(f32[512,2048]{1,0:T(8,128)} %fusion.22, f32[512,2048]{1,0:T(8,128)} %fusion.124, bf16[2048,1024]{1,0:T(8,128)(2,1)} %get-tuple-element.79, bf16[512,2048]{1,0:T(8,128)(2,1)} %copy-done.31), kind=kOutput, calls=%fused_computation.30 | convolution fusion | flops 2150629376 | bytes 15728640 | tf_op jit(solution)/shard_map/dot_general | solution.py:58
  577.3 4.1 collective-permute-start.81
  590.2 7.2 fusion.172
  618.7 20.9 %collective-permute-start.65 = (bf16[128,2048]{1,0:T(8,128)(2,1)}, bf16[128,2048]{1,0:T(8,128)(2,1)}, u32[]{:S(2)}, u32[]{:S(2)}) collective-permute-start(bf16[128,2048]{1,0:T(8,128)(2,1)} %get-tuple-element.209), channel_id=1, source_target_pairs={{0,4},{1,5},{2,6},{3,7},{4,0},{5,1},{6,2},{7,3},{8,12},{9,13},{10,... | collective-permute-start | bytes 1572872 | tf_op jit(solution)/shard_map/ppermute | solution.py:121
  641.1 5.9 add_convert_fusion.1
  664.5 9.5 %collective-permute-done.67 = bf16[128,2048]{1,0:T(8,128)(2,1)} collective-permute-done((bf16[128,2048]{1,0:T(8,128)(2,1)}, bf16[128,2048]{1,0:T(8,128)(2,1)}, u32[]{:S(2)}, u32[]{:S(2)}) %collective-permute-start.67) | collective-permute-done | bytes 524320 | tf_op jit(solution)/shard_map/ppermute | solution.py:121
  693.2 5.7 collective-permute-start.87
  720.6 5.6 collective-permute-done.76
  731.1 6.8 convert_element_type.254
  738.0 19.3 %reduce-scatter.5.cloned.1.call-done = bf16[256,2048]{1,0:T(8,128)(2,1)} async-done(((bf16[1024,2048]{1,0:T(8,128)(2,1)}), bf16[256,2048]{1,0:T(8,128)(2,1)}) %reduce-scatter.5.cloned.1.call-update) | async-done | bytes 1048592 | tf_op jit(solution)/shard_map/reduce_scatter | solution.py:187
  766.6 7.4 collective-permute-done.77
  (534 shorter events, 287.8 us)
Async XLA Ops:
  7.2 227.2 %all-gather.4.cloned.1.call-start = ((), (), s32[]{:S(2)}) async-start(), calls=%async_computation.4 | async-start | bytes 9437184 | tf_op jit(solution)/shard_map/all_gather | solution.py:159
  49.3 278.7 %all-gather.6.cloned.1.call-start = ((), (), s32[]{:S(2)}) async-start(), calls=%async_computation.5 | async-start | bytes 9437184 | tf_op jit(solution)/shard_map/all_gather | solution.py:159
  49.3 118.1 %collective-permute-start = (bf16[1024,2048]{1,0:T(8,128)(2,1)}, bf16[1024,2048]{1,0:T(8,128)(2,1)}, u32[]{:S(2)}, u32[]{:S(2)}) collective-permute-start(bf16[1024,2048]{1,0:T(8,128)(2,1)} %param.16), channel_id=1, source_target_pairs={{1,4},{3,6},{4,1},{6,3},{9,12},{11,14},{12,9},{14,11},{17,20},{19,... | collective-permute-start | bytes 12582920 | tf_op jit(solution)/shard_map/ppermute | solution.py:121
  57.2 52.3 %collective-permute-start.1 = (bf16[256,1024]{1,0:T(8,128)(2,1)S(1)}, bf16[256,1024]{1,0:T(8,128)(2,1)S(1)}, u32[]{:S(2)}, u32[]{:S(2)}) collective-permute-start(bf16[256,1024]{1,0:T(8,128)(2,1)S(1)} %pad_maximum_fusion.11), channel_id=1, source_target_pairs={{1,4},{3,6},{4,1},{6,3},{9,12},{11,14},{12,9},{14,11},{17,20},{19,... | collective-permute-start | bytes 1572872 | tf_op jit(solution)/shard_map/ppermute | solution.py:121
  59.1 55.5 %collective-permute-start.14 = (s32[2]{0:T(128)S(1)}, s32[2]{0:T(128)S(1)}, u32[]{:S(2)}, u32[]{:S(2)}) collective-permute-start(s32[2]{0:T(128)S(1)} %copy-done.78), channel_id=1, source_target_pairs={{0,1},{1,0},{2,3},{3,2},{4,5},{5,4},{6,7},{7,6},{8,9},{9,8},{10,11... | collective-permute-start | bytes 32 | tf_op jit(solution)/shard_map/ppermute | solution.py:121
  110.5 39.4 %collective-permute-start.11 = (bf16[272,1024]{1,0:T(8,128)(2,1)}, bf16[272,1024]{1,0:T(8,128)(2,1)}, u32[]{:S(2)}, u32[]{:S(2)}) collective-permute-start(bf16[272,1024]{1,0:T(8,128)(2,1)} %collective-permute-done.9.refs_9_), channel_id=1, source_target_pairs={{0,8},{1,9},{2,10},{3,11},{4,12},{5,13},{6,14},{7,15},{8,16},{9,17... | collective-permute-start | bytes 1671176 | tf_op jit(solution)/shard_map/ppermute | solution.py:121
  113.6 37.9 %collective-permute-start.6 = (bf16[272,1024]{1,0:T(8,128)(2,1)S(1)}, bf16[272,1024]{1,0:T(8,128)(2,1)S(1)}, u32[]{:S(2)}, u32[]{:S(2)}) collective-permute-start(bf16[272,1024]{1,0:T(8,128)(2,1)S(1)} %broadcast_select_fusion.12.refs_7_), channel_id=1, source_target_pairs={{0,1},{1,0},{2,3},{3,2},{4,5},{5,4},{6,7},{7,6},{8,9},{9,8},{10,11... | collective-permute-start | bytes 1671176 | tf_op jit(solution)/shard_map/ppermute | solution.py:121
  119.9 34.0 %collective-permute-start.8 = (bf16[272,1024]{1,0:T(8,128)(2,1)}, bf16[272,1024]{1,0:T(8,128)(2,1)}, u32[]{:S(2)}, u32[]{:S(2)}) collective-permute-start(bf16[272,1024]{1,0:T(8,128)(2,1)} %copy-done.79), channel_id=1, source_target_pairs={{0,1},{1,0},{2,3},{3,2},{4,5},{5,4},{6,7},{7,6},{8,9},{9,8},{10,11... | collective-permute-start | bytes 1671176 | tf_op jit(solution)/shard_map/ppermute | solution.py:121
  132.0 27.5 %collective-permute-start.10 = (bf16[272,1024]{1,0:T(8,128)(2,1)}, bf16[272,1024]{1,0:T(8,128)(2,1)}, u32[]{:S(2)}, u32[]{:S(2)}) collective-permute-start(bf16[272,1024]{1,0:T(8,128)(2,1)} %collective-permute-done.9.refs_9_), channel_id=1, source_target_pairs={{0,1},{1,0},{2,3},{3,2},{4,5},{5,4},{6,7},{7,6},{8,9},{9,8},{10,11... | collective-permute-start | bytes 1671176 | tf_op jit(solution)/shard_map/ppermute | solution.py:121
  153.9 34.8 %collective-permute-start.33 = (bf16[256,2048]{1,0:T(8,128)(2,1)S(1)}, bf16[256,2048]{1,0:T(8,128)(2,1)S(1)}, u32[]{:S(2)}, u32[]{:S(2)}) collective-permute-start(bf16[256,2048]{1,0:T(8,128)(2,1)S(1)} %constant_dynamic-update-slice_fusion.16), channel_id=1, source_target_pairs={{1,4},{3,6},{4,1},{6,3},{9,12},{11,14},{12,9},{14,11},{17,20},{19,... | collective-permute-start | bytes 3145736 | tf_op jit(solution)/shard_map/ppermute | solution.py:121
  159.5 29.1 %collective-permute-start.34 = (bf16[256,1024]{1,0:T(8,128)(2,1)S(1)}, bf16[256,1024]{1,0:T(8,128)(2,1)S(1)}, u32[]{:S(2)}, u32[]{:S(2)}) collective-permute-start(bf16[256,1024]{1,0:T(8,128)(2,1)S(1)} %bitcast.66), channel_id=1, source_target_pairs={{1,4},{3,6},{4,1},{6,3},{9,12},{11,14},{12,9},{14,11},{17,20},{19,... | collective-permute-start | bytes 1572872 | tf_op jit(solution)/shard_map/ppermute | solution.py:121
  189.8 166.9 %all-gather.8.cloned.1.call-start = ((), (), s32[]{:S(2)}) async-start(), calls=%async_computation.6 | async-start | bytes 4718592 | tf_op jit(solution)/shard_map/all_gather | solution.py:159
  189.8 56.2 %collective-permute-start.4 = (bf16[1024,2048]{1,0:T(8,128)(2,1)}, bf16[1024,2048]{1,0:T(8,128)(2,1)}, u32[]{:S(2)}, u32[]{:S(2)}) collective-permute-start(bf16[1024,2048]{1,0:T(8,128)(2,1)} %param.31), channel_id=1, source_target_pairs={{1,4},{3,6},{4,1},{6,3},{9,12},{11,14},{12,9},{14,11},{17,20},{19,... | collective-permute-start | bytes 12582920 | tf_op jit(solution)/shard_map/ppermute | solution.py:121
  194.8 22.5 %collective-permute-start.16 = (bf16[256,1024]{1,0:T(8,128)(2,1)}, bf16[256,1024]{1,0:T(8,128)(2,1)S(1)}, u32[]{:S(2)}, u32[]{:S(2)}) collective-permute-start(bf16[256,1024]{1,0:T(8,128)(2,1)} %collective-permute-done.3.refs_9_), channel_id=1, source_target_pairs={{0,8},{1,9},{2,10},{3,11},{4,12},{5,13},{6,14},{7,15},{8,16},{9,17... | collective-permute-start | bytes 1572872 | tf_op jit(solution)/shard_map/ppermute | solution.py:121
  195.0 25.0 %collective-permute-start.17 = (bf16[256,1024]{1,0:T(8,128)(2,1)}, bf16[256,1024]{1,0:T(8,128)(2,1)S(1)}, u32[]{:S(2)}, u32[]{:S(2)}) collective-permute-start(bf16[256,1024]{1,0:T(8,128)(2,1)} %broadcast_select_fusion.14.refs_7_), channel_id=1, source_target_pairs={{0,1},{1,0},{2,3},{3,2},{4,5},{5,4},{6,7},{7,6},{8,9},{9,8},{10,11... | collective-permute-start | bytes 1572872 | tf_op jit(solution)/shard_map/ppermute | solution.py:121
  195.1 24.9 %collective-permute-start.18 = (bf16[256,1024]{1,0:T(8,128)(2,1)}, bf16[256,1024]{1,0:T(8,128)(2,1)}, u32[]{:S(2)}, u32[]{:S(2)}) collective-permute-start(bf16[256,1024]{1,0:T(8,128)(2,1)} %collective-permute-done.2.refs_8_), channel_id=1, source_target_pairs={{0,1},{1,0},{2,3},{3,2},{4,5},{5,4},{6,7},{7,6},{8,9},{9,8},{10,11... | collective-permute-start | bytes 1572872 | tf_op jit(solution)/shard_map/ppermute | solution.py:121
  195.6 24.4 %collective-permute-start.19 = (bf16[256,1024]{1,0:T(8,128)(2,1)}, bf16[256,1024]{1,0:T(8,128)(2,1)}, u32[]{:S(2)}, u32[]{:S(2)}) collective-permute-start(bf16[256,1024]{1,0:T(8,128)(2,1)} %collective-permute-done.3.refs_9_), channel_id=1, source_target_pairs={{0,1},{1,0},{2,3},{3,2},{4,5},{5,4},{6,7},{7,6},{8,9},{9,8},{10,11... | collective-permute-start | bytes 1572872 | tf_op jit(solution)/shard_map/ppermute | solution.py:121
  218.4 358.9 %reduce-scatter.11.cloned.1.call-start = ((), (), s32[]{:S(2)}) async-start(), calls=%async_computation.10 | async-start | bytes 2621440 | tf_op jit(solution)/shard_map/reduce_scatter | solution.py:187
  250.7 22.5 %collective-permute-start.21 = (bf16[128,2048]{1,0:T(8,128)(2,1)S(1)}, bf16[128,2048]{1,0:T(8,128)(2,1)S(1)}, u32[]{:S(2)}, u32[]{:S(2)}) collective-permute-start(bf16[128,2048]{1,0:T(8,128)(2,1)S(1)} %get-tuple-element.234), channel_id=1, source_target_pairs={{0,2},{1,3},{2,0},{3,1},{4,6},{5,7},{6,4},{7,5},{8,10},{9,11},{10,... | collective-permute-start | bytes 1572872 | tf_op jit(solution)/shard_map/ppermute | solution.py:121
  250.9 23.3 %collective-permute-start.22 = (bf16[128,2048]{1,0:T(8,128)(2,1)S(1)}, bf16[128,2048]{1,0:T(8,128)(2,1)S(1)}, u32[]{:S(2)}, u32[]{:S(2)}) collective-permute-start(bf16[128,2048]{1,0:T(8,128)(2,1)S(1)} %get-tuple-element.237), channel_id=1, source_target_pairs={{0,4},{1,5},{2,6},{3,7},{4,0},{5,1},{6,2},{7,3},{8,12},{9,13},{10,... | collective-permute-start | bytes 1572872 | tf_op jit(solution)/shard_map/ppermute | solution.py:121
  263.3 22.1 %collective-permute-start.24 = (bf16[128,2048]{1,0:T(8,128)(2,1)S(1)}, bf16[128,2048]{1,0:T(8,128)(2,1)S(1)}, u32[]{:S(2)}, u32[]{:S(2)}) collective-permute-start(bf16[128,2048]{1,0:T(8,128)(2,1)S(1)} %get-tuple-element.194), channel_id=1, source_target_pairs={{0,4},{1,5},{2,6},{3,7},{4,0},{5,1},{6,2},{7,3},{8,12},{9,13},{10,... | collective-permute-start | bytes 1572872 | tf_op jit(solution)/shard_map/ppermute | solution.py:121
  302.8 23.4 %collective-permute-start.31 = (bf16[128,2048]{1,0:T(8,128)(2,1)S(1)}, bf16[128,2048]{1,0:T(8,128)(2,1)S(1)}, u32[]{:S(2)}, u32[]{:S(2)}) collective-permute-start(bf16[128,2048]{1,0:T(8,128)(2,1)S(1)} %collective-permute-done.27), channel_id=1, source_target_pairs={{0,2},{1,3},{2,0},{3,1},{4,6},{5,7},{6,4},{7,5},{8,10},{9,11},{10,... | collective-permute-start | bytes 1572872 | tf_op jit(solution)/shard_map/ppermute | solution.py:121
  303.8 23.2 %collective-permute-start.32 = (bf16[128,2048]{1,0:T(8,128)(2,1)S(1)}, bf16[128,2048]{1,0:T(8,128)(2,1)S(1)}, u32[]{:S(2)}, u32[]{:S(2)}) collective-permute-start(bf16[128,2048]{1,0:T(8,128)(2,1)S(1)} %collective-permute-done.30), channel_id=1, source_target_pairs={{0,4},{1,5},{2,6},{3,7},{4,0},{5,1},{6,2},{7,3},{8,12},{9,13},{10,... | collective-permute-start | bytes 1572872 | tf_op jit(solution)/shard_map/ppermute | solution.py:121
  389.4 23.9 %collective-permute-start.36 = (bf16[128,2048]{1,0:T(8,128)(2,1)}, bf16[128,2048]{1,0:T(8,128)(2,1)S(1)}, u32[]{:S(2)}, u32[]{:S(2)}) collective-permute-start(bf16[128,2048]{1,0:T(8,128)(2,1)} %get-tuple-element.230), channel_id=1, source_target_pairs={{0,2},{1,3},{2,0},{3,1},{4,6},{5,7},{6,4},{7,5},{8,10},{9,11},{10,... | collective-permute-start | bytes 1572872 | tf_op jit(solution)/shard_map/ppermute | solution.py:121
  390.6 22.7 %collective-permute-start.37 = (bf16[128,2048]{1,0:T(8,128)(2,1)}, bf16[128,2048]{1,0:T(8,128)(2,1)S(1)}, u32[]{:S(2)}, u32[]{:S(2)}) collective-permute-start(bf16[128,2048]{1,0:T(8,128)(2,1)} %get-tuple-element.233), channel_id=1, source_target_pairs={{0,4},{1,5},{2,6},{3,7},{4,0},{5,1},{6,2},{7,3},{8,12},{9,13},{10,... | collective-permute-start | bytes 1572872 | tf_op jit(solution)/shard_map/ppermute | solution.py:121
  434.8 283.1 %reduce-scatter.7.cloned.1.call-start = ((), (), s32[]{:S(2)}) async-start(), calls=%async_computation.8 | async-start | bytes 5242880 | tf_op jit(solution)/shard_map/reduce_scatter | solution.py:187
  434.9 22.1 %collective-permute-start.43 = (bf16[128,2048]{1,0:T(8,128)(2,1)}, bf16[128,2048]{1,0:T(8,128)(2,1)S(1)}, u32[]{:S(2)}, u32[]{:S(2)}) collective-permute-start(bf16[128,2048]{1,0:T(8,128)(2,1)} %get-tuple-element.247), channel_id=1, source_target_pairs={{0,4},{1,5},{2,6},{3,7},{4,0},{5,1},{6,2},{7,3},{8,12},{9,13},{10,... | collective-permute-start | bytes 1572872 | tf_op jit(solution)/shard_map/ppermute | solution.py:121
  436.0 21.8 %collective-permute-start.44 = (bf16[128,2048]{1,0:T(8,128)(2,1)}, bf16[128,2048]{1,0:T(8,128)(2,1)S(1)}, u32[]{:S(2)}, u32[]{:S(2)}) collective-permute-start(bf16[128,2048]{1,0:T(8,128)(2,1)} %get-tuple-element.249), channel_id=1, source_target_pairs={{0,2},{1,3},{2,0},{3,1},{4,6},{5,7},{6,4},{7,5},{8,10},{9,11},{10,... | collective-permute-start | bytes 1572872 | tf_op jit(solution)/shard_map/ppermute | solution.py:121
  445.8 22.6 %collective-permute-start.46 = (bf16[128,2048]{1,0:T(8,128)(2,1)}, bf16[128,2048]{1,0:T(8,128)(2,1)S(1)}, u32[]{:S(2)}, u32[]{:S(2)}) collective-permute-start(bf16[128,2048]{1,0:T(8,128)(2,1)} %collective-permute-done.42), channel_id=1, source_target_pairs={{0,2},{1,3},{2,0},{3,1},{4,6},{5,7},{6,4},{7,5},{8,10},{9,11},{10,... | collective-permute-start | bytes 1572872 | tf_op jit(solution)/shard_map/ppermute | solution.py:121
  447.0 22.2 %collective-permute-start.47 = (bf16[128,2048]{1,0:T(8,128)(2,1)}, bf16[128,2048]{1,0:T(8,128)(2,1)S(1)}, u32[]{:S(2)}, u32[]{:S(2)}) collective-permute-start(bf16[128,2048]{1,0:T(8,128)(2,1)} %collective-permute-done.45), channel_id=1, source_target_pairs={{0,4},{1,5},{2,6},{3,7},{4,0},{5,1},{6,2},{7,3},{8,12},{9,13},{10,... | collective-permute-start | bytes 1572872 | tf_op jit(solution)/shard_map/ppermute | solution.py:121
  476.7 25.0 %collective-permute-start.48 = (bf16[1024,1024]{1,0:T(8,128)(2,1)}, bf16[1024,1024]{1,0:T(8,128)(2,1)S(1)}, u32[]{:S(2)}, u32[]{:S(2)}) collective-permute-start(bf16[1024,1024]{1,0:T(8,128)(2,1)} %fusion.108), channel_id=1, source_target_pairs={{0,1},{1,0},{2,3},{3,2},{4,5},{5,4},{6,7},{7,6},{8,9},{9,8},{10,11... | collective-permute-start | bytes 6291464 | tf_op jit(solution)/shard_map/ppermute | solution.py:121
  493.5 65.8 %collective-permute-start.79 = (bf16[1024,2048]{1,0:T(8,128)(2,1)}, bf16[1024,2048]{1,0:T(8,128)(2,1)}, u32[]{:S(2)}, u32[]{:S(2)}) collective-permute-start(bf16[1024,2048]{1,0:T(8,128)(2,1)} %convolution_convert_fusion.1), channel_id=1, source_target_pairs={{0,1},{1,0},{2,3},{3,2},{4,5},{5,4},{6,7},{7,6},{8,9},{9,8},{10,11... | collective-permute-start | bytes 12582920 | tf_op jit(solution)/shard_map/ppermute | solution.py:121
  498.2 49.3 %collective-permute-start.52 = (bf16[128,2048]{1,0:T(8,128)(2,1)}, bf16[128,2048]{1,0:T(8,128)(2,1)}, u32[]{:S(2)}, u32[]{:S(2)}) collective-permute-start(bf16[128,2048]{1,0:T(8,128)(2,1)} %get-tuple-element.218), channel_id=1, source_target_pairs={{0,2},{1,3},{2,0},{3,1},{4,6},{5,7},{6,4},{7,5},{8,10},{9,11},{10,... | collective-permute-start | bytes 1572872 | tf_op jit(solution)/shard_map/ppermute | solution.py:121
  499.4 50.6 %collective-permute-start.54 = (bf16[128,2048]{1,0:T(8,128)(2,1)}, bf16[128,2048]{1,0:T(8,128)(2,1)}, u32[]{:S(2)}, u32[]{:S(2)}) collective-permute-start(bf16[128,2048]{1,0:T(8,128)(2,1)} %get-tuple-element.219), channel_id=1, source_target_pairs={{0,4},{1,5},{2,6},{3,7},{4,0},{5,1},{6,2},{7,3},{8,12},{9,13},{10,... | collective-permute-start | bytes 1572872 | tf_op jit(solution)/shard_map/ppermute | solution.py:121
  501.7 75.5 %collective-permute-start.50 = (bf16[128,2048]{1,0:T(8,128)(2,1)}, bf16[128,2048]{1,0:T(8,128)(2,1)}, u32[]{:S(2)}, u32[]{:S(2)}) collective-permute-start(bf16[128,2048]{1,0:T(8,128)(2,1)} %get-tuple-element.221), channel_id=1, source_target_pairs={{0,2},{1,3},{2,0},{3,1},{4,6},{5,7},{6,4},{7,5},{8,10},{9,11},{10,... | collective-permute-start | bytes 1572872 | tf_op jit(solution)/shard_map/ppermute | solution.py:121
  504.5 76.9 %collective-permute-start.51 = (bf16[128,2048]{1,0:T(8,128)(2,1)}, bf16[128,2048]{1,0:T(8,128)(2,1)}, u32[]{:S(2)}, u32[]{:S(2)}) collective-permute-start(bf16[128,2048]{1,0:T(8,128)(2,1)} %get-tuple-element.220), channel_id=1, source_target_pairs={{0,4},{1,5},{2,6},{3,7},{4,0},{5,1},{6,2},{7,3},{8,12},{9,13},{10,... | collective-permute-start | bytes 1572872 | tf_op jit(solution)/shard_map/ppermute | solution.py:121
  509.9 218.5 %reduce-scatter.9.cloned.1.call-start = ((), (), s32[]{:S(2)}) async-start(), calls=%async_computation.9 | async-start | bytes 5242880 | tf_op jit(solution)/shard_map/reduce_scatter | solution.py:187
  547.6 92.0 %collective-permute-start.63 = (bf16[1024,2048]{1,0:T(8,128)(2,1)}, bf16[1024,2048]{1,0:T(8,128)(2,1)}, u32[]{:S(2)}, u32[]{:S(2)}) collective-permute-start(bf16[1024,2048]{1,0:T(8,128)(2,1)} %convolution_convert_fusion), channel_id=1, source_target_pairs={{0,1},{1,0},{2,3},{3,2},{4,5},{5,4},{6,7},{7,6},{8,9},{9,8},{10,11... | collective-permute-start | bytes 12582920 | tf_op jit(solution)/shard_map/ppermute | solution.py:121
  552.6 28.8 %collective-permute-start.53 = (bf16[128,2048]{1,0:T(8,128)(2,1)}, bf16[128,2048]{1,0:T(8,128)(2,1)S(1)}, u32[]{:S(2)}, u32[]{:S(2)}) collective-permute-start(bf16[128,2048]{1,0:T(8,128)(2,1)} %get-tuple-element.154), channel_id=1, source_target_pairs={{0,4},{1,5},{2,6},{3,7},{4,0},{5,1},{6,2},{7,3},{8,12},{9,13},{10,... | collective-permute-start | bytes 1572872 | tf_op jit(solution)/shard_map/ppermute | solution.py:121
  559.2 23.0 %collective-permute-start.55 = (bf16[128,2048]{1,0:T(8,128)(2,1)S(1)}, bf16[128,2048]{1,0:T(8,128)(2,1)}, u32[]{:S(2)}, u32[]{:S(2)}) collective-permute-start(bf16[128,2048]{1,0:T(8,128)(2,1)S(1)} %get-tuple-element.155), channel_id=1, source_target_pairs={{0,2},{1,3},{2,0},{3,1},{4,6},{5,7},{6,4},{7,5},{8,10},{9,11},{10,... | collective-permute-start | bytes 1572872 | tf_op jit(solution)/shard_map/ppermute | solution.py:121
  577.3 23.1 %collective-permute-start.81 = (bf16[256,1024]{1,0:T(8,128)(2,1)}, bf16[256,1024]{1,0:T(8,128)(2,1)}, u32[]{:S(2)}, u32[]{:S(2)}) collective-permute-start(bf16[256,1024]{1,0:T(8,128)(2,1)} %reduce-scatter.11.cloned.1.call-done), channel_id=1, source_target_pairs={{1,4},{3,6},{4,1},{6,3},{9,12},{11,14},{12,9},{14,11},{17,20},{19,... | collective-permute-start | bytes 1572872 | tf_op jit(solution)/shard_map/ppermute | solution.py:121
  597.5 159.8 %reduce-scatter.5.cloned.1.call-start = ((), (), s32[]{:S(2)}) async-start(), calls=%async_computation.7 | async-start | bytes 5242880 | tf_op jit(solution)/shard_map/reduce_scatter | solution.py:187
  600.4 55.4 %collective-permute-start.66 = (bf16[128,2048]{1,0:T(8,128)(2,1)}, bf16[128,2048]{1,0:T(8,128)(2,1)S(1)}, u32[]{:S(2)}, u32[]{:S(2)}) collective-permute-start(bf16[128,2048]{1,0:T(8,128)(2,1)} %get-tuple-element.208), channel_id=1, source_target_pairs={{0,2},{1,3},{2,0},{3,1},{4,6},{5,7},{6,4},{7,5},{8,10},{9,11},{10,... | collective-permute-start | bytes 1572872 | tf_op jit(solution)/shard_map/ppermute | solution.py:121
  603.2 52.6 %collective-permute-start.68 = (bf16[128,2048]{1,0:T(8,128)(2,1)S(1)}, bf16[128,2048]{1,0:T(8,128)(2,1)S(1)}, u32[]{:S(2)}, u32[]{:S(2)}) collective-permute-start(bf16[128,2048]{1,0:T(8,128)(2,1)S(1)} %copy-done.39), channel_id=1, source_target_pairs={{0,4},{1,5},{2,6},{3,7},{4,0},{5,1},{6,2},{7,3},{8,12},{9,13},{10,... | collective-permute-start | bytes 1572872 | tf_op jit(solution)/shard_map/ppermute | solution.py:121
  613.5 51.0 %collective-permute-start.64 = (bf16[128,2048]{1,0:T(8,128)(2,1)}, bf16[128,2048]{1,0:T(8,128)(2,1)}, u32[]{:S(2)}, u32[]{:S(2)}) collective-permute-start(bf16[128,2048]{1,0:T(8,128)(2,1)} %get-tuple-element.206), channel_id=1, source_target_pairs={{0,2},{1,3},{2,0},{3,1},{4,6},{5,7},{6,4},{7,5},{8,10},{9,11},{10,... | collective-permute-start | bytes 1572872 | tf_op jit(solution)/shard_map/ppermute | solution.py:121
  618.7 45.8 %collective-permute-start.65 = (bf16[128,2048]{1,0:T(8,128)(2,1)}, bf16[128,2048]{1,0:T(8,128)(2,1)}, u32[]{:S(2)}, u32[]{:S(2)}) collective-permute-start(bf16[128,2048]{1,0:T(8,128)(2,1)} %get-tuple-element.209), channel_id=1, source_target_pairs={{0,4},{1,5},{2,6},{3,7},{4,0},{5,1},{6,2},{7,3},{8,12},{9,13},{10,... | collective-permute-start | bytes 1572872 | tf_op jit(solution)/shard_map/ppermute | solution.py:121
  639.6 23.5 %collective-permute-start.62 = (bf16[256,2048]{1,0:T(8,128)(2,1)S(1)}, bf16[256,2048]{1,0:T(8,128)(2,1)}, u32[]{:S(2)}, u32[]{:S(2)}) collective-permute-start(bf16[256,2048]{1,0:T(8,128)(2,1)S(1)} %collective-permute-done.61), channel_id=1, source_target_pairs={{0,1},{2,3},{5,4},{7,6},{8,9},{10,11},{13,12},{15,14},{16,17},{18,... | collective-permute-start | bytes 3145736 | tf_op jit(solution)/shard_map/ppermute | solution.py:121
  728.3 35.4 %collective-permute-start.80 = (bf16[256,2048]{1,0:T(8,128)(2,1)}, bf16[256,2048]{1,0:T(8,128)(2,1)}, u32[]{:S(2)}, u32[]{:S(2)}) collective-permute-start(bf16[256,2048]{1,0:T(8,128)(2,1)} %reduce-scatter.9.cloned.1.call-done), channel_id=1, source_target_pairs={{1,4},{3,6},{4,1},{6,3},{9,12},{11,14},{12,9},{14,11},{17,20},{19,... | collective-permute-start | bytes 3145736 | tf_op jit(solution)/shard_map/ppermute | solution.py:121
  (142 other events, 1810.2 us)
Sparse Core Ops, SparseCore 0:
  49.4 107.5 all-gather.3
  189.9 89.6 all-gather.5
  281.2 44.6 all-gather.7
  435.0 46.3 reduce-scatter.10
  510.0 80.6 reduce-scatter.6
  597.6 79.7 reduce-scatter.8
  679.7 77.5 reduce-scatter.4
